TPU v7x, 32 devices: a whole 2x2x4 slice. The times are simulated.
32 devices in a mesh: seq: 4 (over y, x), ctx: 8 (over z, core).
Axes of the slice: x: 2, y: 2, z: 4, core: 2. Of those that a mesh axis runs over, the one named last changes fastest.
Arguments:
- hidden_in: bfloat16 [4096, 2048], P(('seq', 'ctx')), may hold values from -6 to 6
- out_grad: bfloat16 [4096, 2048], P(('seq', 'ctx')), may hold values from -6 to 6
- prefix_len: int32 [4], P('seq'), may hold values from 102 to 512
- norm_gains: float32 [4352], P(('seq', 'ctx')), may hold values from 0.5 to 1.5
- query_weight: float32 [2048, 2048], P(('seq', 'ctx')), may hold values from -0.125 to 0.125
- key_weight: float32 [2048, 1024], P(('seq', 'ctx')), may hold values from -0.125 to 0.125
- value_weight: float32 [2048, 1024], P(('seq', 'ctx')), may hold values from -0.125 to 0.125
- head_gate_weight: float32 [2048, 16], P(('seq', 'ctx')), may hold values from -0.125 to 0.125
- out_weight: float32 [2048, 2048], P(('seq', 'ctx')), may hold values from -3 to 3
- gate_weight: float32 [2048, 6144], P(('seq', 'ctx')), may hold values from -0.125 to 0.125
- up_weight: float32 [2048, 6144], P(('seq', 'ctx')), may hold values from -0.125 to 0.125
- down_weight: float32 [6144, 2048], P(('seq', 'ctx')), may hold values from -0.109375 to 0.109375
Outputs:
- hidden_out: bfloat16 [4096, 2048], P(('seq', 'ctx'))
- hidden_grad: bfloat16 [4096, 2048], P(('seq', 'ctx'))
- gains_grad: float32 [4352], P(('seq', 'ctx'))
- query_grad: float32 [2048, 2048], P(('seq', 'ctx'))
- key_grad: float32 [2048, 1024], P(('seq', 'ctx'))
- value_grad: float32 [2048, 1024], P(('seq', 'ctx'))
- head_gate_grad: float32 [2048, 16], P(('seq', 'ctx'))
- out_weight_grad: float32 [2048, 2048], P(('seq', 'ctx'))
- gate_grad: float32 [2048, 6144], P(('seq', 'ctx'))
- up_grad: float32 [2048, 6144], P(('seq', 'ctx'))
- down_grad: float32 [6144, 2048], P(('seq', 'ctx'))
Inputs may be any that keep to these rules, and one draw needn't show every extreme that they name: prefix_len[s] is the number of leading tokens of sequence s that attend to each other in both directions.
All inputs are finite; a program needn't handle non-finite values.
Results may differ from a plain program's by a relative error of at most 0.02.
Values may be sent and summed in bfloat16 or wider, within the bound.
A program may use at most 448 MiB of HBM per device.

v0:
```python
from functools import partial

import jax
import jax.numpy as jnp
from jax import lax
from jax.sharding import PartitionSpec as P

H = 16
KV = 8
HD = 128


epsilon = 1e-06
rope_base = 1000000.0
negative = -1e30


def product(left_side, right_side):
    return jnp.dot(left_side, right_side, preferred_element_type=jnp.float32)


def rms_scale(values, gain_vector):
    inverse = lax.rsqrt(jnp.mean(values * values, axis=-1, keepdims=True) + epsilon)
    return values * inverse * gain_vector


def rope_tables(positions, head_width):
    half_width = head_width // 2
    inverse = rope_base ** (-jnp.arange(half_width, dtype=jnp.float32) * 2.0 / head_width)
    angles = positions.astype(jnp.float32)[:, None] * inverse[None, :]
    angles = jnp.concatenate([angles, angles], axis=-1)
    return (jnp.cos(angles)[:, None, :], jnp.sin(angles)[:, None, :])


def rotate(values, cosine_table, sine_table):
    half_width = values.shape[-1] // 2
    turned = jnp.concatenate([-values[..., half_width:], values[..., :half_width]], axis=-1)
    return values * cosine_table + turned * sine_table


def qk_piece(query_raw, key_raw, query_gain, key_gain, cosine_table, sine_table):
    row_count = query_raw.shape[0]
    queries = rms_scale(query_raw.reshape(row_count, H, HD), query_gain)
    keys = rms_scale(key_raw.reshape(row_count, KV, HD), key_gain)
    return (rotate(queries, cosine_table, sine_table), rotate(keys, cosine_table, sine_table))


def gate_heads(attended_rows, gate_raw):
    row_count = attended_rows.shape[0]
    scaled = attended_rows.reshape(row_count, H, HD) * jax.nn.sigmoid(gate_raw)[:, :, None]
    return scaled.reshape(row_count, H * HD)


def swiglu(gate_pre, up_pre):
    return jax.nn.silu(gate_pre) * up_pre


def block_scores(queries, key_blk, first_key, key_block, limits):
    score_scale = queries.shape[-1] ** (-0.5)
    scores = (
        jnp.einsum("tkgd,skd->kgts", queries, key_blk, preferred_element_type=jnp.float32)
        * score_scale
    )
    key_pos = first_key + jnp.arange(key_block, dtype=jnp.int32)
    allowed = key_pos[None, :] <= limits[:, None]
    return jnp.where(allowed, scores, negative)


def attend_forward(queries, keys_all, values_all, positions, prefix, key_block):
    row_count, kv_heads, group_size, head_width = queries.shape
    block_count = keys_all.shape[0] // key_block
    limits = jnp.maximum(positions, prefix - 1)
    reach = jnp.maximum(positions[-1], prefix - 1)

    def step(carried, block_index):
        first_key = block_index * key_block

        def work(state_in):
            running_max, running_sum, accum = state_in
            key_blk = lax.dynamic_slice_in_dim(keys_all, first_key, key_block, 0)
            value_blk = lax.dynamic_slice_in_dim(values_all, first_key, key_block, 0)
            scores = block_scores(queries, key_blk, first_key, key_block, limits)
            new_max = jnp.maximum(running_max, jnp.max(scores, axis=-1))
            rescale = jnp.exp(running_max - new_max)
            expanded = jnp.exp(scores - new_max[..., None])
            running_sum = running_sum * rescale + jnp.sum(expanded, axis=-1)
            update = jnp.einsum(
                "kgts,skd->kgtd",
                expanded.astype(jnp.bfloat16),
                value_blk,
                preferred_element_type=jnp.float32,
            )
            accum = accum * rescale[..., None] + update
            return (new_max, running_sum, accum)

        return (lax.cond(first_key <= reach, work, lambda state_in: state_in, carried), None)

    start_state = (
        jnp.full((kv_heads, group_size, row_count), negative, jnp.float32),
        jnp.zeros((kv_heads, group_size, row_count), jnp.float32),
        jnp.zeros((kv_heads, group_size, row_count, head_width), jnp.float32),
    )
    (running_max, running_sum, accum), unused = lax.scan(
        step, start_state, jnp.arange(block_count, dtype=jnp.int32)
    )
    return (accum / running_sum[..., None], running_max + jnp.log(running_sum))


def attend_backward(
    queries, keys_all, values_all, positions, prefix, key_block, log_norm, grad_heads, row_delta
):
    row_count, kv_heads, group_size, head_width = queries.shape
    score_scale = head_width ** (-0.5)
    block_count = keys_all.shape[0] // key_block
    limits = jnp.maximum(positions, prefix - 1)
    reach = jnp.maximum(positions[-1], prefix - 1)

    def step(query_accum, block_index):
        first_key = block_index * key_block

        def work(accum_in):
            key_blk = lax.dynamic_slice_in_dim(keys_all, first_key, key_block, 0)
            value_blk = lax.dynamic_slice_in_dim(values_all, first_key, key_block, 0)
            scores = block_scores(queries, key_blk, first_key, key_block, limits)
            probabilities = jnp.exp(scores - log_norm[..., None])
            prob_grad = jnp.einsum(
                "kgtd,skd->kgts", grad_heads, value_blk, preferred_element_type=jnp.float32
            )
            score_grad = (probabilities * (prob_grad - row_delta[..., None])).astype(jnp.bfloat16)
            accum_out = (
                accum_in
                + jnp.einsum(
                    "kgts,skd->tkgd", score_grad, key_blk, preferred_element_type=jnp.float32
                )
                * score_scale
            )
            key_part = (
                jnp.einsum(
                    "kgts,tkgd->skd", score_grad, queries, preferred_element_type=jnp.float32
                )
                * score_scale
            )
            value_part = jnp.einsum(
                "kgts,kgtd->skd",
                probabilities.astype(jnp.bfloat16),
                grad_heads,
                preferred_element_type=jnp.float32,
            )
            return (accum_out, key_part, value_part)

        def skip(accum_in):
            empty = jnp.zeros((key_block, kv_heads, head_width), jnp.float32)
            return (accum_in, empty, empty)

        accum_out, key_part, value_part = lax.cond(first_key <= reach, work, skip, query_accum)
        return (accum_out, (key_part, value_part))

    start_accum = jnp.zeros((row_count, kv_heads, group_size, head_width), jnp.float32)
    query_accum, (key_parts, value_parts) = lax.scan(
        step, start_accum, jnp.arange(block_count, dtype=jnp.int32)
    )
    total_keys = block_count * key_block
    return (
        query_accum,
        key_parts.reshape(total_keys, kv_heads * head_width),
        value_parts.reshape(total_keys, kv_heads * head_width),
    )


def on_device(
    hidden_in,
    out_grad,
    prefix_len,
    norm_gains,
    query_weight,
    key_weight,
    value_weight,
    head_gate_weight,
    out_weight,
    gate_weight,
    up_weight,
    down_weight,
):
    row_count = hidden_in.shape[0]
    width_model = hidden_in.shape[1]
    pieces = lax.axis_size("ctx")
    length = row_count * pieces
    key_block = min(512, length)
    group_size = H // KV
    positions = lax.axis_index("ctx") * row_count + jnp.arange(row_count, dtype=jnp.int32)
    prefix = prefix_len[0]
    gains_low, query_low, key_low, value_low, gate_low, output_low = (
        lax.all_gather(norm_gains.astype(jnp.bfloat16), ("seq", "ctx"), axis=0, tiled=True),
        lax.all_gather(query_weight.astype(jnp.bfloat16), ("seq", "ctx"), axis=0, tiled=True),
        lax.all_gather(key_weight.astype(jnp.bfloat16), ("seq", "ctx"), axis=0, tiled=True),
        lax.all_gather(value_weight.astype(jnp.bfloat16), ("seq", "ctx"), axis=0, tiled=True),
        lax.all_gather(head_gate_weight.astype(jnp.bfloat16), ("seq", "ctx"), axis=0, tiled=True),
        lax.all_gather(out_weight.astype(jnp.bfloat16), ("seq", "ctx"), axis=0, tiled=True),
    )
    gains_full = gains_low.astype(jnp.float32)
    attention_gain = gains_full[:width_model]
    swiglu_gain = gains_full[width_model : 2 * width_model]
    query_gain = gains_full[2 * width_model : 2 * width_model + HD]
    key_gain = gains_full[2 * width_model + HD :]
    residual_in = hidden_in.astype(jnp.float32)
    normed_full, pull_norm_one = jax.vjp(rms_scale, residual_in, attention_gain)
    normed = normed_full.astype(jnp.bfloat16)
    query_raw = product(normed, query_low)
    key_raw = product(normed, key_low)
    values = product(normed, value_low).astype(jnp.bfloat16)
    gate_raw = product(normed, gate_low)
    cosine_table, sine_table = rope_tables(positions, HD)
    (queries_full, keys_full), pull_rope = jax.vjp(
        partial(qk_piece, cosine_table=cosine_table, sine_table=sine_table),
        query_raw,
        key_raw,
        query_gain,
        key_gain,
    )
    queries = queries_full.astype(jnp.bfloat16).reshape(row_count, KV, group_size, HD)
    keys_local = keys_full.astype(jnp.bfloat16).reshape(row_count, KV * HD)
    keys_all, values_all = (
        lax.all_gather(keys_local, "ctx", axis=0, tiled=True),
        lax.all_gather(values, "ctx", axis=0, tiled=True),
    )
    keys_all = keys_all.reshape(length, KV, HD)
    values_all = values_all.reshape(length, KV, HD)
    attended, log_norm = attend_forward(queries, keys_all, values_all, positions, prefix, key_block)
    attended_rows = attended.transpose(2, 0, 1, 3).reshape(row_count, H * HD)
    gated_full, pull_gate = jax.vjp(gate_heads, attended_rows, gate_raw)
    gated = gated_full.astype(jnp.bfloat16)
    middle = residual_in + product(gated, output_low)
    gate_low_ff, up_low_ff, down_low_ff = (
        lax.all_gather(gate_weight.astype(jnp.bfloat16), ("seq", "ctx"), axis=0, tiled=True),
        lax.all_gather(up_weight.astype(jnp.bfloat16), ("seq", "ctx"), axis=0, tiled=True),
        lax.all_gather(down_weight.astype(jnp.bfloat16), ("seq", "ctx"), axis=0, tiled=True),
    )
    normed_two_full, pull_norm_two = jax.vjp(rms_scale, middle, swiglu_gain)
    normed_two = normed_two_full.astype(jnp.bfloat16)
    gate_pre = product(normed_two, gate_low_ff)
    up_pre = product(normed_two, up_low_ff)
    hidden_ff_full, pull_swiglu = jax.vjp(swiglu, gate_pre, up_pre)
    hidden_ff = hidden_ff_full.astype(jnp.bfloat16)
    hidden_out = (middle + product(hidden_ff, down_low_ff)).astype(jnp.bfloat16)
    gate_low_ff, up_low_ff, down_low_ff = (
        lax.all_gather(gate_weight.astype(jnp.bfloat16), ("seq", "ctx"), axis=0, tiled=True),
        lax.all_gather(up_weight.astype(jnp.bfloat16), ("seq", "ctx"), axis=0, tiled=True),
        lax.all_gather(down_weight.astype(jnp.bfloat16), ("seq", "ctx"), axis=0, tiled=True),
    )
    grad_hidden_ff = product(out_grad, down_low_ff.T)
    down_term = product(hidden_ff.T, out_grad)
    down_share = lax.psum_scatter(down_term, ("seq", "ctx"), scatter_dimension=0, tiled=True)
    grad_gate_full, grad_up_full = pull_swiglu(grad_hidden_ff)
    grad_gate = grad_gate_full.astype(jnp.bfloat16)
    grad_up = grad_up_full.astype(jnp.bfloat16)
    grad_normed_two = product(grad_gate, gate_low_ff.T) + product(grad_up, up_low_ff.T)
    gate_term = product(normed_two.T, grad_gate)
    up_term = product(normed_two.T, grad_up)
    gate_share, up_share = (
        lax.psum_scatter(gate_term, ("seq", "ctx"), scatter_dimension=0, tiled=True),
        lax.psum_scatter(up_term, ("seq", "ctx"), scatter_dimension=0, tiled=True),
    )
    grad_middle_part, swiglu_gain_grad = pull_norm_two(grad_normed_two)
    grad_middle = out_grad.astype(jnp.float32) + grad_middle_part
    grad_branch = grad_middle.astype(jnp.bfloat16)
    query_low, key_low, value_low, gate_low, output_low = (
        lax.all_gather(query_weight.astype(jnp.bfloat16), ("seq", "ctx"), axis=0, tiled=True),
        lax.all_gather(key_weight.astype(jnp.bfloat16), ("seq", "ctx"), axis=0, tiled=True),
        lax.all_gather(value_weight.astype(jnp.bfloat16), ("seq", "ctx"), axis=0, tiled=True),
        lax.all_gather(head_gate_weight.astype(jnp.bfloat16), ("seq", "ctx"), axis=0, tiled=True),
        lax.all_gather(out_weight.astype(jnp.bfloat16), ("seq", "ctx"), axis=0, tiled=True),
    )
    grad_gated = product(grad_branch, output_low.T)
    output_term = product(gated.T, grad_branch)
    grad_attended_full, grad_gate_raw_full = pull_gate(grad_gated)
    grad_attended = grad_attended_full.astype(jnp.bfloat16)
    grad_gate_raw = grad_gate_raw_full.astype(jnp.bfloat16)
    grad_heads = grad_attended.reshape(row_count, KV, group_size, HD).transpose(1, 2, 0, 3)
    row_delta = jnp.sum(grad_heads.astype(jnp.float32) * attended, axis=-1)
    query_accum, key_terms, value_terms = attend_backward(
        queries, keys_all, values_all, positions, prefix, key_block, log_norm, grad_heads, row_delta
    )
    key_own, value_own = (
        lax.psum_scatter(
            key_terms.astype(jnp.bfloat16), "ctx", scatter_dimension=0, tiled=True
        ).astype(jnp.float32),
        lax.psum_scatter(
            value_terms.astype(jnp.bfloat16), "ctx", scatter_dimension=0, tiled=True
        ).astype(jnp.float32),
    )
    grad_values = value_own.astype(jnp.bfloat16)
    grad_query_full, grad_key_full, query_gain_grad, key_gain_grad = pull_rope(
        (query_accum.reshape(row_count, H, HD), key_own.reshape(row_count, KV, HD))
    )
    grad_query_raw = grad_query_full.astype(jnp.bfloat16)
    grad_key_raw = grad_key_full.astype(jnp.bfloat16)
    grad_normed = (
        product(grad_query_raw, query_low.T)
        + product(grad_key_raw, key_low.T)
        + product(grad_values, value_low.T)
        + product(grad_gate_raw, gate_low.T)
    )
    query_term = product(normed.T, grad_query_raw)
    key_term = product(normed.T, grad_key_raw)
    value_term = product(normed.T, grad_values)
    head_term = product(normed.T, grad_gate_raw)
    grad_input_part, attention_gain_grad = pull_norm_one(grad_normed)
    hidden_grad = (grad_middle + grad_input_part).astype(jnp.bfloat16)
    gains_term = jnp.concatenate(
        [attention_gain_grad, swiglu_gain_grad, query_gain_grad, key_gain_grad]
    )
    gains_share, query_share, key_share, value_share, head_share, output_share = (
        lax.psum_scatter(gains_term, ("seq", "ctx"), scatter_dimension=0, tiled=True),
        lax.psum_scatter(query_term, ("seq", "ctx"), scatter_dimension=0, tiled=True),
        lax.psum_scatter(key_term, ("seq", "ctx"), scatter_dimension=0, tiled=True),
        lax.psum_scatter(value_term, ("seq", "ctx"), scatter_dimension=0, tiled=True),
        lax.psum_scatter(head_term, ("seq", "ctx"), scatter_dimension=0, tiled=True),
        lax.psum_scatter(output_term, ("seq", "ctx"), scatter_dimension=0, tiled=True),
    )
    return (
        hidden_out,
        hidden_grad,
        gains_share,
        query_share,
        key_share,
        value_share,
        head_share,
        output_share,
        gate_share,
        up_share,
        down_share,
    )


def solution(mesh):
    placed = (
        P(("seq", "ctx"), None),
        P(("seq", "ctx"), None),
        P("seq"),
        P(("seq", "ctx")),
        P(("seq", "ctx"), None),
        P(("seq", "ctx"), None),
        P(("seq", "ctx"), None),
        P(("seq", "ctx"), None),
        P(("seq", "ctx"), None),
        P(("seq", "ctx"), None),
        P(("seq", "ctx"), None),
        P(("seq", "ctx"), None),
    )
    return jax.shard_map(
        on_device,
        mesh=mesh,
        in_specs=placed,
        out_specs=(
            P(("seq", "ctx"), None),
            P(("seq", "ctx"), None),
            P(("seq", "ctx")),
            P(("seq", "ctx"), None),
            P(("seq", "ctx"), None),
            P(("seq", "ctx"), None),
            P(("seq", "ctx"), None),
            P(("seq", "ctx"), None),
            P(("seq", "ctx"), None),
            P(("seq", "ctx"), None),
            P(("seq", "ctx"), None),
        ),
        check_vma=False,
    )
```

profile of v0, /device:TPU:1, one launch (start us, length us, event | category | flops | bytes accessed | tf_op | source)
XLA Modules:
  0.0 3129.4 jit_solution(9583039066270076540)
XLA Ops:
  12.1 41.2 %all-reduce.4 = bf16[4352]{0:T(1024)(128)(2,1)S(1)} all-reduce(bf16[4352]{0:T(1024)(128)(2,1)S(1)} %dynamic-update-slice), channel_id=1, replica_groups=mesh['seq'=4,'ctx'=8] {'seq','ctx'}, use_global_device_ids=true, to_apply=%add.4 | all-reduce | flops 4352 | bytes 17408
  55.1 21.2 all-gather.11.cloned.1.call-done
  81.9 58.7 %all-gather.17.cloned.1.call-done = bf16[2048,1024]{1,0:T(8,128)(2,1)} async-done(((bf16[64,1024]{1,0:T(8,128)(2,1)}), bf16[2048,1024]{1,0:T(8,128)(2,1)}) %all-gather.17.cloned.1.call-update) | async-done | bytes 4194320 | tf_op jit(solution)/shard_map/all_gather | solution.py:196
  154.1 40.9 %all-gather = bf16[32,64,16]{1,2,0:T(8,128)(2,1)S(1)} all-gather(bf16[1,64,16]{1,2,0:T(8,128)(2,1)S(1)} %convert_bitcast_fusion.1), channel_id=1, replica_groups=mesh['seq'=4,'ctx'=8] {'seq','ctx'}, dimensions={0}, use_global_device_ids=true | all-gather | bytes 67584 | tf_op jit(solution)/shard_map/all_gather | solution.py:197
  205.2 76.9 %all-gather.15.cloned.1.call-done = bf16[2048,2048]{1,0:T(8,128)(2,1)} async-done(((bf16[64,2048]{1,0:T(8,128)(2,1)}), bf16[2048,2048]{1,0:T(8,128)(2,1)}) %all-gather.15.cloned.1.call-update) | async-done | bytes 8388624 | tf_op jit(solution)/shard_map/all_gather | solution.py:194
  322.9 38.7 %all-gather.21.cloned.1.call-done = bf16[2048,2048]{1,0:T(8,128)(2,1)} async-done(((bf16[64,2048]{1,0:T(8,128)(2,1)}), bf16[2048,2048]{1,0:T(8,128)(2,1)}) %all-gather.21.cloned.1.call-update) | async-done | bytes 8388624 | tf_op jit(solution)/shard_map/all_gather | solution.py:198
  368.5 149.4 %all-gather.23.cloned.1.call-done = bf16[2048,6144]{1,0:T(8,128)(2,1)} async-done(((bf16[64,6144]{1,0:T(8,128)(2,1)}), bf16[2048,6144]{1,0:T(8,128)(2,1)}) %all-gather.23.cloned.1.call-update) | async-done | bytes 25165840 | tf_op jit(solution)/shard_map/all_gather | solution.py:234
  531.3 142.5 %all-gather.25.cloned.1.call-done = bf16[2048,6144]{1,0:T(8,128)(2,1)} async-done(((bf16[64,6144]{1,0:T(8,128)(2,1)}), bf16[2048,6144]{1,0:T(8,128)(2,1)}) %all-gather.25.cloned.1.call-update) | async-done | bytes 25165840 | tf_op jit(solution)/shard_map/all_gather | solution.py:235
  687.2 142.4 %all-gather.27.cloned.1.call-done = bf16[6144,2048]{1,0:T(8,128)(2,1)} async-done(((bf16[192,2048]{1,0:T(8,128)(2,1)}), bf16[6144,2048]{1,0:T(8,128)(2,1)}) %all-gather.27.cloned.1.call-update) | async-done | bytes 25165840 | tf_op jit(solution)/shard_map/all_gather | solution.py:236
  894.0 19.1 while.34
  927.1 27.5 reduce-scatter.13.cloned.1.call-done
  961.9 29.4 reduce-scatter.15.cloned.1.call-done
  1019.1 20.8 fusion.126
  1040.0 20.9 fusion.127
  1062.3 20.5 fusion.128
  1101.3 23.0 reduce-scatter.31.cloned.1.call-done
  1132.1 43.1 %all-reduce.5 = f32[4352]{0:T(1024)S(1)} all-reduce(f32[4352]{0:T(1024)S(1)} %pad_maximum_fusion.1), channel_id=4, replica_groups=mesh['seq'=4,'ctx'=8] {'seq','ctx'}, use_global_device_ids=true, to_apply=%region_26.27.clone | all-reduce | flops 4352 | bytes 34816
  1177.0 100.1 %reduce-scatter.19.cloned.1.call-done = f32[64,1024]{1,0:T(8,128)} async-done(((f32[2048,1024]{1,0:T(8,128)}), f32[64,1024]{1,0:T(8,128)}) %reduce-scatter.19.cloned.1.call-update) | async-done | bytes 262160 | tf_op jit(solution)/shard_map/reduce_scatter | solution.py:315
  1277.1 152.9 %reduce-scatter.21.cloned.1.call-done = f32[64,1024]{1,0:T(8,128)} async-done(((f32[2048,1024]{1,0:T(8,128)}), f32[64,1024]{1,0:T(8,128)}) %reduce-scatter.21.cloned.1.call-update) | async-done | bytes 262160 | tf_op jit(solution)/shard_map/reduce_scatter | solution.py:316
  1430.0 187.0 %reduce-scatter.17.cloned.1.call-done = f32[64,2048]{1,0:T(8,128)} async-done(((f32[2048,2048]{1,0:T(8,128)}), f32[64,2048]{1,0:T(8,128)}) %reduce-scatter.17.cloned.1.call-update) | async-done | bytes 524304 | tf_op jit(solution)/shard_map/reduce_scatter | solution.py:314
  1617.0 187.3 %reduce-scatter.23.cloned.1.call-done = f32[64,2048]{1,0:T(8,128)} async-done(((f32[2048,2048]{1,0:T(8,128)}), f32[64,2048]{1,0:T(8,128)}) %reduce-scatter.23.cloned.1.call-update) | async-done | bytes 524304 | tf_op jit(solution)/shard_map/reduce_scatter | solution.py:318
  1804.3 441.1 %reduce-scatter.25.cloned.1.call-done = f32[64,6144]{1,0:T(8,128)} async-done(((f32[2048,6144]{1,0:T(8,128)}), f32[64,6144]{1,0:T(8,128)}) %reduce-scatter.25.cloned.1.call-update) | async-done | bytes 1572880 | tf_op jit(solution)/shard_map/reduce_scatter | solution.py:260
  2245.4 438.5 %reduce-scatter.27.cloned.1.call-done = f32[64,6144]{1,0:T(8,128)} async-done(((f32[2048,6144]{1,0:T(8,128)}), f32[64,6144]{1,0:T(8,128)}) %reduce-scatter.27.cloned.1.call-update) | async-done | bytes 1572880 | tf_op jit(solution)/shard_map/reduce_scatter | solution.py:261
  2683.9 438.7 %reduce-scatter.29.cloned.1.call-done = f32[192,2048]{1,0:T(8,128)} async-done(((f32[6144,2048]{1,0:T(8,128)}), f32[192,2048]{1,0:T(8,128)}) %reduce-scatter.29.cloned.1.call-update) | async-done | bytes 1572880 | tf_op jit(solution)/shard_map/reduce_scatter | solution.py:252
  (317 shorter events, 289.7 us)
Async XLA Ops:
  7.2 69.2 %all-gather.11.cloned.1.call-start = ((), (), s32[]{:S(2)}) async-start(), calls=%async_computation.10 | async-start | bytes 4325376 | tf_op jit(solution)/shard_map/all_gather | solution.py:195
  8.9 131.7 %all-gather.17.cloned.1.call-start = ((), (), s32[]{:S(2)}) async-start(), calls=%async_computation.13 | async-start | bytes 4325376 | tf_op jit(solution)/shard_map/all_gather | solution.py:196
  10.6 185.7 %all-gather.13.cloned.1.call-start = ((), (), s32[]{:S(2)}) async-start(), calls=%async_computation.11 | async-start | bytes 2359296 | tf_op jit(solution)/shard_map/all_gather | solution.py:223
  11.8 289.5 %copy-start.33 = (f32[128,128]{1,0:T(8,128)}, f32[128,128]{1,0:T(8,128)S(1)}, u32[]{:S(2)}) copy-start(f32[128,128]{1,0:T(8,128)S(1)} %copy.110) | copy-start | bytes 196612
  11.9 289.4 %copy-start.31 = (f32[128,128]{1,0:T(8,128)}, f32[128,128]{1,0:T(8,128)S(1)}, u32[]{:S(2)}) copy-start(f32[128,128]{1,0:T(8,128)S(1)} %copy.109) | copy-start | bytes 196612
  54.6 227.5 %copy-start.45 = (f32[128]{0:T(128)}, f32[128]{0:T(128)S(1)}, u32[]{:S(2)}) copy-start(f32[128]{0:T(128)S(1)} %fusion.101) | copy-start | bytes 1540
  55.1 246.2 %copy-start.58 = (f32[128]{0:T(128)}, f32[128]{0:T(128)S(1)}, u32[]{:S(2)}) copy-start(f32[128]{0:T(128)S(1)} %get-tuple-element.487) | copy-start | bytes 1540
  55.1 227.0 %copy-start.22 = (f32[2048]{0:T(1024)}, f32[2048]{0:T(1024)S(1)}, u32[]{:S(2)}) copy-start(f32[2048]{0:T(1024)S(1)} %get-tuple-element.486) | copy-start | bytes 24580
  81.9 120.0 %all-gather.19.cloned.1.call-start = ((), (), s32[]{:S(2)}) async-start(), calls=%async_computation.14 | async-start | bytes 2359296 | tf_op jit(solution)/shard_map/all_gather | solution.py:224
  144.3 137.8 %all-gather.15.cloned.1.call-start = ((), (), s32[]{:S(2)}) async-start(), calls=%async_computation.12 | async-start | bytes 8650752 | tf_op jit(solution)/shard_map/all_gather | solution.py:194
  146.1 215.4 %all-gather.21.cloned.1.call-start = ((), (), s32[]{:S(2)}) async-start(), calls=%async_computation.15 | async-start | bytes 8650752 | tf_op jit(solution)/shard_map/all_gather | solution.py:198
  148.0 369.8 %all-gather.23.cloned.1.call-start = ((), (), s32[]{:S(2)}) async-start(), calls=%async_computation.16 | async-start | bytes 25952256 | tf_op jit(solution)/shard_map/all_gather | solution.py:234
  149.1 524.6 %all-gather.25.cloned.1.call-start = ((), (), s32[]{:S(2)}) async-start(), calls=%async_computation.17 | async-start | bytes 25952256 | tf_op jit(solution)/shard_map/all_gather | solution.py:235
  151.7 678.0 %all-gather.27.cloned.1.call-start = ((), (), s32[]{:S(2)}) async-start(), calls=%async_computation.18 | async-start | bytes 25952256 | tf_op jit(solution)/shard_map/all_gather | solution.py:236
  152.7 801.9 %reduce-scatter.13.cloned.1.call-start = ((), (), s32[]{:S(2)}) async-start(), calls=%async_computation.19 | async-start | bytes 2359296 | tf_op jit(solution)/shard_map/reduce_scatter | solution.py:284
  918.1 73.3 %reduce-scatter.15.cloned.1.call-start = ((), (), s32[]{:S(2)}) async-start(), calls=%async_computation.20 | async-start | bytes 2359296 | tf_op jit(solution)/shard_map/reduce_scatter | solution.py:287
  921.5 202.8 %reduce-scatter.31.cloned.1.call-start = ((), (), s32[]{:S(2)}) async-start(), calls=%async_computation.28 | async-start | bytes 1081344
  926.9 350.2 %reduce-scatter.19.cloned.1.call-start = ((), (), s32[]{:S(2)}) async-start(), calls=%async_computation.22 | async-start | bytes 8650752 | tf_op jit(solution)/shard_map/reduce_scatter | solution.py:315
  961.9 468.1 %reduce-scatter.21.cloned.1.call-start = ((), (), s32[]{:S(2)}) async-start(), calls=%async_computation.23 | async-start | bytes 8650752 | tf_op jit(solution)/shard_map/reduce_scatter | solution.py:316
  997.1 619.9 %reduce-scatter.17.cloned.1.call-start = ((), (), s32[]{:S(2)}) async-start(), calls=%async_computation.21 | async-start | bytes 17301504 | tf_op jit(solution)/shard_map/reduce_scatter | solution.py:314
  1008.5 795.8 %reduce-scatter.23.cloned.1.call-start = ((), (), s32[]{:S(2)}) async-start(), calls=%async_computation.24 | async-start | bytes 17301504 | tf_op jit(solution)/shard_map/reduce_scatter | solution.py:318
  1018.0 1227.3 %reduce-scatter.25.cloned.1.call-start = ((), (), s32[]{:S(2)}) async-start(), calls=%async_computation.25 | async-start | bytes 51904512 | tf_op jit(solution)/shard_map/reduce_scatter | solution.py:260
  1039.9 1643.9 %reduce-scatter.27.cloned.1.call-start = ((), (), s32[]{:S(2)}) async-start(), calls=%async_computation.26 | async-start | bytes 51904512 | tf_op jit(solution)/shard_map/reduce_scatter | solution.py:261
  1060.9 2061.7 %reduce-scatter.29.cloned.1.call-start = ((), (), s32[]{:S(2)}) async-start(), calls=%async_computation.27 | async-start | bytes 51904512 | tf_op jit(solution)/shard_map/reduce_scatter | solution.py:252
  (58 other events, 670.1 us)
Sparse Core Ops, SparseCore 0:
  11.6 64.6 all-gather.10
  79.9 60.6 all-gather.16
  142.8 28.3 all-gather.12
  173.2 28.6 all-gather.18
  205.3 76.7 all-gather.14
  285.5 75.9 all-gather.20
  364.5 153.2 all-gather.22
  520.8 152.8 all-gather.24
  676.7 152.8 all-gather.26
  918.2 36.3 reduce-scatter.12
  956.9 34.3 reduce-scatter.14
  993.5 130.7 reduce-scatter.30
  1127.3 149.7 reduce-scatter.18
  1279.9 150.0 reduce-scatter.20
  1432.8 184.1 reduce-scatter.16
  1619.8 184.3 reduce-scatter.22
  1812.2 433.0 reduce-scatter.24
  2253.4 430.4 reduce-scatter.26
  2692.0 430.5 reduce-scatter.28
where the time goes:
time: 3140 us; the launch traced here: 3130 us
  waiting for transfers between devices  2660 us (85%)
  matrix products  224 us (7%)
  blocking collectives  125 us (4%)
  local copies, waits for them, and re-layouts  61.5 us (2%)
  other arithmetic  37.9 us (1%)
    reduce_scatter x1, waiting for transfers between devices, on_device(): lax.psum_scatter(gate_term, ('seq', 'ctx'), scatter_dimension=0, tiled=True)  441 us
    reduce_scatter x1, waiting for transfers between devices, on_device(): lax.psum_scatter(down_term, ('seq', 'ctx'), scatter_dimension=0, tiled=True)  439 us
    reduce_scatter x1, waiting for transfers between devices, on_device(): lax.psum_scatter(up_term, ('seq', 'ctx'), scatter_dimension=0, tiled=True)  438 us
    dot_general x23, matrix products, product(): return jnp.dot(left_side, right_side, preferred_element_type=jnp.float32)  213 us
    reduce_scatter x1, waiting for transfers between devices, on_device(): lax.psum_scatter(output_term, ('seq', 'ctx'), scatter_dimension=0, tiled=...  187 us
    reduce_scatter x1, waiting for transfers between devices, on_device(): lax.psum_scatter(query_term, ('seq', 'ctx'), scatter_dimension=0, tiled=T...  187 us
    reduce_scatter x1, waiting for transfers between devices, on_device(): lax.psum_scatter(value_term, ('seq', 'ctx'), scatter_dimension=0, tiled=T...  153 us
    all_gather x1, waiting for transfers between devices, on_device(): lax.all_gather(gate_weight.astype(jnp.bfloat16), ('seq', 'ctx'), axis=0,...  149 us
  transfers between devices with their start and end apart: 19, of which 18 were waited for; matrix products, arithmetic and copies ran while one was open for 7% of the time, Pallas kernels for 0%

commit v1 on v0

v1 whole, which is shorter than its diff:
```python
from functools import partial

import jax
import jax.numpy as jnp
from jax import lax
from jax.sharding import PartitionSpec as P

H = 16
KV = 8
HD = 128


epsilon = 1e-06
rope_base = 1000000.0
negative = -1e30
low = jnp.bfloat16


def product(left_side, right_side):
    return jnp.dot(left_side, right_side, preferred_element_type=jnp.float32)


def product_nt(left_side, right_side):
    return lax.dot_general(
        left_side, right_side, (((1,), (1,)), ((), ())), preferred_element_type=jnp.float32
    )


def product_tn(left_side, right_side):
    return lax.dot_general(
        left_side, right_side, (((0,), (0,)), ((), ())), preferred_element_type=jnp.float32
    )


def rms_scale(values, gain_vector):
    inverse = lax.rsqrt(jnp.mean(values * values, axis=-1, keepdims=True) + epsilon)
    return values * inverse * gain_vector


def rope_tables(positions, head_width):
    half_width = head_width // 2
    inverse = rope_base ** (-jnp.arange(half_width, dtype=jnp.float32) * 2.0 / head_width)
    angles = positions.astype(jnp.float32)[:, None] * inverse[None, :]
    angles = jnp.concatenate([angles, angles], axis=-1)
    return (jnp.cos(angles)[:, None, :], jnp.sin(angles)[:, None, :])


def rotate(values, cosine_table, sine_table):
    half_width = values.shape[-1] // 2
    turned = jnp.concatenate([-values[..., half_width:], values[..., :half_width]], axis=-1)
    return values * cosine_table + turned * sine_table


def qk_piece(query_raw, key_raw, query_gain, key_gain, cosine_table, sine_table):
    queries = rms_scale(query_raw, query_gain)
    keys = rms_scale(key_raw, key_gain)
    return (rotate(queries, cosine_table, sine_table), rotate(keys, cosine_table, sine_table))


def gate_heads(attended, gate_raw):
    return attended * jax.nn.sigmoid(gate_raw)[:, :, None]


def swiglu(gate_pre, up_pre):
    return jax.nn.silu(gate_pre) * up_pre


def gather_ctx(block):
    return lax.all_gather(block, "ctx", axis=0, tiled=True)


def gather_seq(block):
    return lax.all_gather(block, "seq", axis=0, tiled=True)


def scatter_ctx(block):
    return lax.psum_scatter(block.astype(low), "ctx", scatter_dimension=0, tiled=True).astype(
        jnp.float32
    )


def scatter_seq(block):
    return lax.psum_scatter(block.astype(low), "seq", scatter_dimension=0, tiled=True)


def to_columns(block):
    rows, pieces, width = block.shape
    return lax.all_to_all(block, "ctx", split_axis=1, concat_axis=0, tiled=True).reshape(
        pieces * rows, width
    )


def to_rows(block, pieces):
    rows = block.shape[0] // pieces
    block = block.reshape(pieces * rows, 1, block.shape[1])
    return lax.all_to_all(block, "ctx", split_axis=0, concat_axis=1, tiled=True)


def on_device(
    hidden_in,
    out_grad,
    prefix_len,
    norm_gains,
    query_weight,
    key_weight,
    value_weight,
    head_gate_weight,
    out_weight,
    gate_weight,
    up_weight,
    down_weight,
):
    row_count, model = hidden_in.shape
    groups = lax.axis_size("seq")
    pieces = lax.axis_size("ctx")
    length = row_count * pieces
    weight_rows = query_weight.shape[0]
    heads = H // pieces
    kv_heads = max(1, KV // pieces)
    copies = max(1, pieces // KV)
    per_kv = heads // kv_heads
    ff_block = down_weight.shape[0]
    ff_own = ff_block * groups
    prefix = prefix_len[0]
    q_width, kv_width = heads * HD, kv_heads * HD
    attn_width = -(-(q_width + 2 * kv_width + heads) // 128) * 128

    def kv_columns(weight):
        columns = weight.astype(low).reshape(weight_rows, KV, HD)
        return jnp.repeat(columns, copies, axis=1).reshape(weight_rows, pieces, kv_width)

    def ff_columns(weight):
        columns = weight.astype(low).reshape(weight_rows, groups, pieces, ff_block)
        return columns.transpose(0, 2, 1, 3).reshape(weight_rows, pieces, ff_own)

    attn_rows = jnp.concatenate(
        [
            query_weight.astype(low).reshape(weight_rows, pieces, q_width),
            kv_columns(key_weight),
            kv_columns(value_weight),
            head_gate_weight.astype(low).reshape(weight_rows, pieces, heads),
            jnp.zeros(
                (weight_rows, pieces, attn_width - q_width - 2 * kv_width - heads), low
            ),
        ],
        axis=-1,
    )
    attn_low = gather_seq(to_columns(attn_rows))
    ff_rows = jnp.concatenate([ff_columns(gate_weight), ff_columns(up_weight)], axis=-1)
    ff_low = gather_seq(to_columns(ff_rows))
    down_low = gather_seq(down_weight.astype(low))
    spread = [(i, (i % groups) * pieces + i // groups) for i in range(groups * pieces)]
    collect = [(target, source) for source, target in spread]
    out_low = gather_seq(lax.ppermute(out_weight.astype(low), ("seq", "ctx"), spread))
    gains_full = lax.all_gather(
        norm_gains.astype(low), ("seq", "ctx"), axis=0, tiled=True
    ).astype(jnp.float32)
    attention_gain = gains_full[:model]
    swiglu_gain = gains_full[model : 2 * model]
    query_gain = gains_full[2 * model : 2 * model + HD]
    key_gain = gains_full[2 * model + HD :]

    residual_in = hidden_in.astype(jnp.float32)
    normed_local, pull_norm_one = jax.vjp(rms_scale, residual_in, attention_gain)
    normed = gather_ctx(normed_local.astype(low))
    out_grad_all = gather_ctx(out_grad)
    raw = product(normed, attn_low)
    query_raw = raw[:, :q_width].reshape(length, heads, HD)
    key_raw = raw[:, q_width : q_width + kv_width].reshape(length, kv_heads, HD)
    values = raw[:, q_width + kv_width : q_width + 2 * kv_width].astype(low)
    values = values.reshape(length, kv_heads, HD)
    gate_raw = raw[:, q_width + 2 * kv_width : q_width + 2 * kv_width + heads]
    positions = jnp.arange(length, dtype=jnp.int32)
    cosine_table, sine_table = rope_tables(positions, HD)
    (queries_full, keys_full), pull_rope = jax.vjp(
        partial(qk_piece, cosine_table=cosine_table, sine_table=sine_table),
        query_raw,
        key_raw,
        query_gain,
        key_gain,
    )
    queries = queries_full.astype(low).reshape(length, kv_heads, per_kv, HD)
    keys = keys_full.astype(low)
    limits = jnp.maximum(positions, prefix - 1)
    allowed = positions[None, :] <= limits[:, None]
    score_scale = HD ** (-0.5)
    scores = (
        jnp.einsum("tkgd,skd->kgts", queries, keys, preferred_element_type=jnp.float32)
        * score_scale
    )
    scores = jnp.where(allowed, scores, negative)
    row_max = jnp.max(scores, axis=-1, keepdims=True)
    expanded = jnp.exp(scores - row_max)
    row_sum = jnp.sum(expanded, axis=-1, keepdims=True)
    log_norm = row_max + jnp.log(row_sum)
    attended = (
        jnp.einsum("kgts,skd->kgtd", expanded.astype(low), values, preferred_element_type=jnp.float32)
        / row_sum
    )
    attended_rows = attended.transpose(2, 0, 1, 3).reshape(length, heads, HD)
    gated_full, pull_gate = jax.vjp(gate_heads, attended_rows, gate_raw)
    gated = gated_full.astype(low).reshape(length, q_width)
    middle = residual_in + scatter_ctx(product(gated, out_low))

    normed_two_local, pull_norm_two = jax.vjp(rms_scale, middle, swiglu_gain)
    normed_two = gather_ctx(normed_two_local.astype(low))
    pre = product(normed_two, ff_low)
    gate_pre, up_pre = pre[:, :ff_own], pre[:, ff_own:]
    hidden_ff_full, pull_swiglu = jax.vjp(swiglu, gate_pre, up_pre)
    hidden_ff = hidden_ff_full.astype(low)
    hidden_out = (middle + scatter_ctx(product(hidden_ff, down_low))).astype(low)

    grad_hidden_ff = product_nt(out_grad_all, down_low)
    grad_gate_full, grad_up_full = pull_swiglu(grad_hidden_ff)
    grad_pre = jnp.concatenate([grad_gate_full.astype(low), grad_up_full.astype(low)], axis=-1)
    grad_normed_two = scatter_ctx(product_nt(grad_pre, ff_low))
    down_share = scatter_seq(product_tn(hidden_ff, out_grad_all)).astype(jnp.float32)
    ff_share = to_rows(scatter_seq(product_tn(normed_two, grad_pre)), pieces).astype(jnp.float32)

    def ff_back(columns):
        columns = columns.reshape(weight_rows, pieces, groups, ff_block)
        return columns.transpose(0, 2, 1, 3).reshape(weight_rows, groups * pieces * ff_block)

    gate_share = ff_back(ff_share[:, :, :ff_own])
    up_share = ff_back(ff_share[:, :, ff_own:])

    grad_middle_part, swiglu_gain_grad = pull_norm_two(grad_normed_two)
    grad_middle = out_grad.astype(jnp.float32) + grad_middle_part
    grad_branch = gather_ctx(grad_middle.astype(low))
    grad_gated = product_nt(grad_branch, out_low).reshape(length, heads, HD)
    output_share = lax.ppermute(
        scatter_seq(product_tn(gated, grad_branch)), ("seq", "ctx"), collect
    ).astype(jnp.float32)
    grad_attended_full, grad_gate_raw_full = pull_gate(grad_gated)
    grad_attended = grad_attended_full.astype(low)
    grad_heads = grad_attended.reshape(length, kv_heads, per_kv, HD).transpose(1, 2, 0, 3)
    row_delta = jnp.sum(grad_heads.astype(jnp.float32) * attended, axis=-1, keepdims=True)
    probabilities = jnp.exp(scores - log_norm)
    prob_grad = jnp.einsum(
        "kgtd,skd->kgts", grad_heads, values, preferred_element_type=jnp.float32
    )
    score_grad = (probabilities * (prob_grad - row_delta)).astype(low)
    grad_queries = (
        jnp.einsum("kgts,skd->tkgd", score_grad, keys, preferred_element_type=jnp.float32)
        * score_scale
    )
    grad_keys = (
        jnp.einsum("kgts,tkgd->skd", score_grad, queries, preferred_element_type=jnp.float32)
        * score_scale
    )
    grad_values = jnp.einsum(
        "kgts,kgtd->skd", probabilities.astype(low), grad_heads, preferred_element_type=jnp.float32
    )
    grad_query_full, grad_key_full, query_gain_grad, key_gain_grad = pull_rope(
        (grad_queries.reshape(length, heads, HD), grad_keys)
    )
    grad_raw = jnp.concatenate(
        [
            grad_query_full.reshape(length, q_width).astype(low),
            grad_key_full.reshape(length, kv_width).astype(low),
            grad_values.reshape(length, kv_width).astype(low),
            grad_gate_raw_full.astype(low),
            jnp.zeros((length, attn_width - q_width - 2 * kv_width - heads), low),
        ],
        axis=-1,
    )
    grad_normed = scatter_ctx(product_nt(grad_raw, attn_low))
    attn_share = to_rows(scatter_seq(product_tn(normed, grad_raw)), pieces).astype(jnp.float32)

    def kv_back(columns):
        columns = columns.reshape(weight_rows, KV, copies, HD)
        return columns.sum(axis=2).reshape(weight_rows, KV * HD)

    query_share = attn_share[:, :, :q_width].reshape(weight_rows, H * HD)
    key_share = kv_back(attn_share[:, :, q_width : q_width + kv_width])
    value_share = kv_back(attn_share[:, :, q_width + kv_width : q_width + 2 * kv_width])
    head_share = attn_share[
        :, :, q_width + 2 * kv_width : q_width + 2 * kv_width + heads
    ].reshape(weight_rows, H)
    grad_input_part, attention_gain_grad = pull_norm_one(grad_normed)
    hidden_grad = (grad_middle + grad_input_part).astype(low)
    gains_term = jnp.concatenate(
        [attention_gain_grad, swiglu_gain_grad, query_gain_grad, key_gain_grad]
    )
    gains_share = lax.psum_scatter(gains_term, ("seq", "ctx"), scatter_dimension=0, tiled=True)
    return (
        hidden_out,
        hidden_grad,
        gains_share,
        query_share,
        key_share,
        value_share,
        head_share,
        output_share,
        gate_share,
        up_share,
        down_share,
    )


def solution(mesh):
    rows = P(("seq", "ctx"), None)
    return jax.shard_map(
        on_device,
        mesh=mesh,
        in_specs=(rows, rows, P("seq"), P(("seq", "ctx"))) + (rows,) * 8,
        out_specs=(rows, rows, P(("seq", "ctx"))) + (rows,) * 8,
        check_vma=False,
    )
```

time: 3140 us -> 898 us (0.29)
  waiting for transfers between devices: 2660 us -> 461 us
  matrix products: 224 us -> 109 us
  blocking collectives: 125 us -> 161 us
    reduce_scatter x9 -> x8, waiting for transfers between devices: 2000 us -> 184 us  [the longest x4 107 us: scatter_seq(): lax.psum_scatter(block.astype(low), 'seq', scatter_dimension=0, tiled=True)]
    all_gather x9 -> x8, waiting for transfers between devices: 633 us -> 254 us  [the longest x4 154 us: gather_ctx(): return lax.all_gather(block, 'ctx', axis=0, tiled=True)]
    dot_general x23 -> x4, matrix products: 213 us -> 28.8 us  [product(): return jnp.dot(left_side, right_side, preferred_element_type=jnp.float32)]
    all_to_all x0 -> x2, blocking collectives: none -> 81.8 us  [to_columns(): lax.all_to_all(block, 'ctx', split_axis=1, concat_axis=0, tiled=True)]
    dot_general x7 -> x14, matrix products: 9.66 us -> 80.4 us  [the longest x4 32.7 us: product_nt(): lax.dot_general(left_side, right_side, (((1,), (1,)), ((), ())), preferre...]
    all_gather x1 -> x0, blocking collectives: 40.9 us -> none  [on_device(): lax.all_gather(head_gate_weight.astype(jnp.bfloat16), ('seq', 'ctx'), axi...]
  transfers between devices with their start and end apart: 19 -> 20, of which waited for: 18 -> 15; matrix products, arithmetic and copies ran while one was open for 7% -> 21% of each run, Pallas kernels for 0% -> 0%
where the time goes in v1:
time: 898 us; the launch traced here: 891 us
  waiting for transfers between devices  461 us (51%)
  blocking collectives  161 us (18%)
  matrix products  109 us (12%)
  local copies, waits for them, and re-layouts  65.2 us (7%)
  other arithmetic  55.8 us (6%)
  starting transfers between devices  22.1 us (2%)
  between operations  16 us (2%)
    all_gather x4, waiting for transfers between devices, gather_ctx(): return lax.all_gather(block, 'ctx', axis=0, tiled=True)  154 us
    reduce_scatter x4, waiting for transfers between devices, scatter_seq(): lax.psum_scatter(block.astype(low), 'seq', scatter_dimension=0, tiled=True)  107 us
    all_gather x4, waiting for transfers between devices, gather_seq(): return lax.all_gather(block, 'seq', axis=0, tiled=True)  100 us
    all_to_all x2, blocking collectives, to_columns(): lax.all_to_all(block, 'ctx', split_axis=1, concat_axis=0, tiled=True)  81.8 us
    unnamed x2, blocking collectives  79.4 us
    reduce_scatter x4, waiting for transfers between devices, scatter_ctx(): lax.psum_scatter(block.astype(low), 'ctx', scatter_dimension=0, tiled=True)  77.1 us
    dot_general x4, matrix products, product_nt(): lax.dot_general(left_side, right_side, (((1,), (1,)), ((), ())), preferre...  32.7 us
    dot_general x4, matrix products, product_tn(): lax.dot_general(left_side, right_side, (((0,), (0,)), ((), ())), preferre...  31.3 us
  transfers between devices with their start and end apart: 20, of which 15 were waited for; matrix products, arithmetic and copies ran while one was open for 21% of the time, Pallas kernels for 0%

profile of v1, /device:TPU:1, one launch (start us, length us, event | category | flops | bytes accessed | tf_op | source)
XLA Modules:
  0.0 890.8 jit_solution(8673287428202948809)
XLA Ops:
  11.8 23.6 %all_to_all.48 = bf16[64,8,640]{2,0,1:T(8,128)(2,1)} all-to-all(bf16[64,8,640]{2,0,1:T(8,128)(2,1)S(1)} %copy.84), channel_id=1, replica_groups=mesh['seq'=4,'ctx'=8] {'ctx'}, dimensions={1} | all-to-all | bytes 1310720 | tf_op jit(solution)/shard_map/all_to_all | solution.py:88
  35.8 39.6 %all-reduce.4 = bf16[4352]{0:T(1024)(128)(2,1)S(1)} all-reduce(bf16[4352]{0:T(1024)(128)(2,1)S(1)} %dynamic-update-slice), channel_id=1, replica_groups=mesh['seq'=4,'ctx'=8] {'seq','ctx'}, use_global_device_ids=true, to_apply=%add.4 | all-reduce | flops 4352 | bytes 17408
  84.6 22.0 %collective-permute-done = bf16[64,2048]{1,0:T(8,128)(2,1)S(1)} collective-permute-done((bf16[64,2048]{1,0:T(8,128)(2,1)S(1)}, bf16[64,2048]{1,0:T(8,128)(2,1)S(1)}, u32[]{:S(2)}, u32[]{:S(2)}) %collective-permute-start) | collective-permute-done | bytes 262176 | tf_op jit(solution)/shard_map/ppermute | solution.py:154
  107.9 26.9 %all-gather.9.cloned.1.call-done = bf16[1024,2048]{1,0:T(8,128)(2,1)} async-done(((bf16[128,2048]{1,0:T(8,128)(2,1)}), bf16[1024,2048]{1,0:T(8,128)(2,1)}) %all-gather.9.cloned.1.call-update) | async-done | bytes 4194320 | tf_op jit(solution)/shard_map/all_gather | solution.py:69
  190.0 58.2 %all_to_all.49 = bf16[64,8,1536]{2,0,1:T(8,128)(2,1)} all-to-all(bf16[64,8,1536]{2,0,1:T(8,128)(2,1)S(1)} %copy.90), channel_id=1, replica_groups=mesh['seq'=4,'ctx'=8] {'ctx'}, dimensions={1} | all-to-all | bytes 3145728 | tf_op jit(solution)/shard_map/all_to_all | solution.py:88
  255.2 62.8 %all-gather.17.cloned.1.call-done = bf16[2048,1536]{1,0:T(8,128)(2,1)} async-done(((bf16[512,1536]{1,0:T(8,128)(2,1)}), bf16[2048,1536]{1,0:T(8,128)(2,1)}) %all-gather.17.cloned.1.call-update) | async-done | bytes 6291472 | tf_op jit(solution)/shard_map/all_gather | solution.py:73
  317.9 49.6 %all-gather.15.cloned.1.call-done = bf16[1024,2048]{1,0:T(8,128)(2,1)} async-done(((bf16[128,2048]{1,0:T(8,128)(2,1)}), bf16[1024,2048]{1,0:T(8,128)(2,1)}) %all-gather.15.cloned.1.call-update) | async-done | bytes 4194320 | tf_op jit(solution)/shard_map/all_gather | solution.py:69
  367.5 11.7 %fusion.101 = f32[1024,1536]{1,0:T(8,128)} fusion(bf16[1024,2048]{1,0:T(8,128)(2,1)} %all-gather.15.cloned.1.call-done, bf16[2048,1536]{1,0:T(8,128)(2,1)} %all-gather.17.cloned.1.call-done), kind=kOutput, calls=%fused_computation.185 | convolution fusion | flops 6442450944 | bytes 16777216 | tf_op jit(solution)/shard_map/dot_general | solution.py:20
  379.2 33.1 %all-gather.19.cloned.1.call-done = bf16[768,2048]{1,0:T(8,128)(2,1)} async-done(((bf16[192,2048]{1,0:T(8,128)(2,1)}), bf16[768,2048]{1,0:T(8,128)(2,1)}) %all-gather.19.cloned.1.call-update) | async-done | bytes 3145744 | tf_op jit(solution)/shard_map/all_gather | solution.py:73
  412.3 49.2 %all-gather.21.cloned.1.call-done = bf16[1024,2048]{1,0:T(8,128)(2,1)} async-done(((bf16[128,2048]{1,0:T(8,128)(2,1)}), bf16[1024,2048]{1,0:T(8,128)(2,1)}) %all-gather.21.cloned.1.call-update) | async-done | bytes 4194320 | tf_op jit(solution)/shard_map/all_gather | solution.py:69
  461.4 10.5 %fusion.16 = (bf16[1024,768]{1,0:T(8,128)(2,1)S(1)}, bf16[1024,768]{1,0:T(8,128)(2,1)S(1)}, bf16[1024,768]{1,0:T(8,128)(2,1)}) fusion(f32[1024,1536]{1,0:T(8,128)} %fusion.101, bf16[1024,2048]{1,0:T(8,128)(2,1)} %all-gather.21.cloned.1.call-done, bf16[768,2048]{1,0:T(8,128)(2,1)} %all-gather.19.cloned.1.call-done), kind=kOutput, calls=%fused_computation.27 | convolution fusion | flops 3233808384 | bytes 18350080 | tf_op jit(solution)/shard_map/dot_general | solution.py:24
  473.6 11.0 %convolution_convert_fusion.1 = bf16[1024,2048]{1,0:T(8,128)(2,1)} fusion(bf16[2048,1536]{1,0:T(8,128)(2,1)} %all-gather.17.cloned.1.call-done, bf16[1024,768]{1,0:T(8,128)(2,1)S(1)} %get-tuple-element.24, bf16[1024,768]{1,0:T(8,128)(2,1)S(1)} %get-tuple-element.23), kind=kOutput, calls=%fused_computation.19 | convolution fusion | flops 6450839552 | bytes 13631488 | tf_op jit(solution)/shard_map/dot_general | solution.py:24
  484.7 46.3 %reduce-scatter.13.cloned.1.call-done = bf16[128,2048]{1,0:T(8,128)(2,1)} async-done(((bf16[1024,2048]{1,0:T(8,128)(2,1)}), bf16[128,2048]{1,0:T(8,128)(2,1)}) %reduce-scatter.13.cloned.1.call-update) | async-done | bytes 524304 | tf_op jit(solution)/shard_map/reduce_scatter | solution.py:77
  535.8 11.2 %convolution_convert_fusion = bf16[2048,1536]{1,0:T(8,128)(2,1)} fusion(bf16[1024,2048]{1,0:T(8,128)(2,1)} %all-gather.15.cloned.1.call-done, bf16[1024,768]{1,0:T(8,128)(2,1)} %copy-done.40, bf16[1024,768]{1,0:T(8,128)(2,1)} %copy-done.39), kind=kOutput, calls=%fused_computation.5 | convolution fusion | flops 6451888128 | bytes 13631488 | tf_op jit(solution)/shard_map/dot_general | solution.py:30
  547.1 7.8 convolution_convert_fusion.5
  555.0 28.4 %all-gather.23.cloned.1.call-done = bf16[1024,2048]{1,0:T(8,128)(2,1)} async-done(((bf16[128,2048]{1,0:T(8,128)(2,1)}), bf16[1024,2048]{1,0:T(8,128)(2,1)}) %all-gather.23.cloned.1.call-update) | async-done | bytes 4194320 | tf_op jit(solution)/shard_map/all_gather | solution.py:69
  606.8 7.7 convolution_convert_fusion.6
  634.8 20.1 %reduce-scatter.21.cloned.1.call-done = bf16[512,1536]{1,0:T(8,128)(2,1)} async-done(((bf16[2048,1536]{1,0:T(8,128)(2,1)}), bf16[512,1536]{1,0:T(8,128)(2,1)}) %reduce-scatter.21.cloned.1.call-update) | async-done | bytes 1572880 | tf_op jit(solution)/shard_map/reduce_scatter | solution.py:83
  666.4 35.3 %reduce-scatter.23.cloned.1.call-done = bf16[192,2048]{1,0:T(8,128)(2,1)} async-done(((bf16[768,2048]{1,0:T(8,128)(2,1)}), bf16[192,2048]{1,0:T(8,128)(2,1)}) %reduce-scatter.23.cloned.1.call-update) | async-done | bytes 786448 | tf_op jit(solution)/shard_map/reduce_scatter | solution.py:83
  708.1 36.1 %reduce-scatter.17.cloned.1.call-done = bf16[512,640]{1,0:T(8,128)(2,1)} async-done(((bf16[2048,640]{1,0:T(8,128)(2,1)}), bf16[512,640]{1,0:T(8,128)(2,1)}) %reduce-scatter.17.cloned.1.call-update) | async-done | bytes 655376 | tf_op jit(solution)/shard_map/reduce_scatter | solution.py:83
  759.9 15.5 %reduce-scatter.19.cloned.1.call-done = bf16[64,2048]{1,0:T(8,128)(2,1)} async-done(((bf16[256,2048]{1,0:T(8,128)(2,1)}), bf16[64,2048]{1,0:T(8,128)(2,1)}) %reduce-scatter.19.cloned.1.call-update) | async-done | bytes 262160 | tf_op jit(solution)/shard_map/reduce_scatter | solution.py:83
  807.9 22.8 %reduce-scatter.15.cloned.1.call-done = bf16[128,2048]{1,0:T(8,128)(2,1)} async-done(((bf16[1024,2048]{1,0:T(8,128)(2,1)}), bf16[128,2048]{1,0:T(8,128)(2,1)}) %reduce-scatter.15.cloned.1.call-update) | async-done | bytes 524304 | tf_op jit(solution)/shard_map/reduce_scatter | solution.py:77
  832.3 39.7 %all-reduce.5 = f32[4352]{0:T(1024)S(1)} all-reduce(f32[4352]{0:T(1024)S(1)} %pad_maximum_fusion.6), channel_id=6, replica_groups=mesh['seq'=4,'ctx'=8] {'seq','ctx'}, use_global_device_ids=true, to_apply=%region_20.21.clone | all-reduce | flops 4352 | bytes 34816
  872.8 8.0 reduce-scatter.11.cloned.1.call-done
  (242 shorter events, 197.7 us)
Async XLA Ops:
  7.2 100.7 %all-gather.11.cloned.1.call-start = ((), (), s32[]{:S(2)}) async-start(), calls=%async_computation.13 | async-start | bytes 3276800 | tf_op jit(solution)/shard_map/all_gather | solution.py:73
  35.4 99.4 %all-gather.9.cloned.1.call-start = ((), (), s32[]{:S(2)}) async-start(), calls=%async_computation.12 | async-start | bytes 4718592 | tf_op jit(solution)/shard_map/all_gather | solution.py:69
  76.6 84.1 %all-gather.13.cloned.1.call-start = ((), (), s32[]{:S(2)}) async-start(), calls=%async_computation.14 | async-start | bytes 1310720 | tf_op jit(solution)/shard_map/all_gather | solution.py:73
  76.7 29.8 %collective-permute-start = (bf16[64,2048]{1,0:T(8,128)(2,1)S(1)}, bf16[64,2048]{1,0:T(8,128)(2,1)S(1)}, u32[]{:S(2)}, u32[]{:S(2)}) collective-permute-start(bf16[64,2048]{1,0:T(8,128)(2,1)S(1)} %convert_element_type.222), channel_id=1, source_target_pairs={{0,0},{1,8},{2,16},{3,24},{4,1},{5,9},{6,17},{7,25},{8,2},{9,10},{... | collective-permute-start | bytes 786440 | tf_op jit(solution)/shard_map/ppermute | solution.py:154
  107.3 141.0 %reduce-scatter.9.cloned.1.call-start = ((), (), s32[]{:S(2)}) async-start(), calls=%async_computation.15 | async-start | bytes 4718592 | tf_op jit(solution)/shard_map/reduce_scatter | solution.py:77
  165.4 152.5 %all-gather.17.cloned.1.call-start = ((), (), s32[]{:S(2)}) async-start(), calls=%async_computation.17 | async-start | bytes 7864320 | tf_op jit(solution)/shard_map/all_gather | solution.py:73
  248.2 119.3 %all-gather.15.cloned.1.call-start = ((), (), s32[]{:S(2)}) async-start(), calls=%async_computation.16 | async-start | bytes 4718592 | tf_op jit(solution)/shard_map/all_gather | solution.py:69
  249.6 283.1 %copy-start.27 = (f32[128]{0:T(128)}, f32[128]{0:T(128)S(1)}, u32[]{:S(2)}) copy-start(f32[128]{0:T(128)S(1)} %fusion.85) | copy-start | bytes 1540
  251.7 160.6 %all-gather.19.cloned.1.call-start = ((), (), s32[]{:S(2)}) async-start(), calls=%async_computation.18 | async-start | bytes 3932160 | tf_op jit(solution)/shard_map/all_gather | solution.py:73
  254.1 207.3 %all-gather.21.cloned.1.call-start = ((), (), s32[]{:S(2)}) async-start(), calls=%async_computation.20 | async-start | bytes 4718592 | tf_op jit(solution)/shard_map/all_gather | solution.py:69
  254.9 276.1 %reduce-scatter.13.cloned.1.call-start = ((), (), s32[]{:S(2)}) async-start(), calls=%async_computation.21 | async-start | bytes 4718592 | tf_op jit(solution)/shard_map/reduce_scatter | solution.py:77
  484.7 98.7 %all-gather.23.cloned.1.call-start = ((), (), s32[]{:S(2)}) async-start(), calls=%async_computation.22 | async-start | bytes 4718592 | tf_op jit(solution)/shard_map/all_gather | solution.py:69
  535.3 119.6 %reduce-scatter.21.cloned.1.call-start = ((), (), s32[]{:S(2)}) async-start(), calls=%async_computation.26 | async-start | bytes 7864320 | tf_op jit(solution)/shard_map/reduce_scatter | solution.py:83
  547.0 154.7 %reduce-scatter.23.cloned.1.call-start = ((), (), s32[]{:S(2)}) async-start(), calls=%async_computation.27 | async-start | bytes 3932160 | tf_op jit(solution)/shard_map/reduce_scatter | solution.py:83
  554.9 189.4 %reduce-scatter.17.cloned.1.call-start = ((), (), s32[]{:S(2)}) async-start(), calls=%async_computation.24 | async-start | bytes 3276800 | tf_op jit(solution)/shard_map/reduce_scatter | solution.py:83
  614.5 160.9 %reduce-scatter.19.cloned.1.call-start = ((), (), s32[]{:S(2)}) async-start(), calls=%async_computation.25 | async-start | bytes 1310720 | tf_op jit(solution)/shard_map/reduce_scatter | solution.py:83
  619.4 211.4 %reduce-scatter.15.cloned.1.call-start = ((), (), s32[]{:S(2)}) async-start(), calls=%async_computation.23 | async-start | bytes 4718592 | tf_op jit(solution)/shard_map/reduce_scatter | solution.py:77
  626.4 254.4 %reduce-scatter.11.cloned.1.call-start = ((), (), s32[]{:S(2)}) async-start(), calls=%async_computation.19 | async-start | bytes 4718592 | tf_op jit(solution)/shard_map/reduce_scatter | solution.py:77
  661.1 43.1 %all-to-all-start.3 = ((bf16[8,2,49152]{2,1,0:T(2,128)(2,1)}), bf16[8,2,49152]{2,1,0:T(2,128)(2,1)S(1)}, u32[]{:S(2)}, u32[]{:S(2)}) async-start(bf16[8,2,49152]{2,1,0:T(2,128)(2,1)} %reshape.522), calls=%async_computation.10 | async-start | bytes 3145728 | tf_op jit(solution)/shard_map/all_to_all | solution.py:96
  747.5 54.0 %all-to-all-start.2 = ((bf16[8,2,20480]{2,1,0:T(2,128)(2,1)}), bf16[8,2,20480]{2,1,0:T(2,128)(2,1)S(1)}, u32[]{:S(2)}, u32[]{:S(2)}) async-start(bf16[8,2,20480]{2,1,0:T(2,128)(2,1)} %reshape.520), calls=%async_computation.7 | async-start | bytes 1310720 | tf_op jit(solution)/shard_map/all_to_all | solution.py:96
  775.4 25.3 %collective-permute-start.1 = (bf16[64,2048]{1,0:T(8,128)(2,1)}, bf16[64,2048]{1,0:T(8,128)(2,1)S(1)}, u32[]{:S(2)}, u32[]{:S(2)}) collective-permute-start(bf16[64,2048]{1,0:T(8,128)(2,1)} %reduce-scatter.19.cloned.1.call-done), channel_id=1, source_target_pairs={{0,0},{8,1},{16,2},{24,3},{1,4},{9,5},{17,6},{25,7},{2,8},{10,9},{... | collective-permute-start | bytes 786440 | tf_op jit(solution)/shard_map/ppermute | solution.py:231
  803.7 77.1 %copy-start.1 = (bf16[128,2048]{1,0:T(8,128)(2,1)S(1)}, bf16[128,2048]{1,0:T(8,128)(2,1)}, u32[]{:S(2)}) copy-start(bf16[128,2048]{1,0:T(8,128)(2,1)} %reduce-scatter.9.cloned.1.call-done) | copy-start | bytes 1572868
  803.7 77.1 %copy-start.11 = (bf16[128,2048]{1,0:T(8,128)(2,1)S(1)}, bf16[128,2048]{1,0:T(8,128)(2,1)}, u32[]{:S(2)}) copy-start(bf16[128,2048]{1,0:T(8,128)(2,1)} %param.13) | copy-start | bytes 1572868
  803.7 77.1 %copy-start.12 = (bf16[128,2048]{1,0:T(8,128)(2,1)S(1)}, bf16[128,2048]{1,0:T(8,128)(2,1)}, u32[]{:S(2)}) copy-start(bf16[128,2048]{1,0:T(8,128)(2,1)} %reduce-scatter.13.cloned.1.call-done) | copy-start | bytes 1572868
  (39 other events, 645.9 us)
Sparse Core Ops, SparseCore 0:
  35.5 39.4 all-gather.10
  77.2 57.5 all-gather.8
  137.2 23.4 all-gather.12
  165.5 67.5 reduce-scatter.8
  248.3 69.5 all-gather.16
  319.9 47.5 all-gather.14
  369.9 42.2 all-gather.18
  413.9 47.5 all-gather.20
  484.8 46.1 reduce-scatter.12
  535.4 47.8 all-gather.22
  586.3 68.5 reduce-scatter.20
  657.7 43.9 reduce-scatter.22
  704.7 39.5 reduce-scatter.16
  747.6 27.7 reduce-scatter.18
  777.6 53.0 reduce-scatter.14
  833.0 47.7 reduce-scatter.10

commit v2 on v1

v2 whole, which is shorter than its diff:
```python
import functools

import jax
import jax.numpy as jnp
from jax import lax
from jax.experimental import pallas as pl
from jax.experimental.pallas import tpu as pltpu
from jax.sharding import PartitionSpec as P

H = 16
KV = 8
HD = 128


epsilon = 1e-06
rope_base = 1000000.0
negative = -1e30
low = jnp.bfloat16
full = jnp.float32
MESH = pl.DeviceIdType.MESH
ANY = pl.BlockSpec(memory_space=pl.ANY)
IN_VMEM = pl.BlockSpec(memory_space=pltpu.VMEM)
DMA = pltpu.SemaphoreType.DMA
GAIN_COLUMNS = 3


def product(left_side, right_side):
    return jnp.dot(left_side, right_side, preferred_element_type=full)


def product_nt(left_side, right_side):
    return lax.dot_general(
        left_side, right_side, (((1,), (1,)), ((), ())), preferred_element_type=full
    )


def product_tn(left_side, right_side):
    return lax.dot_general(
        left_side, right_side, (((0,), (0,)), ((), ())), preferred_element_type=full
    )


def rms_scale(values, gain_vector):
    inverse = lax.rsqrt(jnp.mean(values * values, axis=-1, keepdims=True) + epsilon)
    return values * inverse * gain_vector


def rms_scale_back(values, gain_vector, grad):
    inverse = lax.rsqrt(jnp.mean(values * values, axis=-1, keepdims=True) + epsilon)
    scaled = grad * gain_vector
    return inverse * scaled - values * (
        inverse * inverse * inverse * jnp.mean(scaled * values, axis=-1, keepdims=True)
    )


def rope_tables(positions, head_width):
    half_width = head_width // 2
    inverse = rope_base ** (-jnp.arange(half_width, dtype=full) * 2.0 / head_width)
    angles = positions.astype(full)[:, None] * inverse[None, :]
    angles = jnp.concatenate([angles, angles], axis=-1)
    return (jnp.cos(angles)[:, None, :], jnp.sin(angles)[:, None, :])


def rotate(values, cosine_table, sine_table):
    half_width = values.shape[-1] // 2
    turned = jnp.concatenate([-values[..., half_width:], values[..., :half_width]], axis=-1)
    return values * cosine_table + turned * sine_table


def qk_piece(query_raw, key_raw, query_gain, key_gain, cosine_table, sine_table):
    queries = rms_scale(query_raw, query_gain)
    keys = rms_scale(key_raw, key_gain)
    return (rotate(queries, cosine_table, sine_table), rotate(keys, cosine_table, sine_table))


def gate_heads(attended, gate_raw):
    return attended * jax.nn.sigmoid(gate_raw)[:, :, None]


def swiglu(gate_pre, up_pre):
    return jax.nn.silu(gate_pre) * up_pre


def remote(source, target, send, receive, axis, peer):
    return pltpu.make_async_remote_copy(
        src_ref=source,
        dst_ref=target,
        send_sem=send,
        recv_sem=receive,
        device_id={axis: peer},
        device_id_type=MESH,
    )


def greet(peers):
    barrier = pltpu.get_barrier_semaphore()
    for axis, peer, exists in peers:
        if exists is True:
            pl.semaphore_signal(barrier, inc=1, device_id={axis: peer}, device_id_type=MESH)
        else:

            @pl.when(exists)
            def _():
                pl.semaphore_signal(barrier, inc=1, device_id={axis: peer}, device_id_type=MESH)

    arrivals = sum(1 for _, _, exists in peers if exists is True)
    for _, _, exists in peers:
        if exists is not True:
            arrivals = arrivals + exists.astype(jnp.int32)
    pl.semaphore_wait(barrier, arrivals)


def others(axis, count):
    me = lax.axis_index(axis)
    return [(axis, lax.rem(me + shift, count), True) for shift in range(1, count)]


class Line:
    def __init__(self, pieces):
        self.chips = pieces // 2
        self.me = lax.axis_index("ctx")
        self.chip, self.core = self.me // 2, lax.rem(self.me, 2)
        self.sibling = self.me + 1 - 2 * self.core
        self.right, self.left = self.me + 2, self.me - 2
        self.has_right, self.has_left = self.chip < self.chips - 1, self.chip > 0

    def peers(self):
        return [
            ("ctx", self.sibling, True),
            ("ctx", self.right, self.has_right),
            ("ctx", self.left, self.has_left),
        ]


def gather_scratch(pieces, parts):
    chips = pieces // 2
    return [DMA((chips, 2, parts))] * 2 + [DMA((chips, parts))] * 4


class Gather:
    def __init__(self, line, parts, rows, out_ref, sems):
        self.line, self.parts, self.rows, self.out_ref = line, parts, rows, out_ref
        self.size = rows // parts
        self.sib_send, self.sib_recv, self.r_send, self.r_recv, self.l_send, self.l_recv = sems

    def at(self, position, part):
        start = pl.multiple_of(position * self.rows + part * self.size, self.size)
        return self.out_ref.at[pl.ds(start, self.size)]

    def to_sibling(self, source, hop, side, part, position):
        return remote(
            source,
            self.at(position, part),
            self.sib_send.at[hop, side, part],
            self.sib_recv.at[hop, side, part],
            "ctx",
            self.line.sibling,
        )

    def to_right(self, source, hop, part, position):
        return remote(
            source,
            self.at(position, part),
            self.r_send.at[hop, part],
            self.r_recv.at[hop, part],
            "ctx",
            self.line.right,
        )

    def to_left(self, source, hop, part, position):
        return remote(
            source,
            self.at(position, part),
            self.l_send.at[hop, part],
            self.l_recv.at[hop, part],
            "ctx",
            self.line.left,
        )

    def start(self, x_ref):
        line = self.line
        for part in range(self.parts):
            piece = x_ref.at[pl.ds(part * self.size, self.size)]

            @pl.when(line.has_right)
            def _():
                self.to_right(piece, 0, part, line.me).start()

            @pl.when(line.has_left)
            def _():
                self.to_left(piece, 0, part, line.me).start()

            self.to_sibling(piece, 0, 0, part, line.me).start()

    def forward(self, hop):
        line = self.line
        for part in range(self.parts):
            from_left, from_right = line.me - 2 * hop, line.me + 2 * hop

            @pl.when(line.chip - hop >= 0)
            def _():
                piece = self.at(from_left, part)
                self.to_right(piece, hop - 1, part, from_left).wait_recv()

                @pl.when(line.has_right)
                def _():
                    self.to_right(piece, hop, part, from_left).start()

                self.to_sibling(piece, hop, 0, part, from_left).start()

            @pl.when(line.chip + hop < line.chips)
            def _():
                piece = self.at(from_right, part)
                self.to_left(piece, hop - 1, part, from_right).wait_recv()

                @pl.when(line.has_left)
                def _():
                    self.to_left(piece, hop, part, from_right).start()

                self.to_sibling(piece, hop, 1, part, from_right).start()

    def finish(self):
        line = self.line
        for hop in range(line.chips):
            for part in range(self.parts):
                for side in range(1 if hop == 0 else 2):
                    there = (line.chip - hop >= 0) if side == 0 else (line.chip + hop < line.chips)
                    position = (line.me - 2 * hop) if side == 0 else (line.me + 2 * hop)

                    @pl.when(there)
                    def _():
                        piece = self.at(position, part)
                        copy = self.to_sibling(piece, hop, side, part, position)
                        copy.wait_recv()
                        copy.wait_send()
                        if side == 0:

                            @pl.when(line.has_right)
                            def _():
                                self.to_right(piece, hop, part, position).wait_send()

                        if side == 1 or hop == 0:

                            @pl.when(line.has_left)
                            def _():
                                self.to_left(piece, hop, part, position).wait_send()


def gather_kernel(pieces, parts, x_ref, out_ref, own_sem, *sems):
    line = Line(pieces)
    greet(line.peers())
    rows = x_ref.shape[0]
    gather = Gather(line, parts, rows, out_ref, sems)
    gather.start(x_ref)
    start = pl.multiple_of(line.me * rows, rows)
    own = pltpu.make_async_copy(x_ref, out_ref.at[pl.ds(start, rows)], own_sem)
    own.start()
    for hop in range(1, line.chips):
        gather.forward(hop)
    own.wait()
    gather.finish()


def gather_ctx(x, number, parts=2):
    pieces = lax.axis_size("ctx")
    return pl.pallas_call(
        functools.partial(gather_kernel, pieces, parts),
        out_shape=jax.ShapeDtypeStruct((pieces * x.shape[0],) + x.shape[1:], x.dtype),
        in_specs=[IN_VMEM],
        out_specs=ANY,
        scratch_shapes=[DMA] + gather_scratch(pieces, parts),
        compiler_params=pltpu.CompilerParams(collective_id=number, has_side_effects=True),
        name=f"gather_rows_{number}",
    )(x)


def scatter_scratch(pieces, rows, width):
    chips = pieces // 2
    slots = pltpu.VMEM((chips, rows, width), low)
    return [slots, slots, pltpu.VMEM((2, chips, rows, width), low), slots, slots] + [
        DMA((2, chips))
    ] * 2 + [DMA((chips,))] * 4


class Scatter:
    def __init__(self, line, p_ref, rows, scratch):
        self.line, self.p_ref, self.rows = line, p_ref, rows
        (
            self.stage_r,
            self.stage_l,
            self.sib,
            self.in_r,
            self.in_l,
            self.sib_send,
            self.sib_recv,
            self.r_send,
            self.r_recv,
            self.l_send,
            self.l_recv,
        ) = scratch

    def block(self, chip, core):
        start = pl.multiple_of((chip * 2 + core) * self.rows, self.rows)
        return self.p_ref.at[pl.ds(start, self.rows)]

    def there(self, far, side):
        line = self.line
        return (line.chip + far < line.chips) if side == 0 else (line.chip - far >= 0)

    def target(self, far, side):
        return self.line.chip + far if side == 0 else self.line.chip - far

    def exchange(self, far, side):
        return remote(
            self.block(self.target(far, side), 1 - self.line.core),
            self.sib.at[side, far],
            self.sib_send.at[side, far],
            self.sib_recv.at[side, far],
            "ctx",
            self.line.sibling,
        )

    def send(self, far, side):
        if side == 0:
            return remote(
                self.stage_r.at[far],
                self.in_r.at[far - 1],
                self.r_send.at[far],
                self.r_recv.at[far - 1],
                "ctx",
                self.line.right,
            )
        return remote(
            self.stage_l.at[far],
            self.in_l.at[far - 1],
            self.l_send.at[far],
            self.l_recv.at[far - 1],
            "ctx",
            self.line.left,
        )

    def order(self):
        return [
            (far, side)
            for far in range(self.line.chips - 1, -1, -1)
            for side in range(2 if far else 1)
        ]

    def swap(self, far, side):
        @pl.when(self.there(far, side))
        def _():
            self.exchange(far, side).start()

    def push(self, far, side):
        line = self.line
        stage, arrived = (self.stage_r, self.in_r) if side == 0 else (self.stage_l, self.in_l)
        behind = line.has_left if side == 0 else line.has_right

        @pl.when(self.there(far, side))
        def _():
            self.exchange(far, side).wait_recv()
            own = self.block(self.target(far, side), line.core)
            if far == line.chips - 1:
                stage[far] = (own[...].astype(full) + self.sib[side, far].astype(full)).astype(low)
            else:

                @pl.when(behind)
                def _():
                    self.send(far + 1, side).wait_recv()
                    stage[far] = (
                        own[...].astype(full)
                        + self.sib[side, far].astype(full)
                        + arrived[far].astype(full)
                    ).astype(low)

                @pl.when(jnp.logical_not(behind))
                def _():
                    stage[far] = (
                        own[...].astype(full) + self.sib[side, far].astype(full)
                    ).astype(low)

            self.send(far, side).start()

    def total(self, total_ref):
        line = self.line
        self.exchange(0, 0).wait_recv()
        total_ref[...] = self.block(line.chip, line.core)[...].astype(full) + self.sib[
            0, 0
        ].astype(full)

        @pl.when(line.has_left)
        def _():
            self.send(1, 0).wait_recv()
            total_ref[...] += self.in_r[0].astype(full)

        @pl.when(line.has_right)
        def _():
            self.send(1, 1).wait_recv()
            total_ref[...] += self.in_l[0].astype(full)

    def finish(self):
        for far, side in self.order():

            @pl.when(self.there(far, side))
            def _():
                self.exchange(far, side).wait_send()
                if far > 0:
                    self.send(far, side).wait_send()


def scatter_kernel(pieces, p_ref, out_ref, *scratch):
    line = Line(pieces)
    greet(line.peers())
    scatter = Scatter(line, p_ref, out_ref.shape[0], scratch)
    for far, side in scatter.order():
        scatter.swap(far, side)
    for far, side in scatter.order():
        if far > 0:
            scatter.push(far, side)
    scatter.total(out_ref)
    scatter.finish()


def scatter_ctx(p, number):
    pieces = lax.axis_size("ctx")
    rows, width = p.shape[0] // pieces, p.shape[1]
    return pl.pallas_call(
        functools.partial(scatter_kernel, pieces),
        out_shape=jax.ShapeDtypeStruct((rows, width), full),
        in_specs=[IN_VMEM],
        out_specs=IN_VMEM,
        scratch_shapes=scatter_scratch(pieces, rows, width),
        compiler_params=pltpu.CompilerParams(
            collective_id=number, has_side_effects=True, vmem_limit_bytes=60 << 20
        ),
        name=f"scatter_rows_{number}",
    )(p.astype(low))


class Swap:
    def __init__(self, pieces, send_of, recv_of, send_sem, recv_sem):
        self.pieces, self.me = pieces, lax.axis_index("ctx")
        self.send_of, self.recv_of = send_of, recv_of
        self.send_sem, self.recv_sem = send_sem, recv_sem

    def copy(self, shift):
        peer = lax.rem(self.me + shift, self.pieces)
        return remote(
            self.send_of(peer),
            self.recv_of(self.me),
            self.send_sem.at[shift],
            self.recv_sem.at[shift],
            "ctx",
            peer,
        )

    def start(self):
        for shift in range(1, self.pieces):
            self.copy(shift).start()

    def wait_recv(self, shift):
        source = lax.rem(self.me + self.pieces - shift, self.pieces)
        remote(
            self.send_of(source),
            self.recv_of(source),
            self.send_sem.at[shift],
            self.recv_sem.at[shift],
            "ctx",
            source,
        ).wait_recv()
        return source

    def finish(self):
        for shift in range(1, self.pieces):
            self.copy(shift).wait_send()


def ff_columns_kernel(pieces, groups, block, gate_ref, up_ref, out_ref, send, own_sem, s_sem, r_sem):
    greet(others("ctx", pieces))
    me = lax.axis_index("ctx")
    own_width = groups * block
    for half, weight_ref in enumerate((gate_ref, up_ref)):
        for group in range(groups):
            for piece in range(pieces):
                start = (group * pieces + piece) * block
                send[piece, :, pl.ds(half * own_width + group * block, block)] = weight_ref[
                    :, pl.ds(start, block)
                ].astype(low)
    swap = Swap(pieces, lambda peer: send.at[peer], lambda peer: out_ref.at[peer], s_sem, r_sem)
    swap.start()
    own = pltpu.make_async_copy(send.at[me], out_ref.at[me], own_sem)
    own.start()
    for shift in range(1, pieces):
        swap.wait_recv(shift)
    own.wait()
    swap.finish()


def ff_columns(gate_weight, up_weight, block, number):
    pieces, groups = lax.axis_size("ctx"), lax.axis_size("seq")
    rows = gate_weight.shape[0]
    shape = (pieces, rows, 2 * groups * block)
    return pl.pallas_call(
        functools.partial(ff_columns_kernel, pieces, groups, block),
        out_shape=jax.ShapeDtypeStruct(shape, low),
        in_specs=[IN_VMEM, IN_VMEM],
        out_specs=ANY,
        scratch_shapes=[pltpu.VMEM(shape, low), DMA, DMA((pieces,)), DMA((pieces,))],
        compiler_params=pltpu.CompilerParams(
            collective_id=number, has_side_effects=True, vmem_limit_bytes=60 << 20
        ),
        name=f"ff_columns_{number}",
    )(gate_weight, up_weight)


def ff_rows_kernel(pieces, groups, block, x_ref, gate_ref, up_ref, recv, s_sem, r_sem):
    greet(others("ctx", pieces))
    me = lax.axis_index("ctx")
    swap = Swap(pieces, lambda peer: x_ref.at[peer], lambda peer: recv.at[peer], s_sem, r_sem)
    swap.start()
    recv[me] = x_ref[me]
    for shift in range(1, pieces):
        swap.wait_recv(shift)
    own_width = groups * block
    for half, grad_ref in enumerate((gate_ref, up_ref)):
        for group in range(groups):
            for piece in range(pieces):
                start = (group * pieces + piece) * block
                grad_ref[:, pl.ds(start, block)] = recv[
                    piece, :, pl.ds(half * own_width + group * block, block)
                ].astype(full)
    swap.finish()


def ff_rows(x, block, number):
    pieces, groups = lax.axis_size("ctx"), lax.axis_size("seq")
    rows = x.shape[1]
    grad = jax.ShapeDtypeStruct((rows, pieces * groups * block), full)
    return pl.pallas_call(
        functools.partial(ff_rows_kernel, pieces, groups, block),
        out_shape=(grad, grad),
        in_specs=[IN_VMEM],
        out_specs=(IN_VMEM, IN_VMEM),
        scratch_shapes=[pltpu.VMEM(x.shape, low), DMA((pieces,)), DMA((pieces,))],
        compiler_params=pltpu.CompilerParams(
            collective_id=number, has_side_effects=True, vmem_limit_bytes=60 << 20
        ),
        name=f"ff_rows_{number}",
    )(x)


def attn_rows_kernel(pieces, x_ref, out_ref, s_sem, r_sem):
    greet(others("ctx", pieces))
    me = lax.axis_index("ctx")
    swap = Swap(pieces, lambda peer: x_ref.at[peer], lambda peer: out_ref.at[peer], s_sem, r_sem)
    swap.start()
    out_ref[me] = x_ref[me]
    for shift in range(1, pieces):
        swap.wait_recv(shift)
    swap.finish()


def attn_rows(x, number):
    pieces = lax.axis_size("ctx")
    return pl.pallas_call(
        functools.partial(attn_rows_kernel, pieces),
        out_shape=jax.ShapeDtypeStruct(x.shape, low),
        in_specs=[IN_VMEM],
        out_specs=IN_VMEM,
        scratch_shapes=[DMA((pieces,)), DMA((pieces,))],
        compiler_params=pltpu.CompilerParams(
            collective_id=number, has_side_effects=True, vmem_limit_bytes=60 << 20
        ),
        name=f"attn_rows_{number}",
    )(x)


def opening_kernel(
    pieces,
    groups,
    parts,
    hidden_ref,
    gains_ref,
    attn_ref,
    normed_ref,
    attn_out,
    gains_out,
    gains_row,
    gains_all,
    gain_vector,
    normed,
    own_sem,
    own_attn,
    ga_send,
    ga_recv,
    gs_send,
    gs_recv,
    at_send,
    at_recv,
    as_send,
    as_recv,
    *sems,
):
    line = Line(pieces)
    me, group = line.me, lax.axis_index("seq")
    greet(others("ctx", pieces) + others("seq", groups))
    rows, model = hidden_ref.shape
    gain_count = gains_ref.shape[1]
    gains_row[...] = jnp.zeros(gains_row.shape, full)
    gains_row[0:1, pl.ds(0, gain_count)] = gains_ref[...].astype(low).astype(full)
    gains_all[group, me] = gains_row[...]
    gain_swap = Swap(
        pieces, lambda peer: gains_row, lambda peer: gains_all.at[group, peer], ga_send, ga_recv
    )
    gain_swap.start()
    attn_swap = Swap(
        pieces, lambda peer: attn_ref.at[peer], lambda peer: attn_out.at[group, peer], at_send, at_recv
    )
    attn_swap.start()
    attn_own = pltpu.make_async_copy(attn_ref.at[me], attn_out.at[group, me], own_attn)
    attn_own.start()
    values = hidden_ref[...].astype(full)
    inverse = lax.rsqrt(jnp.mean(values * values, axis=-1, keepdims=True) + epsilon)

    def to_groups(ref, sends, receives, shift):
        peer = lax.rem(group + shift, groups)
        return remote(ref.at[group], ref.at[group], sends.at[shift], receives.at[shift], "seq", peer)

    def from_groups(ref, sends, receives, shift):
        peer = lax.rem(group + groups - shift, groups)
        remote(
            ref.at[peer], ref.at[peer], sends.at[shift], receives.at[shift], "seq", peer
        ).wait_recv()

    for shift in range(1, pieces):
        gain_swap.wait_recv(shift)
    for shift in range(1, groups):
        to_groups(gains_all, gs_send, gs_recv, shift).start()
    for shift in range(1, groups):
        from_groups(gains_all, gs_send, gs_recv, shift)
    for index in range(groups * pieces):
        gain_vector[0:1, pl.ds(index * gain_count, gain_count)] = gains_all[
            index // pieces, index % pieces, 0:1, pl.ds(0, gain_count)
        ]
    gains_out[...] = gain_vector[...]
    normed[...] = (values * inverse * gain_vector[0:1, pl.ds(0, model)]).astype(low)
    gather = Gather(line, parts, rows, normed_ref, sems)
    gather.start(normed)
    start = pl.multiple_of(me * rows, rows)
    own = pltpu.make_async_copy(normed, normed_ref.at[pl.ds(start, rows)], own_sem)
    own.start()
    for shift in range(1, pieces):
        attn_swap.wait_recv(shift)
    attn_own.wait()
    for shift in range(1, groups):
        to_groups(attn_out, as_send, as_recv, shift).start()
    for hop in range(1, line.chips):
        gather.forward(hop)
    own.wait()
    gather.finish()
    for shift in range(1, groups):
        from_groups(attn_out, as_send, as_recv, shift)
    gain_swap.finish()
    attn_swap.finish()
    for shift in range(1, groups):
        to_groups(gains_all, gs_send, gs_recv, shift).wait_send()
        to_groups(attn_out, as_send, as_recv, shift).wait_send()


def opening(hidden_in, norm_gains, attn_blocks, number, parts=2):
    pieces, groups = lax.axis_size("ctx"), lax.axis_size("seq")
    rows, model = hidden_in.shape
    gains = norm_gains.shape[0]
    lanes = -(-gains // 128) * 128
    return pl.pallas_call(
        functools.partial(opening_kernel, pieces, groups, parts),
        out_shape=(
            jax.ShapeDtypeStruct((pieces * rows, model), low),
            jax.ShapeDtypeStruct((groups,) + attn_blocks.shape, low),
            jax.ShapeDtypeStruct((1, groups * pieces * gains), full),
        ),
        in_specs=[IN_VMEM, IN_VMEM, IN_VMEM],
        out_specs=(ANY, ANY, IN_VMEM),
        scratch_shapes=[
            pltpu.VMEM((8, lanes), full),
            pltpu.VMEM((groups, pieces, 8, lanes), full),
            pltpu.VMEM((1, groups * pieces * gains), full),
            pltpu.VMEM((rows, model), low),
            DMA,
            DMA,
            DMA((pieces,)),
            DMA((pieces,)),
            DMA((groups,)),
            DMA((groups,)),
            DMA((pieces,)),
            DMA((pieces,)),
            DMA((groups,)),
            DMA((groups,)),
        ]
        + gather_scratch(pieces, parts),
        compiler_params=pltpu.CompilerParams(
            collective_id=number, has_side_effects=True, vmem_limit_bytes=60 << 20
        ),
        name=f"opening_{number}",
    )(hidden_in, norm_gains.reshape(1, gains), attn_blocks)


def gather_seq(block):
    return lax.all_gather(block, "seq", axis=0, tiled=True)


def scatter_seq(block):
    return lax.psum_scatter(block.astype(low), "seq", scatter_dimension=0, tiled=True)


def on_device(
    hidden_in,
    out_grad,
    prefix_len,
    norm_gains,
    query_weight,
    key_weight,
    value_weight,
    head_gate_weight,
    out_weight,
    gate_weight,
    up_weight,
    down_weight,
):
    row_count, model = hidden_in.shape
    groups = lax.axis_size("seq")
    pieces = lax.axis_size("ctx")
    length = row_count * pieces
    weight_rows = query_weight.shape[0]
    heads = H // pieces
    kv_heads = max(1, KV // pieces)
    copies = max(1, pieces // KV)
    per_kv = heads // kv_heads
    ff_block = down_weight.shape[0]
    ff_own = ff_block * groups
    prefix = prefix_len[0]
    q_width, kv_width = heads * HD, kv_heads * HD
    gain_count = norm_gains.shape[0]
    gain_columns = -(-gain_count // weight_rows)
    used = q_width + 2 * kv_width + heads
    attn_width = -(-(used + gain_columns) // 128) * 128

    def kv_columns(weight):
        columns = weight.astype(low).reshape(weight_rows, KV, HD)
        return jnp.repeat(columns, copies, axis=1).reshape(weight_rows, pieces, kv_width)

    attn_blocks = jnp.concatenate(
        [
            query_weight.astype(low).reshape(weight_rows, pieces, q_width),
            kv_columns(key_weight),
            kv_columns(value_weight),
            head_gate_weight.astype(low).reshape(weight_rows, pieces, heads),
            jnp.zeros((weight_rows, pieces, attn_width - used), low),
        ],
        axis=-1,
    ).transpose(1, 0, 2)
    normed, attn_low, gains_full = opening(hidden_in, norm_gains, attn_blocks, 0)
    attn_low = attn_low.reshape(model, attn_width)
    gains_full = gains_full.reshape(-1)
    ff_low = gather_seq(
        ff_columns(gate_weight, up_weight, ff_block, 1).reshape(pieces * weight_rows, 2 * ff_own)
    )
    down_low = gather_seq(down_weight.astype(low))
    spread = [(i, (i % groups) * pieces + i // groups) for i in range(groups * pieces)]
    collect = [(target, source) for source, target in spread]
    out_low = gather_seq(lax.ppermute(out_weight.astype(low), ("seq", "ctx"), spread))
    attention_gain = gains_full[:model]
    swiglu_gain = gains_full[model : 2 * model]
    query_gain = gains_full[2 * model : 2 * model + HD]
    key_gain = gains_full[2 * model + HD :]

    residual_in = hidden_in.astype(full)
    out_grad_all = gather_ctx(out_grad, 2)
    raw = product(normed, attn_low)
    query_raw = raw[:, :q_width].reshape(length, heads, HD)
    key_raw = raw[:, q_width : q_width + kv_width].reshape(length, kv_heads, HD)
    values = raw[:, q_width + kv_width : q_width + 2 * kv_width].astype(low)
    values = values.reshape(length, kv_heads, HD)
    gate_raw = raw[:, q_width + 2 * kv_width : used]
    positions = jnp.arange(length, dtype=jnp.int32)
    cosine_table, sine_table = rope_tables(positions, HD)
    (queries_full, keys_full), pull_rope = jax.vjp(
        functools.partial(qk_piece, cosine_table=cosine_table, sine_table=sine_table),
        query_raw,
        key_raw,
        query_gain,
        key_gain,
    )
    queries = queries_full.astype(low).reshape(length, kv_heads, per_kv, HD)
    keys = keys_full.astype(low)
    limits = jnp.maximum(positions, prefix - 1)
    allowed = positions[None, :] <= limits[:, None]
    score_scale = HD ** (-0.5)
    scores = (
        jnp.einsum("tkgd,skd->kgts", queries, keys, preferred_element_type=full) * score_scale
    )
    scores = jnp.where(allowed, scores, negative)
    row_max = jnp.max(scores, axis=-1, keepdims=True)
    expanded = jnp.exp(scores - row_max)
    row_sum = jnp.sum(expanded, axis=-1, keepdims=True)
    log_norm = row_max + jnp.log(row_sum)
    attended = (
        jnp.einsum("kgts,skd->kgtd", expanded.astype(low), values, preferred_element_type=full)
        / row_sum
    )
    attended_rows = attended.transpose(2, 0, 1, 3).reshape(length, heads, HD)
    gated_full, pull_gate = jax.vjp(gate_heads, attended_rows, gate_raw)
    gated = gated_full.astype(low).reshape(length, q_width)
    middle = residual_in + scatter_ctx(product(gated, out_low), 3)

    normed_two = gather_ctx(rms_scale(middle, swiglu_gain).astype(low), 4)
    pre = product(normed_two, ff_low)
    gate_pre, up_pre = pre[:, :ff_own], pre[:, ff_own:]
    hidden_ff_full, pull_swiglu = jax.vjp(swiglu, gate_pre, up_pre)
    hidden_ff = hidden_ff_full.astype(low)

    grad_hidden_ff = product_nt(out_grad_all, down_low)
    grad_gate_full, grad_up_full = pull_swiglu(grad_hidden_ff)
    grad_pre = jnp.concatenate([grad_gate_full.astype(low), grad_up_full.astype(low)], axis=-1)
    grad_normed_two = scatter_ctx(product_nt(grad_pre, ff_low), 5)
    ff_term = product_tn(normed_two, grad_pre)
    swiglu_gain_grad = jnp.sum(ff_term * ff_low.astype(full), axis=-1) / swiglu_gain
    ff_share = scatter_seq(ff_term).reshape(pieces, weight_rows, 2 * ff_own)
    down_share = scatter_seq(product_tn(hidden_ff, out_grad_all)).astype(full)

    grad_middle = out_grad.astype(full) + rms_scale_back(middle, swiglu_gain, grad_normed_two)
    grad_branch = gather_ctx(grad_middle.astype(low), 6)
    hidden_out = (middle + scatter_ctx(product(hidden_ff, down_low), 7)).astype(low)
    gate_share, up_share = ff_rows(ff_share, ff_block, 8)
    grad_gated = product_nt(grad_branch, out_low).reshape(length, heads, HD)
    output_share = lax.ppermute(
        scatter_seq(product_tn(gated, grad_branch)), ("seq", "ctx"), collect
    ).astype(full)
    grad_attended_full, grad_gate_raw_full = pull_gate(grad_gated)
    grad_attended = grad_attended_full.astype(low)
    grad_heads = grad_attended.reshape(length, kv_heads, per_kv, HD).transpose(1, 2, 0, 3)
    row_delta = jnp.sum(grad_heads.astype(full) * attended, axis=-1, keepdims=True)
    probabilities = jnp.exp(scores - log_norm)
    prob_grad = jnp.einsum("kgtd,skd->kgts", grad_heads, values, preferred_element_type=full)
    score_grad = (probabilities * (prob_grad - row_delta)).astype(low)
    grad_queries = (
        jnp.einsum("kgts,skd->tkgd", score_grad, keys, preferred_element_type=full) * score_scale
    )
    grad_keys = (
        jnp.einsum("kgts,tkgd->skd", score_grad, queries, preferred_element_type=full)
        * score_scale
    )
    grad_values = jnp.einsum(
        "kgts,kgtd->skd", probabilities.astype(low), grad_heads, preferred_element_type=full
    )
    grad_query_full, grad_key_full, query_gain_grad, key_gain_grad = pull_rope(
        (grad_queries.reshape(length, heads, HD), grad_keys)
    )
    grad_raw = jnp.concatenate(
        [
            grad_query_full.reshape(length, q_width).astype(low),
            grad_key_full.reshape(length, kv_width).astype(low),
            grad_values.reshape(length, kv_width).astype(low),
            grad_gate_raw_full.astype(low),
            jnp.zeros((length, attn_width - used), low),
        ],
        axis=-1,
    )
    attn_term = product_tn(normed, grad_raw)
    attention_gain_grad = jnp.sum(attn_term * attn_low.astype(full), axis=-1) / attention_gain
    gains_term = jnp.concatenate(
        [attention_gain_grad, swiglu_gain_grad, query_gain_grad, key_gain_grad]
    ).reshape(groups * pieces, gain_count)
    gains_term = jnp.pad(gains_term, ((0, 0), (0, gain_columns * weight_rows - gain_count)))
    gains_term = gains_term.reshape(model, gain_columns)
    attn_term = jnp.concatenate(
        [
            attn_term[:, :used].astype(low),
            gains_term.astype(low),
            jnp.zeros((model, attn_width - used - gain_columns), low),
        ],
        axis=-1,
    )
    attn_share = scatter_seq(attn_term).reshape(pieces, weight_rows, attn_width)
    grad_normed = scatter_ctx(product_nt(grad_raw, attn_low), 9)
    hidden_grad = (grad_middle + rms_scale_back(residual_in, attention_gain, grad_normed)).astype(
        low
    )
    attn_share = attn_rows(attn_share, 10).transpose(1, 0, 2).astype(full)

    def kv_back(columns):
        columns = columns.reshape(weight_rows, KV, copies, HD)
        return columns.sum(axis=2).reshape(weight_rows, KV * HD)

    query_share = attn_share[:, :, :q_width].reshape(weight_rows, H * HD)
    key_share = kv_back(attn_share[:, :, q_width : q_width + kv_width])
    value_share = kv_back(attn_share[:, :, q_width + kv_width : q_width + 2 * kv_width])
    head_share = attn_share[:, :, q_width + 2 * kv_width : used].reshape(weight_rows, H)
    gains_share = attn_share[:, :, used : used + gain_columns].sum(axis=1).reshape(-1)[:gain_count]
    return (
        hidden_out,
        hidden_grad,
        gains_share,
        query_share,
        key_share,
        value_share,
        head_share,
        output_share,
        gate_share,
        up_share,
        down_share,
    )


def solution(mesh):
    rows = P(("seq", "ctx"), None)
    return jax.shard_map(
        on_device,
        mesh=mesh,
        in_specs=(rows, rows, P("seq"), P(("seq", "ctx"))) + (rows,) * 8,
        out_specs=(rows, rows, P(("seq", "ctx"))) + (rows,) * 8,
        check_vma=False,
    )
```

time: 898 us -> 720 us (0.80)
  Pallas kernels: 0 us -> 453 us
  waiting for transfers between devices: 461 us -> 46 us
  blocking collectives: 161 us -> 0 us
  local copies, waits for them, and re-layouts: 65.2 us -> 38 us
  other arithmetic: 55.8 us -> 39.4 us
  starting transfers between devices: 22.1 us -> 6.75 us
    pallas_call x0 -> x11, Pallas kernels: none -> 453 us  [the longest x4 173 us: scatter_ctx(): pl.pallas_call(functools.partial(scatter_kernel, pieces), out_shape=jax.S...]
    all_gather x4 -> x0, waiting for transfers between devices: 154 us -> none  [gather_ctx(): return lax.all_gather(block, 'ctx', axis=0, tiled=True)]
    all_gather x4 -> x3, waiting for transfers between devices: 100 us -> 0.04 us  [gather_seq(): return lax.all_gather(block, 'seq', axis=0, tiled=True)]
    reduce_scatter x4, waiting for transfers between devices: 107 us -> 20.3 us  [scatter_seq(): lax.psum_scatter(block.astype(low), 'seq', scatter_dimension=0, tiled=True)]
    all_to_all x2 -> x0, blocking collectives: 81.8 us -> none  [to_columns(): lax.all_to_all(block, 'ctx', split_axis=1, concat_axis=0, tiled=True)]
    unnamed x2 -> x0, blocking collectives: 79.4 us -> none
    reduce_scatter x4 -> x0, waiting for transfers between devices: 77.1 us -> none  [scatter_ctx(): lax.psum_scatter(block.astype(low), 'ctx', scatter_dimension=0, tiled=True)]
    reshape x13 -> x5, local copies, waits for them, and re-layouts: 34.8 us -> 8.47 us  [the longest x1 4.97 us: on_device(): attn_low = attn_low.reshape(model, attn_width)]
  transfers between devices with their start and end apart: 20 -> 9, of which waited for: 15 -> 3; matrix products, arithmetic and copies ran while one was open for 21% -> 15% of each run, Pallas kernels for 0% -> 47%
where the time goes in v2:
time: 720 us; the launch traced here: 707 us
  Pallas kernels  453 us (63%)
  matrix products  108 us (15%)
  waiting for transfers between devices  46 us (6%)
  other arithmetic  39.4 us (5%)
  local copies, waits for them, and re-layouts  38 us (5%)
  between operations  16.1 us (2%)
    pallas_call x4, Pallas kernels, scatter_ctx(): pl.pallas_call(functools.partial(scatter_kernel, pieces), out_shape=jax.S...  173 us
    pallas_call x3, Pallas kernels, gather_ctx(): pl.pallas_call(functools.partial(gather_kernel, pieces, parts), out_shape...  124 us
    pallas_call x1, Pallas kernels, opening(): pl.pallas_call(functools.partial(opening_kernel, pieces, groups, parts),...  67.6 us
    pallas_call x1, Pallas kernels, ff_columns(): pl.pallas_call(functools.partial(ff_columns_kernel, pieces, groups, block...  38 us
    pallas_call x1, Pallas kernels, ff_rows(): pl.pallas_call(functools.partial(ff_rows_kernel, pieces, groups, block),...  33.8 us
    dot_general x4, matrix products, product_tn(): lax.dot_general(left_side, right_side, (((0,), (0,)), ((), ())), preferre...  31.1 us
    dot_general x4, matrix products, product_nt(): lax.dot_general(left_side, right_side, (((1,), (1,)), ((), ())), preferre...  29.6 us
    dot_general x4, matrix products, product(): return jnp.dot(left_side, right_side, preferred_element_type=full)  29 us
  transfers between devices with their start and end apart: 9, of which 3 were waited for; matrix products, arithmetic and copies ran while one was open for 15% of the time, Pallas kernels for 47%

profile of v2, /device:TPU:1, one launch (start us, length us, event | category | flops | bytes accessed | tf_op | source)
XLA Modules:
  0.0 707.1 jit_solution(4763662882183179458)
XLA Ops:
  12.8 13.5 %collective-permute-done = bf16[64,2048]{1,0:T(8,128)(2,1)S(1)} collective-permute-done((bf16[64,2048]{1,0:T(8,128)(2,1)S(1)}, bf16[64,2048]{1,0:T(8,128)(2,1)S(1)}, u32[]{:S(2)}, u32[]{:S(2)}) %collective-permute-start) | collective-permute-done | bytes 262176 | tf_op jit(solution)/shard_map/ppermute | solution.py:771
  27.1 38.0 %ff_columns_1.1 = bf16[8,64,1536]{2,1,0:T(8,128)(2,1)} custom-call(f32[64,6144]{1,0:T(8,128)} %gate_ref.1, f32[64,6144]{1,0:T(8,128)} %up_ref.1), custom_call_target="tpu_custom_call" | custom-call | tf_op jit(solution)/shard_map/ff_columns_1/pallas_call | solution.py:503
  70.4 67.6 %opening_0.1 = (bf16[1024,2048]{1,0:T(8,128)(2,1)}, bf16[4,8,64,640]{3,2,1,0:T(8,128)(2,1)}, f32[1,4352]{1,0:T(1,128)}) custom-call(bf16[128,2048]{1,0:T(8,128)(2,1)} %hidden_ref.1, f32[1,136]{1,0:T(1,128)} %bitcast.268, bf16[8,64,640]{2,1,0:T(8,128)(2,1)} %bitcast.247), custom_call_target="tpu_custom_call" | custom-call | tf_op jit(solution)/shard_map/opening_0/pallas_call | solution.py:675
  138.0 5.7 fusion.92
  154.7 39.9 %gather_rows_2.1 = bf16[1024,2048]{1,0:T(8,128)(2,1)} custom-call(bf16[128,2048]{1,0:T(8,128)(2,1)} %x_ref.1), custom_call_target="tpu_custom_call" | custom-call | tf_op jit(solution)/shard_map/gather_rows_2/pallas_call | solution.py:266
  216.9 42.1 %scatter_rows_3.1 = f32[128,2048]{1,0:T(8,128)} custom-call(bf16[1024,2048]{1,0:T(8,128)(2,1)} %convolution_convert_fusion.2.p_ref), custom_call_target="tpu_custom_call" | custom-call | tf_op jit(solution)/shard_map/scatter_rows_3/pallas_call | solution.py:427
  262.6 41.9 %gather_rows_4.1 = bf16[1024,2048]{1,0:T(8,128)(2,1)} custom-call(bf16[128,2048]{1,0:T(8,128)(2,1)} %multiply_convert_fusion.3.x_ref), custom_call_target="tpu_custom_call" | custom-call | tf_op jit(solution)/shard_map/gather_rows_4/pallas_call | solution.py:266
  304.6 11.8 %fusion.93 = f32[1024,1536]{1,0:T(8,128)} fusion(bf16[1024,2048]{1,0:T(8,128)(2,1)} %gather_rows_4.1, bf16[2048,1536]{0,1:T(8,128)(2,1)} %all-gather.6.cloned.1.call-done), kind=kOutput, calls=%fused_computation.174 | convolution fusion | flops 6442450944 | bytes 16777216 | tf_op jit(solution)/shard_map/dot_general | solution.py:28
  316.4 10.6 %fusion.16 = (bf16[1024,768]{1,0:T(8,128)(2,1)S(1)}, bf16[1024,768]{1,0:T(8,128)(2,1)S(1)}, bf16[1024,768]{1,0:T(8,128)(2,1)}) fusion(f32[1024,1536]{1,0:T(8,128)} %fusion.93, bf16[1024,2048]{1,0:T(8,128)(2,1)} %gather_rows_2.1, bf16[768,2048]{1,0:T(8,128)(2,1)} %all-gather.8.cloned.1.call-done), kind=kOutput, calls=%fused_computation.28 | convolution fusion | flops 3233808384 | bytes 18350080 | tf_op jit(solution)/shard_map/dot_general | solution.py:32
  328.7 8.2 %convolution_convert_fusion.p_ref = bf16[1024,2048]{1,0:T(8,128)(2,1)} fusion(bf16[2048,1536]{0,1:T(8,128)(2,1)S(1)} %copy-done.30, bf16[1024,768]{1,0:T(8,128)(2,1)S(1)} %get-tuple-element.34, bf16[1024,768]{1,0:T(8,128)(2,1)S(1)} %get-tuple-element.33), kind=kOutput, calls=%fused_computation.21 | convolution fusion | flops 6450839552 | bytes 13631488 | tf_op jit(solution)/shard_map/dot_general | solution.py:32
  336.9 42.2 %scatter_rows_5.1 = f32[128,2048]{1,0:T(8,128)} custom-call(bf16[1024,2048]{1,0:T(8,128)(2,1)} %convolution_convert_fusion.p_ref), custom_call_target="tpu_custom_call" | custom-call | tf_op jit(solution)/shard_map/scatter_rows_5/pallas_call | solution.py:427
  383.0 42.0 %gather_rows_6.1 = bf16[1024,2048]{1,0:T(8,128)(2,1)} custom-call(bf16[128,2048]{1,0:T(8,128)(2,1)} %fusion.85.x_ref), custom_call_target="tpu_custom_call" | custom-call | tf_op jit(solution)/shard_map/gather_rows_6/pallas_call | solution.py:266
  433.9 6.8 fusion.28
  457.0 5.7 multiply_reduce_fusion.1
  464.3 12.9 %fusion.87 = (bf16[2048,1536]{0,1:T(8,128)(2,1)}, f32[2048]{0:T(1024)S(1)}) fusion(bf16[2048,1536]{0,1:T(8,128)(2,1)} %all-gather.6.cloned.1.call-done, bf16[1024,2048]{1,0:T(8,128)(2,1)} %gather_rows_4.1, bf16[1024,768]{1,0:T(8,128)(2,1)} %copy-done.33, bf16[1024,768]{1,0:T(8,128)(2,1)} %copy-done.32), kind=kOutput, calls=%fused_computation.168 | convolution fusion | flops 6461323264 | bytes 19931136 | tf_op jit(solution)/shard_map/dot_general | solution.py:38
  482.4 7.8 %convolution_convert_fusion.4 = bf16[768,2048]{1,0:T(8,128)(2,1)} fusion(bf16[1024,768]{1,0:T(8,128)(2,1)} %get-tuple-element.35, bf16[1024,2048]{1,0:T(8,128)(2,1)} %gather_rows_2.1), kind=kOutput, calls=%fused_computation.25 | convolution fusion | flops 3222798336 | bytes 8912896 | tf_op jit(solution)/shard_map/dot_general | solution.py:38
  491.0 6.9 convolution_convert_fusion.1.p_ref
  497.9 41.9 %scatter_rows_9.1 = f32[128,2048]{1,0:T(8,128)} custom-call(bf16[1024,2048]{1,0:T(8,128)(2,1)} %convolution_convert_fusion.1.p_ref), custom_call_target="tpu_custom_call" | custom-call | tf_op jit(solution)/shard_map/scatter_rows_9/pallas_call | solution.py:427
  539.8 6.9 convolution_convert_fusion.3.p_ref
  546.7 47.2 %scatter_rows_7.1 = f32[128,2048]{1,0:T(8,128)} custom-call(bf16[1024,2048]{1,0:T(8,128)(2,1)} %convolution_convert_fusion.3.p_ref), custom_call_target="tpu_custom_call" | custom-call | tf_op jit(solution)/shard_map/scatter_rows_7/pallas_call | solution.py:427
  600.8 11.3 %collective-permute-done.1 = bf16[64,2048]{1,0:T(8,128)(2,1)S(1)} collective-permute-done((bf16[64,2048]{1,0:T(8,128)(2,1)}, bf16[64,2048]{1,0:T(8,128)(2,1)S(1)}, u32[]{:S(2)}, u32[]{:S(2)}) %collective-permute-start.1) | collective-permute-done | bytes 262176 | tf_op jit(solution)/shard_map/ppermute | solution.py:836
  615.1 16.5 %attn_rows_10.1 = bf16[8,64,640]{2,1,0:T(8,128)(2,1)} custom-call(bf16[8,64,640]{2,1,0:T(8,128)(2,1)} %bitcast.248), custom_call_target="tpu_custom_call" | custom-call | tf_op jit(solution)/shard_map/attn_rows_10/pallas_call | solution.py:565
  639.2 20.3 %reduce-scatter.9.cloned.1.call-done = bf16[512,1536]{0,1:T(8,128)(2,1)} async-done(((bf16[2048,1536]{0,1:T(8,128)(2,1)}), bf16[512,1536]{0,1:T(8,128)(2,1)}) %reduce-scatter.9.cloned.1.call-update) | async-done | bytes 1572880 | tf_op jit(solution)/shard_map/reduce_scatter | solution.py:713
  662.1 33.8 %ff_rows_8.1 = (f32[64,6144]{1,0:T(8,128)}, f32[64,6144]{1,0:T(8,128)}) custom-call(bf16[8,64,1536]{2,1,0:T(8,128)(2,1)} %bitcast.241), custom_call_target="tpu_custom_call" | custom-call | tf_op jit(solution)/shard_map/ff_rows_8/pallas_call | solution.py:539
  (185 shorter events, 109.5 us)
Async XLA Ops:
  7.2 204.6 %all-gather.4.cloned.1.call-start = ((), (), s32[]{:S(2)}) async-start(), calls=%async_computation.4 | async-start | bytes 1310720 | tf_op jit(solution)/shard_map/all_gather | solution.py:709
  8.3 18.1 %collective-permute-start = (bf16[64,2048]{1,0:T(8,128)(2,1)S(1)}, bf16[64,2048]{1,0:T(8,128)(2,1)S(1)}, u32[]{:S(2)}, u32[]{:S(2)}) collective-permute-start(bf16[64,2048]{1,0:T(8,128)(2,1)S(1)} %convert_element_type.184), channel_id=1, source_target_pairs={{0,0},{1,8},{2,16},{3,24},{4,1},{5,9},{6,17},{7,25},{8,2},{9,10},{... | collective-permute-start | bytes 786440 | tf_op jit(solution)/shard_map/ppermute | solution.py:771
  27.1 40.9 %copy-start.20 = (f32[192,2048]{1,0:T(8,128)S(1)}, f32[192,2048]{1,0:T(8,128)}, u32[]{:S(2)}) copy-start(f32[192,2048]{1,0:T(8,128)} %param.23) | copy-start | bytes 4718596
  27.1 277.5 %all-gather.6.cloned.1.call-start = ((), (), s32[]{:S(2)}) async-start(), calls=%async_computation.5 | async-start | bytes 7864320 | tf_op jit(solution)/shard_map/all_gather | solution.py:709
  67.9 248.5 %all-gather.8.cloned.1.call-start = ((), (), s32[]{:S(2)}) async-start(), calls=%async_computation.6 | async-start | bytes 3932160 | tf_op jit(solution)/shard_map/all_gather | solution.py:709
  69.0 526.4 %reduce-scatter.7.cloned.1.call-start = ((), (), s32[]{:S(2)}) async-start(), calls=%async_computation.8 | async-start | bytes 1310720 | tf_op jit(solution)/shard_map/reduce_scatter | solution.py:713
  143.8 62.9 %copy-start.2 = (f32[1024,640]{0,1:T(8,128)}, f32[1024,640]{0,1:T(8,128)S(1)}, u32[]{:S(2)}) copy-start(f32[1024,640]{0,1:T(8,128)S(1)} %fusion.92) | copy-start | bytes 7864324
  143.8 5.2 copy-start.28
  194.7 8.0 %copy-start.15 = (pred[1024,1024]{0,1:T(8,128)(4,1)S(1)}, pred[1024,1024]{0,1:T(8,128)(4,1)}, u32[]{:S(2)}) copy-start(pred[1024,1024]{0,1:T(8,128)(4,1)} %iota_compare_fusion) | copy-start | bytes 3145732
  198.4 6.2 copy-start.22
  216.9 42.1 %copy-start.1 = (bf16[128,2048]{1,0:T(8,128)(2,1)S(1)}, bf16[128,2048]{1,0:T(8,128)(2,1)}, u32[]{:S(2)}) copy-start(bf16[128,2048]{1,0:T(8,128)(2,1)} %hidden_ref.1) | copy-start | bytes 1572868
  316.4 12.3 %copy-start.30 = (bf16[2048,1536]{0,1:T(8,128)(2,1)S(1)}, bf16[2048,1536]{0,1:T(8,128)(2,1)}, u32[]{:S(2)}) copy-start(bf16[2048,1536]{0,1:T(8,128)(2,1)} %all-gather.6.cloned.1.call-done) | copy-start | bytes 18874372
  336.9 42.2 %copy-start = (f32[128,2048]{1,0:T(8,128)S(1)}, f32[128,2048]{1,0:T(8,128)}, u32[]{:S(2)}) copy-start(f32[128,2048]{1,0:T(8,128)} %scatter_rows_3.1) | copy-start | bytes 3145732
  336.9 43.8 %copy-start.12 = (bf16[128,2048]{1,0:T(8,128)(2,1)S(1)}, bf16[128,2048]{1,0:T(8,128)(2,1)}, u32[]{:S(2)}) copy-start(bf16[128,2048]{1,0:T(8,128)(2,1)} %x_ref.1) | copy-start | bytes 1572868
  429.7 11.0 %slice-start = ((s8[8388608]{0:T(1024)(128)(4,1)}), s8[4194304]{0:T(1024)(128)(4,1)S(1)}, s32[]{:S(2)}) async-start(s8[8388608]{0:T(1024)(128)(4,1)} %bitcast.239), calls=%async_computation.11 | async-start | bytes 8388608
  433.9 6.8 copy-start.3
  433.9 6.8 slice-start.1
  464.3 148.7 %reduce-scatter.5.cloned.1.call-start = ((), (), s32[]{:S(2)}) async-start(), calls=%async_computation.7 | async-start | bytes 3276800 | tf_op jit(solution)/shard_map/reduce_scatter | solution.py:713
  482.4 154.4 %reduce-scatter.11.cloned.1.call-start = ((), (), s32[]{:S(2)}) async-start(), calls=%async_computation.10 | async-start | bytes 3932160 | tf_op jit(solution)/shard_map/reduce_scatter | solution.py:713
  490.3 169.2 %reduce-scatter.9.cloned.1.call-start = ((), (), s32[]{:S(2)}) async-start(), calls=%async_computation.9 | async-start | bytes 7864320 | tf_op jit(solution)/shard_map/reduce_scatter | solution.py:713
  497.9 41.9 %copy-start.31 = (bf16[1024,768]{1,0:T(8,128)(2,1)S(1)}, bf16[1024,768]{1,0:T(8,128)(2,1)}, u32[]{:S(2)}) copy-start(bf16[1024,768]{1,0:T(8,128)(2,1)} %get-tuple-element.35) | copy-start | bytes 4718596
  546.7 50.6 %copy-start.4 = (f32[128,2048]{1,0:T(8,128)S(1)}, f32[128,2048]{1,0:T(8,128)}, u32[]{:S(2)}) copy-start(f32[128,2048]{1,0:T(8,128)} %scatter_rows_5.1) | copy-start | bytes 3145732
  546.7 50.6 %copy-start.13 = (bf16[128,2048]{1,0:T(8,128)(2,1)S(1)}, bf16[128,2048]{1,0:T(8,128)(2,1)}, u32[]{:S(2)}) copy-start(bf16[128,2048]{1,0:T(8,128)(2,1)} %x_ref.1) | copy-start | bytes 1572868
  595.4 16.7 %collective-permute-start.1 = (bf16[64,2048]{1,0:T(8,128)(2,1)}, bf16[64,2048]{1,0:T(8,128)(2,1)S(1)}, u32[]{:S(2)}, u32[]{:S(2)}) collective-permute-start(bf16[64,2048]{1,0:T(8,128)(2,1)} %reduce-scatter.7.cloned.1.call-done), channel_id=1, source_target_pairs={{0,0},{8,1},{16,2},{24,3},{1,4},{9,5},{17,6},{25,7},{2,8},{10,9},{... | collective-permute-start | bytes 786440 | tf_op jit(solution)/shard_map/ppermute | solution.py:836
  (21 other events, 49.9 us)
Sparse Core Ops, SparseCore 0:
  27.2 31.2 all-gather.3
  68.0 101.7 all-gather.5
  172.2 44.0 all-gather.7
  464.4 26.2 reduce-scatter.6
  493.8 39.5 reduce-scatter.4
  536.5 43.9 reduce-scatter.10
  583.8 75.6 reduce-scatter.8

commit v3 on v2

v3 whole, which is shorter than its diff:
```python
import functools

import jax
import jax.numpy as jnp
from jax import lax
from jax.experimental import pallas as pl
from jax.experimental.pallas import tpu as pltpu
from jax.sharding import PartitionSpec as P

H = 16
KV = 8
HD = 128


epsilon = 1e-06
rope_base = 1000000.0
negative = -1e30
low = jnp.bfloat16
full = jnp.float32
MESH = pl.DeviceIdType.MESH
ANY = pl.BlockSpec(memory_space=pl.ANY)
IN_VMEM = pl.BlockSpec(memory_space=pltpu.VMEM)
DMA = pltpu.SemaphoreType.DMA


def product(left_side, right_side):
    return jnp.dot(left_side, right_side, preferred_element_type=full)


def product_nt(left_side, right_side):
    return lax.dot_general(
        left_side, right_side, (((1,), (1,)), ((), ())), preferred_element_type=full
    )


def product_tn(left_side, right_side):
    return lax.dot_general(
        left_side, right_side, (((0,), (0,)), ((), ())), preferred_element_type=full
    )


def remote(source, target, send, receive, axis, peer):
    return pltpu.make_async_remote_copy(
        src_ref=source,
        dst_ref=target,
        send_sem=send,
        recv_sem=receive,
        device_id={axis: peer},
        device_id_type=MESH,
    )


def greet(peers):
    barrier = pltpu.get_barrier_semaphore()
    for axis, peer, exists in peers:
        if exists is True:
            pl.semaphore_signal(barrier, inc=1, device_id={axis: peer}, device_id_type=MESH)
        else:

            @pl.when(exists)
            def _():
                pl.semaphore_signal(barrier, inc=1, device_id={axis: peer}, device_id_type=MESH)

    arrivals = sum(1 for _, _, exists in peers if exists is True)
    for _, _, exists in peers:
        if exists is not True:
            arrivals = arrivals + exists.astype(jnp.int32)
    pl.semaphore_wait(barrier, arrivals)


def others(axis, count):
    me = lax.axis_index(axis)
    return [(axis, lax.rem(me + shift, count), True) for shift in range(1, count)]


class Line:
    def __init__(self, pieces):
        self.chips = pieces // 2
        self.me = lax.axis_index("ctx")
        self.chip, self.core = self.me // 2, lax.rem(self.me, 2)
        self.sibling = self.me + 1 - 2 * self.core
        self.right, self.left = self.me + 2, self.me - 2
        self.has_right, self.has_left = self.chip < self.chips - 1, self.chip > 0

    def peers(self):
        return [
            ("ctx", self.sibling, True),
            ("ctx", self.right, self.has_right),
            ("ctx", self.left, self.has_left),
        ]


def gather_scratch(pieces, parts):
    chips = pieces // 2
    return [DMA((chips, 2, parts))] * 2 + [DMA((chips, parts))] * 4


class Gather:
    def __init__(self, line, parts, rows, out_ref, sems):
        self.line, self.parts, self.rows, self.out_ref = line, parts, rows, out_ref
        self.size = rows // parts
        self.sib_send, self.sib_recv, self.r_send, self.r_recv, self.l_send, self.l_recv = sems

    def at(self, position, part):
        start = pl.multiple_of(position * self.rows + part * self.size, self.size)
        return self.out_ref.at[pl.ds(start, self.size)]

    def to_sibling(self, source, hop, side, part, position):
        return remote(
            source,
            self.at(position, part),
            self.sib_send.at[hop, side, part],
            self.sib_recv.at[hop, side, part],
            "ctx",
            self.line.sibling,
        )

    def to_right(self, source, hop, part, position):
        return remote(
            source,
            self.at(position, part),
            self.r_send.at[hop, part],
            self.r_recv.at[hop, part],
            "ctx",
            self.line.right,
        )

    def to_left(self, source, hop, part, position):
        return remote(
            source,
            self.at(position, part),
            self.l_send.at[hop, part],
            self.l_recv.at[hop, part],
            "ctx",
            self.line.left,
        )

    def start(self, x_ref):
        line = self.line
        for part in range(self.parts):
            piece = x_ref.at[pl.ds(part * self.size, self.size)]

            @pl.when(line.has_right)
            def _():
                self.to_right(piece, 0, part, line.me).start()

            @pl.when(line.has_left)
            def _():
                self.to_left(piece, 0, part, line.me).start()

            self.to_sibling(piece, 0, 0, part, line.me).start()

    def forward(self, hop):
        line = self.line
        for part in range(self.parts):
            from_left, from_right = line.me - 2 * hop, line.me + 2 * hop

            @pl.when(line.chip - hop >= 0)
            def _():
                piece = self.at(from_left, part)
                self.to_right(piece, hop - 1, part, from_left).wait_recv()

                @pl.when(line.has_right)
                def _():
                    self.to_right(piece, hop, part, from_left).start()

                self.to_sibling(piece, hop, 0, part, from_left).start()

            @pl.when(line.chip + hop < line.chips)
            def _():
                piece = self.at(from_right, part)
                self.to_left(piece, hop - 1, part, from_right).wait_recv()

                @pl.when(line.has_left)
                def _():
                    self.to_left(piece, hop, part, from_right).start()

                self.to_sibling(piece, hop, 1, part, from_right).start()

    def legs(self, hop):
        line = self.line
        return [
            (
                side,
                (line.chip - hop >= 0) if side == 0 else (line.chip + hop < line.chips),
                (line.me - 2 * hop) if side == 0 else (line.me + 2 * hop),
            )
            for side in range(1 if hop == 0 else 2)
        ]

    def arrive(self, hop):
        for side, there, position in self.legs(hop):
            for part in range(self.parts):

                @pl.when(there)
                def _():
                    self.to_sibling(
                        self.at(position, part), hop, side, part, position
                    ).wait_recv()

    def finish(self):
        line = self.line
        for hop in range(line.chips):
            for side, there, position in self.legs(hop):
                for part in range(self.parts):

                    @pl.when(there)
                    def _():
                        piece = self.at(position, part)
                        self.to_sibling(piece, hop, side, part, position).wait_send()
                        if side == 0:

                            @pl.when(line.has_right)
                            def _():
                                self.to_right(piece, hop, part, position).wait_send()

                        if side == 1 or hop == 0:

                            @pl.when(line.has_left)
                            def _():
                                self.to_left(piece, hop, part, position).wait_send()

    def complete(self):
        for hop in range(self.line.chips):
            self.arrive(hop)
        self.finish()


def scatter_scratch(pieces, rows, width):
    chips = pieces // 2
    slots = pltpu.VMEM((chips, rows, width), low)
    return [slots] * 3 + [pltpu.VMEM((chips + 1, rows, width), low)] + [DMA((chips,))] * 6


class Scatter:
    def __init__(self, line, rows, scratch):
        self.line, self.rows = line, rows
        (
            self.own,
            self.give,
            self.sib,
            self.arrived,
            self.sib_send,
            self.sib_recv,
            self.r_send,
            self.r_recv,
            self.l_send,
            self.l_recv,
        ) = scratch

    def there(self, far, side):
        line = self.line
        return (line.chip + far < line.chips) if side == 0 else (line.chip - far >= 0)

    def target(self, far, side):
        return self.line.chip + far if side == 0 else self.line.chip - far

    def exchange(self, target):
        return remote(
            self.give.at[target],
            self.sib.at[target],
            self.sib_send.at[target],
            self.sib_recv.at[target],
            "ctx",
            self.line.sibling,
        )

    def send(self, target, side):
        if side == 0:
            return remote(
                self.own.at[target],
                self.arrived.at[target],
                self.r_send.at[target],
                self.r_recv.at[target],
                "ctx",
                self.line.right,
            )
        chips, chip = self.line.chips, self.line.chip
        return remote(
            self.own.at[target],
            self.arrived.at[jnp.where(target == chip - 1, chips, target)],
            self.l_send.at[target],
            self.l_recv.at[target],
            "ctx",
            self.line.left,
        )

    def order(self):
        return [
            (far, side)
            for far in range(self.line.chips - 1, -1, -1)
            for side in range(2 if far else 1)
        ]

    def fill(self, far, side, block):
        @pl.when(self.there(far, side))
        def _():
            target = self.target(far, side)

            def store(columns, value):
                first, second = value[: self.rows], value[self.rows :]
                mine = self.line.core == 0
                self.own[target, :, columns] = jnp.where(mine, first, second).astype(low)
                self.give[target, :, columns] = jnp.where(mine, second, first).astype(low)

            block(target, store)
            self.exchange(target).start()

    def push(self, far, side):
        line = self.line
        behind = line.has_left if side == 0 else line.has_right

        @pl.when(self.there(far, side))
        def _():
            target = self.target(far, side)
            self.exchange(target).wait_recv()
            total = self.own[target].astype(full) + self.sib[target].astype(full)
            if far == line.chips - 1:
                self.own[target] = total.astype(low)
            else:

                @pl.when(behind)
                def _():
                    self.send(target, side).wait_recv()
                    self.own[target] = (total + self.arrived[target].astype(full)).astype(low)

                @pl.when(jnp.logical_not(behind))
                def _():
                    self.own[target] = total.astype(low)

            self.send(target, side).start()

    def total(self, total_ref):
        line = self.line
        chip = line.chip
        self.exchange(chip).wait_recv()
        total_ref[...] = self.own[chip].astype(full) + self.sib[chip].astype(full)

        @pl.when(line.has_left)
        def _():
            self.send(chip, 0).wait_recv()
            total_ref[...] += self.arrived[chip].astype(full)

        @pl.when(line.has_right)
        def _():
            self.send(chip, 1).wait_recv()
            total_ref[...] += self.arrived[line.chips].astype(full)

    def finish(self):
        for far, side in self.order():

            @pl.when(self.there(far, side))
            def _():
                target = self.target(far, side)
                self.exchange(target).wait_send()
                if far > 0:
                    self.send(target, side).wait_send()


def blocks_nn(left_ref, right_ref, rows, tile=512):
    def block(target, store):
        start = pl.multiple_of(target * 2 * rows, 2 * rows)
        left_side = left_ref[pl.ds(start, 2 * rows), :]

        def step(index, unused):
            columns = pl.ds(pl.multiple_of(index * tile, tile), tile)
            store(columns, product(left_side, right_ref[:, columns]))
            return unused

        lax.fori_loop(0, right_ref.shape[1] // tile, step, 0)

    return block


def blocks_nt(left_ref, right_ref, rows, tile=512):
    def block(target, store):
        start = pl.multiple_of(target * 2 * rows, 2 * rows)
        left_side = left_ref[pl.ds(start, 2 * rows), :]

        def step(index, unused):
            columns = pl.ds(pl.multiple_of(index * tile, tile), tile)
            store(columns, product_nt(left_side, right_ref[columns, :]))
            return unused

        lax.fori_loop(0, right_ref.shape[0] // tile, step, 0)

    return block


class Swap:
    def __init__(self, pieces, send_of, recv_of, send_sem, recv_sem):
        self.pieces, self.me = pieces, lax.axis_index("ctx")
        self.send_of, self.recv_of = send_of, recv_of
        self.send_sem, self.recv_sem = send_sem, recv_sem

    def copy(self, shift):
        peer = lax.rem(self.me + shift, self.pieces)
        return remote(
            self.send_of(peer),
            self.recv_of(self.me),
            self.send_sem.at[shift],
            self.recv_sem.at[shift],
            "ctx",
            peer,
        )

    def start(self):
        for shift in range(1, self.pieces):
            self.copy(shift).start()

    def wait_recv(self, shift):
        source = lax.rem(self.me + self.pieces - shift, self.pieces)
        remote(
            self.send_of(source),
            self.recv_of(source),
            self.send_sem.at[shift],
            self.recv_sem.at[shift],
            "ctx",
            source,
        ).wait_recv()
        return source

    def finish(self):
        for shift in range(1, self.pieces):
            self.copy(shift).wait_send()


def opening_kernel(
    pieces,
    groups,
    parts,
    hidden_ref,
    gains_ref,
    attn_ref,
    normed_ref,
    attn_out,
    gains_out,
    gains_row,
    gains_all,
    gain_vector,
    normed,
    own_sem,
    own_attn,
    ga_send,
    ga_recv,
    gs_send,
    gs_recv,
    at_send,
    at_recv,
    as_send,
    as_recv,
    *sems,
):
    line = Line(pieces)
    me, group = line.me, lax.axis_index("seq")
    greet(others("ctx", pieces) + others("seq", groups))
    rows, model = hidden_ref.shape
    gain_count = gains_ref.shape[1]
    gains_row[...] = jnp.zeros(gains_row.shape, full)
    gains_row[0:1, pl.ds(0, gain_count)] = gains_ref[...].astype(low).astype(full)
    gains_all[group, me] = gains_row[...]
    gain_swap = Swap(
        pieces, lambda peer: gains_row, lambda peer: gains_all.at[group, peer], ga_send, ga_recv
    )
    gain_swap.start()
    attn_swap = Swap(
        pieces, lambda peer: attn_ref.at[peer], lambda peer: attn_out.at[group, peer], at_send, at_recv
    )
    attn_swap.start()
    attn_own = pltpu.make_async_copy(attn_ref.at[me], attn_out.at[group, me], own_attn)
    attn_own.start()
    values = hidden_ref[...].astype(full)
    inverse = lax.rsqrt(jnp.mean(values * values, axis=-1, keepdims=True) + epsilon)

    def to_groups(ref, sends, receives, shift):
        peer = lax.rem(group + shift, groups)
        return remote(ref.at[group], ref.at[group], sends.at[shift], receives.at[shift], "seq", peer)

    def from_groups(ref, sends, receives, shift):
        peer = lax.rem(group + groups - shift, groups)
        remote(
            ref.at[peer], ref.at[peer], sends.at[shift], receives.at[shift], "seq", peer
        ).wait_recv()

    for shift in range(1, pieces):
        gain_swap.wait_recv(shift)
    for shift in range(1, groups):
        to_groups(gains_all, gs_send, gs_recv, shift).start()
    for shift in range(1, groups):
        from_groups(gains_all, gs_send, gs_recv, shift)
    for index in range(groups * pieces):
        gain_vector[0:1, pl.ds(index * gain_count, gain_count)] = gains_all[
            index // pieces, index % pieces, 0:1, pl.ds(0, gain_count)
        ]
    gains_out[...] = gain_vector[...]
    normed[...] = (values * inverse * gain_vector[0:1, pl.ds(0, model)]).astype(low)
    gather = Gather(line, parts, rows, normed_ref, sems)
    gather.start(normed)
    start = pl.multiple_of(me * rows, rows)
    own = pltpu.make_async_copy(normed, normed_ref.at[pl.ds(start, rows)], own_sem)
    own.start()
    for shift in range(1, pieces):
        attn_swap.wait_recv(shift)
    attn_own.wait()
    for shift in range(1, groups):
        to_groups(attn_out, as_send, as_recv, shift).start()
    for hop in range(1, line.chips):
        gather.forward(hop)
    own.wait()
    gather.complete()
    for shift in range(1, groups):
        from_groups(attn_out, as_send, as_recv, shift)
    gain_swap.finish()
    attn_swap.finish()
    for shift in range(1, groups):
        to_groups(gains_all, gs_send, gs_recv, shift).wait_send()
        to_groups(attn_out, as_send, as_recv, shift).wait_send()


def opening(hidden_in, norm_gains, attn_blocks, number, parts=2):
    pieces, groups = lax.axis_size("ctx"), lax.axis_size("seq")
    rows, model = hidden_in.shape
    gains = norm_gains.shape[0]
    lanes = -(-gains // 128) * 128
    return pl.pallas_call(
        functools.partial(opening_kernel, pieces, groups, parts),
        out_shape=(
            jax.ShapeDtypeStruct((pieces * rows, model), low),
            jax.ShapeDtypeStruct((groups,) + attn_blocks.shape, low),
            jax.ShapeDtypeStruct((1, groups * pieces * gains), full),
        ),
        in_specs=[IN_VMEM, IN_VMEM, IN_VMEM],
        out_specs=(ANY, ANY, IN_VMEM),
        scratch_shapes=[
            pltpu.VMEM((8, lanes), full),
            pltpu.VMEM((groups, pieces, 8, lanes), full),
            pltpu.VMEM((1, groups * pieces * gains), full),
            pltpu.VMEM((rows, model), low),
            DMA,
            DMA,
            DMA((pieces,)),
            DMA((pieces,)),
            DMA((groups,)),
            DMA((groups,)),
            DMA((pieces,)),
            DMA((pieces,)),
            DMA((groups,)),
            DMA((groups,)),
        ]
        + gather_scratch(pieces, parts),
        compiler_params=pltpu.CompilerParams(
            collective_id=number, has_side_effects=True, vmem_limit_bytes=60 << 20
        ),
        name=f"opening_{number}",
    )(hidden_in, norm_gains.reshape(1, gains), attn_blocks)


class LineSwap:
    def __init__(self, line, send_of, recv_of, s_sem, r_sem):
        self.line, self.send_of, self.recv_of = line, send_of, recv_of
        self.s_sem, self.r_sem = s_sem, r_sem

    def copy(self, far, side, core):
        line = self.line
        if far == 0:
            peer, slot = line.sibling, self.r_sem.at[0, 0, 0]
        else:
            peer = (line.chip + (far if side == 0 else -far)) * 2 + core
            slot = self.r_sem.at[far, side, line.core]
        return remote(
            self.send_of(peer), self.recv_of(line.me), self.s_sem.at[far, side, core], slot, "ctx", peer
        )

    def legs(self, far):
        line = self.line
        if far == 0:
            return [(0, 0, True, True)]
        return [
            (
                side,
                core,
                (line.chip + far < line.chips) if side == 0 else (line.chip - far >= 0),
                (line.chip - far >= 0) if side == 0 else (line.chip + far < line.chips),
            )
            for side in range(2)
            for core in range(2)
        ]

    def start(self):
        for far in range(self.line.chips):
            for side, core, sends, _ in self.legs(far):
                if far == 0:
                    self.copy(far, side, core).start()
                else:

                    @pl.when(sends)
                    def _():
                        self.copy(far, side, core).start()

    def receive(self, far, then):
        line = self.line
        for side, core, _, comes in self.legs(far):
            if far == 0:
                source, slot = line.sibling, self.r_sem.at[0, 0, 0]
            else:
                source = (line.chip + (-far if side == 0 else far)) * 2 + core
                slot = self.r_sem.at[far, side, core]

            def wait():
                remote(
                    self.recv_of(source),
                    self.recv_of(source),
                    self.s_sem.at[far, side, core],
                    slot,
                    "ctx",
                    source,
                ).wait_recv()
                then(source)

            if far == 0:
                wait()
            else:
                pl.when(comes)(wait)

    def finish(self):
        for far in range(self.line.chips):
            for side, core, sends, _ in self.legs(far):
                if far == 0:
                    self.copy(far, side, core).wait_send()
                else:

                    @pl.when(sends)
                    def _():
                        self.copy(far, side, core).wait_send()


def swap_scratch(pieces):
    return [DMA((pieces // 2, 2, 2))] * 2


class Share:
    def __init__(self, groups, place, s_sem, r_sem):
        self.groups, self.place, self.s_sem, self.r_sem = groups, place, s_sem, r_sem
        self.group = lax.axis_index("seq")

    def copy(self, source, shift, origin=None):
        peer = lax.rem(self.group + shift, self.groups)
        target = self.place(self.group, source)
        return remote(
            target if origin is None else origin,
            target,
            self.s_sem.at[source, shift],
            self.r_sem.at[source, shift],
            "seq",
            peer,
        )

    def send(self, source, origin=None):
        for shift in range(1, self.groups):
            self.copy(source, shift, origin).start()

    def finish(self, sources):
        for source in range(sources):
            for shift in range(1, self.groups):
                peer = lax.rem(self.group + self.groups - shift, self.groups)
                remote(
                    self.place(peer, source),
                    self.place(peer, source),
                    self.s_sem.at[source, shift],
                    self.r_sem.at[source, shift],
                    "seq",
                    peer,
                ).wait_recv()
                self.copy(source, shift).wait_send()


def lanes(start, size):
    return pl.ds(pl.multiple_of(start, 128), size)


def turn(values, cosine, sine):
    half = values.shape[0] // 2
    first, second = values[:half], values[half:]
    return jnp.concatenate(
        [first * cosine - second * sine, second * cosine + first * sine], axis=0
    )


def turn_back(values, cosine, sine):
    half = values.shape[0] // 2
    first, second = values[:half], values[half:]
    return jnp.concatenate(
        [first * cosine + second * sine, second * cosine - first * sine], axis=0
    )


def inverse_rms(values):
    return lax.rsqrt(jnp.mean(values * values, axis=0, keepdims=True) + epsilon)


def kept(first_key, keys, first_query, queries, prefix):
    key = first_key + lax.broadcasted_iota(jnp.int32, (keys, queries), 0)
    query = first_query + lax.broadcasted_iota(jnp.int32, (keys, queries), 1)
    return key <= jnp.maximum(query, prefix - 1)


def query_blocks(length, body):
    tile = min(256, length // 2)
    half = length // 2

    def early(index, unused):
        body(index * tile, tile, half)
        return unused

    def late(index, unused):
        body(half + index * tile, tile, length)
        return unused

    lax.fori_loop(0, half // tile, early, 0)
    lax.fori_loop(0, half // tile, late, 0)


def attend_kernel(
    shape,
    raw,
    cosine,
    sine,
    query_gain,
    key_gain,
    prefix_ref,
    out_low,
    hidden,
    swiglu_gain,
    out_grad,
    gate_weight,
    up_weight,
    raw_t,
    gate_t,
    q_ref,
    qt_ref,
    k_ref,
    kt_ref,
    v_ref,
    att_t,
    lse_ref,
    gated_t,
    middle,
    normed_two,
    og_all,
    ff_low,
    vt_ref,
    gated,
    blocks,
    own_sem,
    og_sem,
    swap_s,
    swap_r,
    share_s,
    share_r,
    *sems,
):
    pieces, groups, heads, kv_heads, ff_block = shape
    gather_sems, scatter_refs = sems[:6], sems[6:]
    line = Line(pieces)
    me, group = line.me, lax.axis_index("seq")
    length, rows = raw.shape[0], hidden.shape[0]
    greet(others("ctx", pieces) + others("seq", groups))
    own_width = groups * ff_block
    for half, weight_ref in enumerate((gate_weight, up_weight)):
        for index in range(groups):
            for piece in range(pieces):
                start = (index * pieces + piece) * ff_block
                blocks[piece, :, pl.ds(half * own_width + index * ff_block, ff_block)] = weight_ref[
                    :, pl.ds(start, ff_block)
                ].astype(low)
    swap = LineSwap(
        line, lambda peer: blocks.at[peer], lambda source: ff_low.at[group, source], swap_s, swap_r
    )
    swap.start()
    share = Share(groups, lambda index, source: ff_low.at[index, source], share_s, share_r)
    share.send(me, blocks.at[me])
    own = pltpu.make_async_copy(blocks.at[me], ff_low.at[group, me], own_sem)
    own.start()

    prefix = prefix_ref[0, 0]
    scale = HD ** (-0.5)
    for head in range(heads + kv_heads):
        part = pl.ds(head * HD, HD)
        values = raw[:, part].T
        raw_t[part, :] = values
        gain = query_gain[...] if head < heads else key_gain[...]
        turned = turn(values * inverse_rms(values) * gain, cosine[...], sine[...])
        if head < heads:
            qt_ref[part, :] = turned.astype(low)
            q_ref[:, part] = turned.T.astype(low)
        else:
            part = pl.ds((head - heads) * HD, HD)
            kt_ref[part, :] = turned.astype(low)
            k_ref[:, part] = turned.T.astype(low)
    for head in range(kv_heads):
        part = pl.ds(head * HD, HD)
        values = raw[:, pl.ds((heads + kv_heads + head) * HD, HD)]
        v_ref[:, part] = values.astype(low)
        vt_ref[part, :] = values.T.astype(low)
    gate_t[...] = raw[:, pl.ds((heads + 2 * kv_heads) * HD, HD)].T[: gate_t.shape[0]]
    swap.receive(0, share.send)
    for head in range(heads):
        part = pl.ds(head * HD, HD)
        kv_part = pl.ds(head * kv_heads // heads * HD, HD)

        def block(first, tile, keys):
            columns = lanes(first, tile)
            scores = product(k_ref[pl.ds(0, keys), kv_part], qt_ref[part, columns]) * scale
            scores = jnp.where(kept(0, keys, first, tile, prefix), scores, negative)
            top = jnp.max(scores, axis=0, keepdims=True)
            expanded = jnp.exp(scores - top)
            total = jnp.sum(expanded, axis=0, keepdims=True)
            lse_ref[head : head + 1, columns] = top + jnp.log(total)
            att_t[part, columns] = (
                product(vt_ref[kv_part, pl.ds(0, keys)], expanded.astype(low)) / total
            )

        query_blocks(length, block)
        scaled = att_t[part, :] * jax.nn.sigmoid(gate_t[head : head + 1, :])
        gated_t[part, :] = scaled.astype(low)
        gated[:, part] = scaled.T.astype(low)
        if head == 0:
            swap.receive(1, share.send)

    gather = Gather(line, 2, rows, og_all, gather_sems)
    scatter = Scatter(line, rows, scatter_refs)
    block = blocks_nn(gated, out_low, rows)
    last = line.chips - 1
    for far, side in scatter.order():
        if far == last:
            scatter.fill(far, side, block)
    gather.start(out_grad)
    start = pl.multiple_of(me * rows, rows)
    og_own = pltpu.make_async_copy(out_grad, og_all.at[pl.ds(start, rows)], og_sem)
    og_own.start()
    for far, side in scatter.order():
        if far == last:
            scatter.push(far, side)
    for far, side in scatter.order():
        if far < last:
            scatter.fill(far, side, block)
    for far in range(2, line.chips):
        swap.receive(far, share.send)
    for hop in range(1, line.chips):
        for far, side in scatter.order():
            if far == last - hop and far > 0:
                scatter.push(far, side)
        gather.forward(hop)
    scatter.total(middle)
    values = hidden[...].astype(full) + middle[...]
    middle[...] = values
    inverse = lax.rsqrt(jnp.mean(values * values, axis=-1, keepdims=True) + epsilon)
    normed_two[...] = (values * inverse * swiglu_gain[...]).astype(low)
    og_own.wait()
    own.wait()
    gather.complete()
    scatter.finish()
    swap.finish()
    share.finish(pieces)


def attend(raw, tables, gains, prefix, out_low, hidden, swiglu_gain, out_grad, weights, shape, number):
    pieces, groups, heads, kv_heads, ff_block = shape
    length, rows, model = raw.shape[0], hidden.shape[0], hidden.shape[1]
    q_width, kv_width = heads * HD, kv_heads * HD
    weight_rows = weights[0].shape[0]
    struct = jax.ShapeDtypeStruct
    return pl.pallas_call(
        functools.partial(attend_kernel, shape),
        out_shape=(
            struct((q_width + kv_width, length), full),
            struct((8, length), full),
            struct((length, q_width), low),
            struct((q_width, length), low),
            struct((length, kv_width), low),
            struct((kv_width, length), low),
            struct((length, kv_width), low),
            struct((q_width, length), full),
            struct((8, length), full),
            struct((q_width, length), low),
            struct((rows, model), full),
            struct((rows, model), low),
            struct((length, model), low),
            struct((groups, pieces, weight_rows, 2 * groups * ff_block), low),
        ),
        in_specs=[IN_VMEM] * 5 + [pl.BlockSpec(memory_space=pltpu.SMEM)] + [IN_VMEM] * 6,
        out_specs=(IN_VMEM,) * 12 + (ANY, ANY),
        scratch_shapes=[
            pltpu.VMEM((kv_width, length), low),
            pltpu.VMEM((length, q_width), low),
            pltpu.VMEM((pieces, weight_rows, 2 * groups * ff_block), low),
            DMA,
            DMA,
        ]
        + swap_scratch(pieces)
        + [DMA((pieces, groups))] * 2
        + gather_scratch(pieces, 2)
        + scatter_scratch(pieces, rows, model),
        compiler_params=pltpu.CompilerParams(
            collective_id=number, has_side_effects=True, vmem_limit_bytes=60 << 20
        ),
        name=f"attend_{number}",
    )(raw, *tables, *gains, prefix, out_low, hidden, swiglu_gain, out_grad, *weights)


def attend_back_kernel(
    shape,
    grad_branch,
    out_low,
    raw_t,
    gate_t,
    q_ref,
    qt_ref,
    k_ref,
    kt_ref,
    v_ref,
    att_t,
    lse_ref,
    cosine,
    sine,
    query_gain,
    key_gain,
    prefix_ref,
    normed,
    attn_low,
    hidden,
    grad_middle,
    attention_gain,
    swiglu_gain_grad,
    ff_share,
    hidden_grad,
    gains_grad,
    query_grad,
    key_grad,
    value_grad,
    head_grad,
    gate_grad,
    up_grad,
    gg_t,
    ga_t,
    ga,
    gqt,
    dk,
    dv,
    grad_t,
    grad,
    total_ref,
    ff_recv,
    normed_part,
    part_sem,
    term,
    term_in,
    attn_send,
    attn_recv,
    gains_vector,
    gain_give,
    gain_sib,
    gain_row,
    gain_last,
    ffs_s,
    ffs_r,
    at_s,
    at_r,
    gc_s,
    gc_r,
    ts_s,
    ts_r,
    gs_s,
    gs_r,
    *scatter_refs,
):
    pieces, groups, heads, kv_heads, ff_block = shape
    line = Line(pieces)
    me, group = line.me, lax.axis_index("seq")
    length, rows = grad_branch.shape[0], hidden.shape[0]
    width, model = attn_low.shape[1], attn_low.shape[0]
    weight_rows = ff_share.shape[1]
    q_width, kv_width = heads * HD, kv_heads * HD
    greet(others("ctx", pieces) + others("seq", groups))
    ff_swap = LineSwap(
        line, lambda peer: ff_share.at[peer], lambda source: ff_recv.at[source], ffs_s, ffs_r
    )
    ff_swap.start()

    prefix = prefix_ref[0, 0]
    scale = HD ** (-0.5)

    def branch(index, unused):
        columns = lanes(index * 256, 256)
        gg_t[:, columns] = product_nt(out_low[...], grad_branch[columns, :])
        return unused

    lax.fori_loop(0, length // 256, branch, 0)
    dk[...] = jnp.zeros(dk.shape, full)
    dv[...] = jnp.zeros(dv.shape, full)
    gate_rows = []
    for head in range(heads):
        part = pl.ds(head * HD, HD)
        kv_part = pl.ds(head * kv_heads // heads * HD, HD)
        sigmoid = jax.nn.sigmoid(gate_t[head : head + 1, :])
        grads = gg_t[part, :]
        rounded = (grads * sigmoid).astype(low)
        ga_t[...] = rounded
        ga[...] = rounded.astype(full).T.astype(low)
        gate_rows.append(
            jnp.sum(grads * att_t[part, :], axis=0, keepdims=True) * sigmoid * (1.0 - sigmoid)
        )

        def block(first, tile, keys):
            columns, across = lanes(first, tile), pl.ds(0, keys)
            scores = product(k_ref[across, kv_part], qt_ref[part, columns]) * scale
            chance = jnp.where(
                kept(0, keys, first, tile, prefix),
                jnp.exp(scores - lse_ref[head : head + 1, columns]),
                0.0,
            )
            taken = ga_t[:, columns]
            delta = jnp.sum(taken.astype(full) * att_t[part, columns], axis=0, keepdims=True)
            change = product(v_ref[across, kv_part], taken)
            score_grad = (chance * (change - delta)).astype(low)
            gqt[part, columns] = product(kt_ref[kv_part, across], score_grad) * scale
            dk[across, kv_part] += product(score_grad, q_ref[columns, part])
            dv[across, kv_part] += product(chance.astype(low), ga[columns, :])

        query_blocks(length, block)

    gain_columns = [jnp.zeros((HD, 1), full), jnp.zeros((HD, 1), full)]
    for head in range(heads + kv_heads):
        part = pl.ds(head * HD, HD)
        if head < heads:
            turned = gqt[part, :]
            gain = query_gain[...]
        else:
            turned = dk[:, pl.ds((head - heads) * HD, HD)].T * scale
            gain = key_gain[...]
        grads = turn_back(turned, cosine[...], sine[...])
        values = raw_t[part, :]
        inverse = inverse_rms(values)
        kind = 0 if head < heads else 1
        gain_columns[kind] = gain_columns[kind] + jnp.sum(
            grads * values * inverse, axis=1, keepdims=True
        )
        scaled = grads * gain
        result = inverse * scaled - values * (
            inverse * inverse * inverse * jnp.mean(scaled * values, axis=0, keepdims=True)
        )
        grad_t[part, :] = result.astype(low)
        grad[:, part] = result.T.astype(low)
    for head in range(kv_heads):
        part = pl.ds((heads + kv_heads + head) * HD, HD)
        values = dv[:, pl.ds(head * HD, HD)]
        grad[:, part] = values.astype(low)
        grad_t[part, :] = values.T.astype(low)
    part = pl.ds((heads + 2 * kv_heads) * HD, HD)
    gate_block = jnp.concatenate(
        gate_rows + [jnp.zeros((HD - heads, length), full)], axis=0
    )
    grad_t[part, :] = gate_block.astype(low)
    grad[:, part] = gate_block.T.astype(low)

    scatter = Scatter(line, rows, scatter_refs)
    block = blocks_nt(grad, attn_low, rows)
    last = line.chips - 1
    for far, side in scatter.order():
        if far == last:
            scatter.fill(far, side, block)
    for far, side in scatter.order():
        if far == last:
            scatter.push(far, side)
    for far, side in scatter.order():
        if far == last - 1:
            scatter.fill(far, side, block)

    share = model // groups

    def to_group(shift):
        peer = lax.rem(group + shift, groups)
        return remote(term.at[peer], term_in.at[shift], ts_s.at[shift], ts_r.at[shift], "seq", peer)

    shifts = list(range(1, groups)) + [0]

    def load(job):
        index = lax.rem(group + shifts[job], groups)
        return pltpu.make_async_copy(
            normed.at[:, lanes(index * share, share)], normed_part.at[job % 2], part_sem.at[job % 2]
        )

    def weight_grad(job, index):
        load(job).wait()
        if job + 1 < groups:
            load(job + 1).start()

        def step(tile, unused):
            value = product(grad_t[...], normed_part[job % 2, :, lanes(tile * 128, 128)])
            term[index, pl.ds(pl.multiple_of(tile * 128, 128), 128), :] = value.T.astype(low)
            return unused

        lax.fori_loop(0, share // 128, step, 0)

    load(0).start()
    for job, shift in enumerate(shifts):
        weight_grad(job, lax.rem(group + shift, groups))
        if shift:
            to_group(shift).start()
    for far, side in scatter.order():
        if far < last - 1:
            scatter.fill(far, side, block)
    for hop in range(1, line.chips):
        for far, side in scatter.order():
            if far == last - hop and far > 0:
                scatter.push(far, side)

    for far in range(line.chips):
        ff_swap.receive(far, lambda source: None)
    ff_recv[me] = ff_share[me]
    own_width = groups * ff_block
    for half, grad_ref in enumerate((gate_grad, up_grad)):
        for index in range(groups):
            for piece in range(pieces):
                start = (index * pieces + piece) * ff_block
                grad_ref[:, pl.ds(start, ff_block)] = ff_recv[
                    piece, :, pl.ds(half * own_width + index * ff_block, ff_block)
                ]

    for shift in range(1, groups):
        peer = lax.rem(group + groups - shift, groups)
        remote(
            term.at[peer], term_in.at[shift], ts_s.at[shift], ts_r.at[shift], "seq", peer
        ).wait_recv()
    for piece in range(pieces):
        across = pl.ds(piece * weight_rows, weight_rows)
        summed = term[group, across, :].astype(full)
        for shift in range(1, groups):
            summed = summed + term_in[shift, across, :].astype(full)
        attn_send[piece] = summed.astype(low)
    attn_swap = LineSwap(
        line, lambda peer: attn_send.at[peer], lambda source: attn_recv.at[source], at_s, at_r
    )
    attn_swap.start()

    scatter.total(total_ref)
    values = hidden[...].astype(full)
    inverse = lax.rsqrt(jnp.mean(values * values, axis=-1, keepdims=True) + epsilon)
    grads = total_ref[...]
    scaled = grads * attention_gain[...]
    hidden_grad[...] = (
        grad_middle[...]
        + inverse * scaled
        - values
        * (inverse * inverse * inverse * jnp.mean(scaled * values, axis=-1, keepdims=True))
    ).astype(low)

    gain_count = gains_grad.shape[1]
    gains_vector[:, pl.ds(0, model)] = jnp.sum(grads * values * inverse, axis=0, keepdims=True)
    gains_vector[:, pl.ds(model, model)] = swiglu_gain_grad[...]
    for kind in range(2):
        wide = jnp.broadcast_to(gain_columns[kind], (HD, HD)).T
        gains_vector[:, pl.ds(2 * model + kind * HD, HD)] = wide[0:1, :]
    gain_give[...] = jnp.zeros(gain_give.shape, full)
    for index in range(groups * pieces):
        gain_give[index % pieces, index // pieces, 0:1, pl.ds(0, gain_count)] = gains_vector[
            :, pl.ds(index * gain_count, gain_count)
        ]
    gain_swap = LineSwap(
        line, lambda peer: gain_give.at[peer], lambda source: gain_sib.at[source], gc_s, gc_r
    )
    gain_swap.start()
    gain_sib[me] = gain_give[me]
    for far in range(line.chips):
        gain_swap.receive(far, lambda source: None)
    gain_row[...] = jnp.sum(gain_sib[...], axis=0)

    def gain_to(shift):
        peer = lax.rem(group + shift, groups)
        return remote(
            gain_row.at[peer], gain_last.at[shift], gs_s.at[shift], gs_r.at[shift], "seq", peer
        )

    for shift in range(1, groups):
        gain_to(shift).start()
    gain_last[0] = gain_row[group]
    for shift in range(1, groups):
        peer = lax.rem(group + groups - shift, groups)
        remote(
            gain_row.at[peer], gain_last.at[shift], gs_s.at[shift], gs_r.at[shift], "seq", peer
        ).wait_recv()
    gains_grad[...] = jnp.sum(gain_last[...], axis=0)[0:1, pl.ds(0, gain_count)]

    for far in range(line.chips):
        attn_swap.receive(far, lambda source: None)
    attn_recv[me] = attn_send[me]
    copies = max(1, pieces // KV)
    for piece in range(pieces):
        query_grad[:, pl.ds(piece * q_width, q_width)] = attn_recv[piece, :, pl.ds(0, q_width)]
        head_grad[:, pl.ds(piece * heads, heads)] = attn_recv[
            piece, :, pl.ds(q_width + 2 * kv_width, heads)
        ].astype(full)
    for place in range(pieces // copies):
        for kind, grad_ref in enumerate((key_grad, value_grad)):
            columns = pl.ds(q_width + kind * kv_width, kv_width)
            summed = attn_recv[place * copies, :, columns].astype(full)
            for copy in range(1, copies):
                summed = summed + attn_recv[place * copies + copy, :, columns].astype(full)
            grad_ref[:, pl.ds(place * kv_width, kv_width)] = summed
    scatter.finish()
    ff_swap.finish()
    attn_swap.finish()
    gain_swap.finish()
    for shift in range(1, groups):
        to_group(shift).wait_send()
        gain_to(shift).wait_send()


def attend_back(
    grad_branch, out_low, saved, tables, gains, prefix, normed, attn_low, hidden, grad_middle,
    attention_gain, swiglu_gain_grad, ff_share, gain_count, shape, number,
):
    pieces, groups, heads, kv_heads, ff_block = shape
    length, (rows, model) = grad_branch.shape[0], hidden.shape
    width = attn_low.shape[1]
    weight_rows = ff_share.shape[1]
    q_width, kv_width = heads * HD, kv_heads * HD
    struct, vmem = jax.ShapeDtypeStruct, pltpu.VMEM
    padded = -(-gain_count // 128) * 128
    return pl.pallas_call(
        functools.partial(attend_back_kernel, shape),
        out_shape=(
            struct((rows, model), low),
            struct((1, gain_count), full),
            struct((weight_rows, H * HD), low),
            struct((weight_rows, KV * HD), full),
            struct((weight_rows, KV * HD), full),
            struct((weight_rows, H), full),
            struct((weight_rows, pieces * groups * ff_block), low),
            struct((weight_rows, pieces * groups * ff_block), low),
        ),
        in_specs=[IN_VMEM] * 15 + [pl.BlockSpec(memory_space=pltpu.SMEM), ANY] + [IN_VMEM] * 6,
        out_specs=(IN_VMEM,) * 8,
        scratch_shapes=[
            vmem((q_width, length), full),
            vmem((HD, length), low),
            vmem((length, HD), low),
            vmem((q_width, length), full),
            vmem((length, kv_width), full),
            vmem((length, kv_width), full),
            vmem((width, length), low),
            vmem((length, width), low),
            vmem((rows, model), full),
            vmem(ff_share.shape, low),
            vmem((2, length, model // groups), low),
            DMA((2,)),
            vmem((groups, model // groups, width), low),
            vmem((groups, model // groups, width), low),
            vmem((pieces, weight_rows, width), low),
            vmem((pieces, weight_rows, width), low),
            vmem((1, 2 * model + 2 * HD), full),
            vmem((pieces, groups, 8, padded), full),
            vmem((pieces, groups, 8, padded), full),
            vmem((groups, 8, padded), full),
            vmem((groups, 8, padded), full),
        ]
        + swap_scratch(pieces) * 3
        + [DMA((groups,))] * 4
        + scatter_scratch(pieces, rows, model),
        compiler_params=pltpu.CompilerParams(
            collective_id=number, has_side_effects=True, vmem_limit_bytes=63 << 20
        ),
        name=f"attend_back_{number}",
    )(
        grad_branch, out_low, *saved, *tables, *gains, prefix, normed, attn_low, hidden, grad_middle,
        attention_gain, swiglu_gain_grad, ff_share,
    )


def feed_kernel(
    shape,
    normed_two,
    ff_low,
    down_low,
    og_all,
    n2_all,
    hidden_ff,
    grad_pre,
    grad_hidden,
    *gather_sems,
):
    pieces = shape[0]
    line = Line(pieces)
    rows, length = normed_two.shape[0], og_all.shape[0]
    own_width = down_low.shape[0]
    tile = own_width // 3 if own_width % 384 == 0 else 128
    greet(line.peers())
    gather = Gather(line, 2, rows, n2_all, gather_sems)
    gather.start(normed_two)
    n2_all[pl.ds(pl.multiple_of(line.me * rows, rows), rows), :] = normed_two[...]

    def backward(index, unused):
        across = pl.ds(pl.multiple_of(index * 256, 256), 256)
        grad_hidden[across, :] = product_nt(og_all[across, :], down_low[...])
        return unused

    lax.fori_loop(0, length // 256, backward, 0)

    def chip_rows(chip):
        across = pl.ds(pl.multiple_of(chip * 2 * rows, 2 * rows), 2 * rows)

        def step(index, unused):
            start = index * tile
            first, second = lanes(start, tile), lanes(own_width + start, tile)
            gate = product(n2_all[across, :], ff_low[:, first])
            up = product(n2_all[across, :], ff_low[:, second])
            grads = grad_hidden[across, first]
            sigmoid = jax.nn.sigmoid(gate)
            silu = gate * sigmoid
            hidden_ff[across, first] = (silu * up).astype(low)
            grad_pre[across, first] = (
                grads * up * (sigmoid * (1.0 + gate * (1.0 - sigmoid)))
            ).astype(low)
            grad_pre[across, second] = (grads * silu).astype(low)
            return unused

        lax.fori_loop(0, own_width // tile, step, 0)

    def compute(far):
        gather.arrive(far)
        if far == 0:
            chip_rows(line.chip)
            return

        @pl.when(line.chip - far >= 0)
        def _():
            chip_rows(line.chip - far)

        @pl.when(line.chip + far < line.chips)
        def _():
            chip_rows(line.chip + far)

    for hop in range(1, line.chips - 1):
        gather.forward(hop)
        compute(hop - 1)
    if line.chips > 1:
        compute(line.chips - 2)
        gather.forward(line.chips - 1)
    compute(line.chips - 1)
    gather.finish()


def feed(normed_two, ff_low, down_low, og_all, shape, number):
    pieces = shape[0]
    length, model = og_all.shape
    own_width = down_low.shape[0]
    struct = jax.ShapeDtypeStruct
    return pl.pallas_call(
        functools.partial(feed_kernel, shape),
        out_shape=(
            struct((length, model), low),
            struct((length, own_width), low),
            struct((length, 2 * own_width), low),
        ),
        in_specs=[IN_VMEM] * 4,
        out_specs=(IN_VMEM,) * 3,
        scratch_shapes=[pltpu.VMEM((length, own_width), full)] + gather_scratch(pieces, 2),
        compiler_params=pltpu.CompilerParams(
            collective_id=number, has_side_effects=True, vmem_limit_bytes=60 << 20
        ),
        name=f"feed_{number}",
    )(normed_two, ff_low, down_low, og_all)


def feed_back_kernel(
    shape,
    grad_pre,
    ff_low,
    hidden_ff,
    down_low,
    og_all,
    n2_all,
    middle,
    out_grad,
    swiglu_gain,
    gb_all,
    grad_middle,
    gain_grad,
    hidden_out,
    ff_share,
    down_term,
    total_ref,
    branch,
    n2_part,
    term,
    term_in,
    part_sem,
    own_sem,
    ts_s,
    ts_r,
    *sems,
):
    pieces, groups = shape[:2]
    buffers, sems = sems[:2], sems[2:]
    gather_sems, sems = sems[:6], sems[6:]
    line = Line(pieces)
    me, group = line.me, lax.axis_index("seq")
    length, rows, model = og_all.shape[0], middle.shape[0], og_all.shape[1]
    weight_rows = ff_share.shape[1]
    greet(line.peers() + others("seq", groups))
    half = len(sems) // 2
    inner = Scatter(line, rows, buffers + sems[:half])
    outer = Scatter(line, rows, buffers + sems[half:])
    block = blocks_nt(grad_pre, ff_low, rows)
    last = line.chips - 1

    def fills(scatter, far, block):
        for distance, side in scatter.order():
            if distance == far:
                scatter.fill(far, side, block)

    def pushes(scatter, far):
        for distance, side in scatter.order():
            if distance == far and far > 0:
                scatter.push(far, side)

    share = model // groups

    def to_group(shift):
        peer = lax.rem(group + shift, groups)
        return remote(
            term.at[peer], term_in.at[shift - 1], ts_s.at[shift], ts_r.at[shift], "seq", peer
        )

    shifts = list(range(1, groups)) + [0]

    def load(job):
        index = lax.rem(group + shifts[job], groups)
        return pltpu.make_async_copy(
            n2_all.at[:, lanes(index * share, share)], n2_part.at[job % 2], part_sem.at[job % 2]
        )

    def ff_grad(job, index):
        load(job).wait()
        if job + 1 < groups:
            load(job + 1).start()

        def step(tile, unused):
            value = product_tn(n2_part[job % 2, :, lanes(tile * 128, 128)], grad_pre[...])
            term[index, pl.ds(pl.multiple_of(tile * 128, 128), 128), :] = value.astype(low)
            return unused

        lax.fori_loop(0, share // 128, step, 0)

    jobs = list(range(groups))

    def some_grads(count):
        for _ in range(min(count, len(jobs))):
            job = jobs.pop(0)
            shift = shifts[job]
            ff_grad(job, lax.rem(group + shift, groups))
            if shift:
                to_group(shift).start()

    load(0).start()
    fills(inner, last, block)
    pushes(inner, last)
    fills(inner, last - 1, block)
    some_grads(1)
    each = -(-(groups - 1) // max(1, last - 1))
    for hop in range(1, line.chips):
        pushes(inner, last - hop)
        if hop < last:
            fills(inner, last - 1 - hop, block)
        some_grads(each)
    some_grads(groups)

    def down_grad(index, unused):
        across = pl.ds(pl.multiple_of(index * 128, 128), 128)
        down_term[across, :] = product_tn(hidden_ff[:, lanes(index * 128, 128)], og_all[...]).astype(
            low
        )
        return unused

    lax.fori_loop(0, down_low.shape[0] // 128, down_grad, 0)
    inner.total(total_ref)
    inner.finish()
    values, grads = middle[...], total_ref[...]
    inverse = lax.rsqrt(jnp.mean(values * values, axis=-1, keepdims=True) + epsilon)
    gain_grad[...] = jnp.sum(grads * values * inverse, axis=0, keepdims=True)
    scaled = grads * swiglu_gain[...]
    result = (
        out_grad[...].astype(full)
        + inverse * scaled
        - values
        * (inverse * inverse * inverse * jnp.mean(scaled * values, axis=-1, keepdims=True))
    )
    grad_middle[...] = result
    branch[...] = result.astype(low)

    gather = Gather(line, 2, rows, gb_all, gather_sems)
    gather.start(branch)
    start = pl.multiple_of(me * rows, rows)
    own = pltpu.make_async_copy(branch, gb_all.at[pl.ds(start, rows)], own_sem)
    own.start()
    block = blocks_nn(hidden_ff, down_low, rows)
    fills(outer, last, block)
    pushes(outer, last)
    fills(outer, last - 1, block)
    for hop in range(1, line.chips):
        gather.forward(hop)
        pushes(outer, last - hop)
        if hop < last:
            fills(outer, last - 1 - hop, block)
    for shift in range(1, groups):
        peer = lax.rem(group + groups - shift, groups)
        remote(
            term.at[peer], term_in.at[shift - 1], ts_s.at[shift], ts_r.at[shift], "seq", peer
        ).wait_recv()
    for piece in range(pieces):
        across = pl.ds(piece * weight_rows, weight_rows)
        summed = term[group, across, :].astype(full)
        for shift in range(1, groups):
            summed = summed + term_in[shift - 1, across, :].astype(full)
        ff_share[piece] = summed.astype(low)
    outer.total(total_ref)
    hidden_out[...] = (middle[...] + total_ref[...]).astype(low)
    own.wait()
    for hop in range(line.chips):
        gather.arrive(hop)
    gather.finish()
    outer.finish()
    for shift in range(1, groups):
        to_group(shift).wait_send()


def feed_back(
    grad_pre, ff_low, hidden_ff, down_low, og_all, n2_all, middle, out_grad, swiglu_gain, shape, number
):
    pieces, groups = shape[:2]
    length, (rows, model) = og_all.shape[0], middle.shape
    own_width, width = hidden_ff.shape[1], grad_pre.shape[1]
    weight_rows = model // (groups * pieces)
    struct, vmem = jax.ShapeDtypeStruct, pltpu.VMEM
    scatter = scatter_scratch(pieces, rows, model)
    return pl.pallas_call(
        functools.partial(feed_back_kernel, shape),
        out_shape=(
            struct((length, model), low),
            struct((rows, model), full),
            struct((1, model), full),
            struct((rows, model), low),
            struct((pieces, weight_rows, width), low),
            struct((own_width, model), low),
        ),
        in_specs=[IN_VMEM] * 5 + [ANY] + [IN_VMEM] * 3,
        out_specs=(ANY,) + (IN_VMEM,) * 5,
        scratch_shapes=[
            vmem((rows, model), full),
            vmem((rows, model), low),
            vmem((2, length, model // groups), low),
            vmem((groups, model // groups, width), low),
            vmem((groups - 1, model // groups, width), low),
            DMA((2,)),
            DMA,
            DMA((groups,)),
            DMA((groups,)),
        ]
        + scatter[:2]
        + gather_scratch(pieces, 2)
        + scatter[2:] * 2,
        compiler_params=pltpu.CompilerParams(
            collective_id=number, has_side_effects=True, vmem_limit_bytes=63 << 20
        ),
        name=f"feed_back_{number}",
    )(grad_pre, ff_low, hidden_ff, down_low, og_all, n2_all, middle, out_grad, swiglu_gain)


def gather_seq(block):
    return lax.all_gather(block, "seq", axis=0, tiled=True)


def scatter_seq(block):
    return lax.psum_scatter(block.astype(low), "seq", scatter_dimension=0, tiled=True)


def on_device(
    hidden_in,
    out_grad,
    prefix_len,
    norm_gains,
    query_weight,
    key_weight,
    value_weight,
    head_gate_weight,
    out_weight,
    gate_weight,
    up_weight,
    down_weight,
):
    row_count, model = hidden_in.shape
    groups = lax.axis_size("seq")
    pieces = lax.axis_size("ctx")
    length = row_count * pieces
    weight_rows = query_weight.shape[0]
    heads = H // pieces
    kv_heads = max(1, KV // pieces)
    copies = max(1, pieces // KV)
    ff_block = down_weight.shape[0]
    ff_own = ff_block * groups
    q_width, kv_width = heads * HD, kv_heads * HD
    gain_count = norm_gains.shape[0]
    attn_width = q_width + 2 * kv_width + HD
    shape = (pieces, groups, heads, kv_heads, ff_block)

    def kv_columns(weight):
        columns = weight.astype(low).reshape(weight_rows, KV, HD)
        return jnp.repeat(columns, copies, axis=1).reshape(weight_rows, pieces, kv_width)

    attn_blocks = jnp.concatenate(
        [
            query_weight.astype(low).reshape(weight_rows, pieces, q_width),
            kv_columns(key_weight),
            kv_columns(value_weight),
            head_gate_weight.astype(low).reshape(weight_rows, pieces, heads),
            jnp.zeros((weight_rows, pieces, HD - heads), low),
        ],
        axis=-1,
    ).transpose(1, 0, 2)
    normed, attn_low, gains_full = opening(hidden_in, norm_gains, attn_blocks, 0)
    attn_low = attn_low.reshape(model, attn_width)
    down_low = gather_seq(down_weight.astype(low))
    spread = [(i, (i % groups) * pieces + i // groups) for i in range(groups * pieces)]
    collect = [(target, source) for source, target in spread]
    out_low = gather_seq(lax.ppermute(out_weight.astype(low), ("seq", "ctx"), spread))
    attention_gain = gains_full[:, :model]
    swiglu_gain = gains_full[:, model : 2 * model]
    head_gains = (
        gains_full[0, 2 * model : 2 * model + HD, None],
        gains_full[0, 2 * model + HD :, None],
    )
    inverse = rope_base ** (-jnp.arange(HD // 2, dtype=full) * 2.0 / HD)
    angles = inverse[:, None] * jnp.arange(length, dtype=jnp.int32).astype(full)[None, :]
    tables = (jnp.cos(angles), jnp.sin(angles))
    prefix = prefix_len.reshape(1, 1)

    raw = product(normed, attn_low)
    *saved, gated_t, middle, normed_two, out_grad_all, ff_low = attend(
        raw,
        tables,
        head_gains,
        prefix,
        out_low,
        hidden_in,
        swiglu_gain,
        out_grad,
        (gate_weight, up_weight),
        shape,
        1,
    )
    ff_low = ff_low.reshape(model, 2 * ff_own)
    n2_all, hidden_ff, grad_pre = feed(normed_two, ff_low, down_low, out_grad_all, shape, 2)
    grad_branch, grad_middle, swiglu_gain_grad, hidden_out, ff_share, down_term = feed_back(
        grad_pre, ff_low, hidden_ff, down_low, out_grad_all, n2_all, middle, out_grad, swiglu_gain, shape, 3
    )
    down_share = scatter_seq(down_term).astype(full)
    output_share = lax.ppermute(
        scatter_seq(product(gated_t, grad_branch)), ("seq", "ctx"), collect
    ).astype(full)
    hidden_grad, gains_share, query_share, key_share, value_share, head_share, gate_share, up_share = (
        attend_back(
            grad_branch,
            out_low,
            saved,
            tables,
            head_gains,
            prefix,
            normed,
            attn_low,
            hidden_in,
            grad_middle,
            attention_gain,
            swiglu_gain_grad,
            ff_share,
            gain_count,
            shape,
            4,
        )
    )
    return (
        hidden_out,
        hidden_grad,
        gains_share.reshape(gain_count),
        query_share.astype(full),
        key_share,
        value_share,
        head_share,
        output_share,
        gate_share.astype(full),
        up_share.astype(full),
        down_share,
    )


def solution(mesh):
    rows = P(("seq", "ctx"), None)
    return jax.shard_map(
        on_device,
        mesh=mesh,
        in_specs=(rows, rows, P("seq"), P(("seq", "ctx"))) + (rows,) * 8,
        out_specs=(rows, rows, P(("seq", "ctx"))) + (rows,) * 8,
        check_vma=False,
    )
```

time: 720 us -> 529 us (0.73)
  matrix products: 108 us -> 12.8 us
  Pallas kernels: 453 us -> 410 us
  local copies, waits for them, and re-layouts: 38 us -> 10.5 us
  other arithmetic: 39.4 us -> 14.2 us
    dot_general x14 -> x0, matrix products: 78.9 us -> none  [the longest x4 31.1 us: product_tn(): lax.dot_general(left_side, right_side, (((0,), (0,)), ((), ())), preferre...]
    pallas_call x10 -> x4, Pallas kernels: 385 us -> 347 us  [the longest x1 99.4 us: feed_back(): pl.pallas_call(functools.partial(feed_back_kernel, shape), out_shape=(str...]
    dot_general x4 -> x2, matrix products: 29 us -> 12.8 us  [product(): return jnp.dot(left_side, right_side, preferred_element_type=full)]
    reduce_scatter x4 -> x2, waiting for transfers between devices: 20.3 us -> 32.1 us  [scatter_seq(): lax.psum_scatter(block.astype(low), 'seq', scatter_dimension=0, tiled=True)]
    ppermute x1, waiting for transfers between devices: 11.3 us -> 0.01 us  [on_device(): lax.ppermute(scatter_seq(product(gated_t, grad_branch)), ('seq', 'ctx'),...]
    reshape x7 -> x0, local copies, waits for them, and re-layouts: 10.7 us -> none  [the longest x1 4.97 us: on_device(): attn_low = attn_low.reshape(model, attn_width)]
    reduce_sum x10 -> x0, other arithmetic: 9.36 us -> none  [the longest x2 2.39 us: rms_scale(): return values * inverse * gain_vector]
    convert_element_type x12 -> x6, other arithmetic: 17.4 us -> 8.73 us  [the longest x1 2.5 us: on_device(): down_share = scatter_seq(down_term).astype(full)]
  transfers between devices with their start and end apart: 9 -> 6, of which waited for: 3 -> 2; matrix products, arithmetic and copies ran while one was open for 15% -> 5% of each run, Pallas kernels for 47% -> 50%
where the time goes in v3:
time: 529 us; the launch traced here: 519 us
  Pallas kernels  410 us (78%)
  waiting for transfers between devices  46.3 us (9%)
  between operations  14.8 us (3%)
  other arithmetic  14.2 us (3%)
  matrix products  12.8 us (2%)
  local copies, waits for them, and re-layouts  10.5 us (2%)
  starting transfers between devices  9.57 us (2%)
    pallas_call x1, Pallas kernels, feed_back(): pl.pallas_call(functools.partial(feed_back_kernel, shape), out_shape=(str...  99.4 us
    pallas_call x1, Pallas kernels, attend_back(): pl.pallas_call(functools.partial(attend_back_kernel, shape), out_shape=(s...  99.1 us
    pallas_call x1, Pallas kernels, attend(): pl.pallas_call(functools.partial(attend_kernel, shape), out_shape=(struct...  98.9 us
    pallas_call x1, Pallas kernels, opening(): pl.pallas_call(functools.partial(opening_kernel, pieces, groups, parts),...  63.8 us
    pallas_call x1, Pallas kernels, feed(): pl.pallas_call(functools.partial(feed_kernel, shape), out_shape=(struct((...  49.3 us
    reduce_scatter x2, waiting for transfers between devices, scatter_seq(): lax.psum_scatter(block.astype(low), 'seq', scatter_dimension=0, tiled=True)  32.1 us
    ppermute x1, waiting for transfers between devices, on_device(): lax.ppermute(out_weight.astype(low), ('seq', 'ctx'), spread)  13.5 us
    dot_general x2, matrix products, product(): return jnp.dot(left_side, right_side, preferred_element_type=full)  12.8 us
  transfers between devices with their start and end apart: 6, of which 2 were waited for; matrix products, arithmetic and copies ran while one was open for 5% of the time, Pallas kernels for 50%

profile of v3, /device:TPU:1, one launch (start us, length us, event | category | flops | bytes accessed | tf_op | source)
XLA Modules:
  0.0 518.5 jit_solution(2663718095587902103)
XLA Ops:
  7.2 1.1 convert_element_type.54
  8.4 4.6 collective-permute-start
  13.0 13.5 %collective-permute-done = bf16[64,2048]{1,0:T(8,128)(2,1)S(1)} collective-permute-done((bf16[64,2048]{1,0:T(8,128)(2,1)S(1)}, bf16[64,2048]{1,0:T(8,128)(2,1)S(1)}, u32[]{:S(2)}, u32[]{:S(2)}) %collective-permute-start) | collective-permute-done | bytes 262176 | tf_op jit(solution)/shard_map/ppermute | solution.py:1635
  27.4 2.4 convert_element_type.55
  30.8 1.0 concatenate.3
  31.9 63.8 %opening_0.1 = (bf16[1024,2048]{1,0:T(8,128)(2,1)}, bf16[4,8,64,640]{3,2,1,0:T(8,128)(2,1)}, f32[1,4352]{1,0:T(1,128)}) custom-call(bf16[128,2048]{1,0:T(8,128)(2,1)} %hidden.3, f32[1,136]{1,0:T(1,128)} %bitcast.40, bf16[8,64,640]{2,1,0:T(8,128)(2,1)} %bitcast.35), custom_call_target="tpu_custom_call" | custom-call | tf_op jit(solution)/shard_map/opening_0/pallas_call | solution.py:525
  97.8 1.8 multiply_sine_fusion
  99.6 1.3 fusion
  100.9 8.4 %fusion.1.raw = f32[1024,640]{1,0:T(8,128)} fusion(bf16[1024,2048]{1,0:T(8,128)(2,1)} %get-tuple-element.45.normed, bf16[2048,640]{1,0:T(8,128)(2,1)} %bitcast.33), kind=kOutput, calls=%fused_computation.13 | convolution fusion | flops 2684354560 | bytes 9437184 | tf_op jit(solution)/shard_map/dot_general | solution.py:27
  109.3 98.9 %attend_1.1 = (f32[384,1024]{1,0:T(8,128)}, f32[8,1024]{1,0:T(8,128)}, bf16[1024,256]{1,0:T(8,128)(2,1)}, bf16[256,1024]{1,0:T(8,128)(2,1)}, bf16[1024,128]{1,0:...) custom-call(f32[1024,640]{1,0:T(8,128)} %fusion.1.raw, ...), custom_call_target="tpu_custom_call" | custom-call | tf_op jit(solution)/shard_map/attend_1/pallas_call | solution.py:873
  208.3 49.3 %feed_2.1 = (bf16[1024,2048]{1,0:T(8,128)(2,1)}, bf16[1024,768]{1,0:T(8,128)(2,1)}, bf16[1024,1536]{1,0:T(8,128)(2,1)}) custom-call(bf16[128,2048]{1,0:T(8,128)(2,1)} %get-tuple-element.48.normed_two, bf16[2048,1536]{1,0:T(8,128)(2,1)} %bitcast.31, bf16[768,2048]{1,0:T(8,128)(2,1)} %all-gather.5.cloned.1.call-done.down_low, ...), custom_call_target="tpu_custom_call" | custom-call | tf_op jit(solution)/shard_map/feed_2/pallas_call | solution.py:1358
  257.6 99.4 %feed_back_3.1 = (bf16[1024,2048]{1,0:T(8,128)(2,1)}, f32[128,2048]{1,0:T(8,128)}, f32[1,2048]{1,0:T(1,128)}, bf16[128,2048]{1,0:T(8,128)(2,1)}, bf16[8,64,1536]...) custom-call(bf16[1024,1536]{1,0:T(8,128)(2,1)} %get-tuple-element.51.grad_pre, bf16[2048,1536]{1,0:T(8,128)(2,1)} %bitcast.32, ...), custom_call_target="tpu_custom_call" | custom-call | tf_op jit(solution)/shard_map/feed_back_3/pallas_call | solution.py:1546
  357.0 4.4 convolution_convert_fusion
  362.0 32.1 %reduce-scatter.3.cloned.1.call-done = bf16[64,2048]{1,0:T(8,128)(2,1)} async-done(((bf16[256,2048]{1,0:T(8,128)(2,1)}), bf16[64,2048]{1,0:T(8,128)(2,1)}) %reduce-scatter.3.cloned.1.call-update) | async-done | bytes 262160 | tf_op jit(solution)/shard_map/reduce_scatter | solution.py:1584
  394.1 4.8 collective-permute-start.1
  398.9 99.1 %attend_back_4.1 = (bf16[128,2048]{1,0:T(8,128)(2,1)}, f32[1,136]{1,0:T(1,128)}, bf16[64,2048]{1,0:T(8,128)(2,1)}, f32[64,1024]{1,0:T(8,128)}, f32[64,1024]{1,0:...) custom-call(bf16[1024,2048]{1,0:T(8,128)(2,1)} %get-tuple-element.56.grad_branch, ...), custom_call_target="tpu_custom_call" | custom-call | tf_op jit(solution)/shard_map/attend_back_4/pallas_call | solution.py:1230
  498.0 1.5 copy.36
  499.5 1.8 convert_element_type.56
  501.2 2.4 convert_element_type.59
  503.6 1.2 convert_element_type.60
  504.9 0.8 convert_element_type.58
  505.7 2.5 convert_element_type.61
  508.2 0.8 copy.50
  509.0 0.8 copy.51
  (50 shorter events, 5.9 us)
Async XLA Ops:
  7.2 23.3 %copy-start.9 = (f32[64,16]{0,1:T(8,128)S(1)}, f32[64,16]{0,1:T(8,128)}, u32[]{:S(2)}) copy-start(f32[64,16]{0,1:T(8,128)} %param.19) | copy-start | bytes 12292
  7.2 23.5 %copy-start.1 = (f32[64,2048]{1,0:T(8,128)S(1)}, f32[64,2048]{1,0:T(8,128)}, u32[]{:S(2)}) copy-start(f32[64,2048]{1,0:T(8,128)} %param.16) | copy-start | bytes 1572868
  7.2 102.1 %all-gather.3.cloned.1.call-start = ((), (), s32[]{:S(2)}) async-start(), calls=%async_computation.2 | async-start | bytes 1310720 | tf_op jit(solution)/shard_map/all_gather | solution.py:1580
  8.4 22.4 %copy-start.4 = (f32[64,1024]{1,0:T(8,128)S(1)}, f32[64,1024]{1,0:T(8,128)}, u32[]{:S(2)}) copy-start(f32[64,1024]{1,0:T(8,128)} %param.17) | copy-start | bytes 786436
  8.4 22.4 %copy-start.5 = (f32[64,1024]{1,0:T(8,128)S(1)}, f32[64,1024]{1,0:T(8,128)}, u32[]{:S(2)}) copy-start(f32[64,1024]{1,0:T(8,128)} %param.18) | copy-start | bytes 786436
  8.4 18.2 %collective-permute-start = (bf16[64,2048]{1,0:T(8,128)(2,1)S(1)}, bf16[64,2048]{1,0:T(8,128)(2,1)S(1)}, u32[]{:S(2)}, u32[]{:S(2)}) collective-permute-start(bf16[64,2048]{1,0:T(8,128)(2,1)S(1)} %convert_element_type.54), channel_id=1, source_target_pairs={{0,0},{1,8},{2,16},{3,24},{4,1},{5,9},{6,17},{7,25},{8,2},{9,10},{... | collective-permute-start | bytes 786440 | tf_op jit(solution)/shard_map/ppermute | solution.py:1635
  26.6 0.7 copy-start.6
  27.3 181.0 %all-gather.5.cloned.1.call-start = ((), (), s32[]{:S(2)}) async-start(), calls=%async_computation.3 | async-start | bytes 3932160 | tf_op jit(solution)/shard_map/all_gather | solution.py:1580
  29.8 364.3 %reduce-scatter.3.cloned.1.call-start = ((), (), s32[]{:S(2)}) async-start(), calls=%async_computation.4 | async-start | bytes 1310720 | tf_op jit(solution)/shard_map/reduce_scatter | solution.py:1584
  257.6 99.4 %copy-start.11 = (bf16[256,1024]{1,0:T(8,128)(2,1)S(1)}, bf16[256,1024]{1,0:T(8,128)(2,1)}, u32[]{:S(2)}) copy-start(bf16[256,1024]{1,0:T(8,128)(2,1)} %get-tuple-element.75) | copy-start | bytes 1572868
  361.4 144.3 %reduce-scatter.5.cloned.1.call-start = ((), (), s32[]{:S(2)}) async-start(), calls=%async_computation.5 | async-start | bytes 3932160 | tf_op jit(solution)/shard_map/reduce_scatter | solution.py:1584
  394.1 110.8 %collective-permute-start.1 = (bf16[64,2048]{1,0:T(8,128)(2,1)}, bf16[64,2048]{1,0:T(8,128)(2,1)S(1)}, u32[]{:S(2)}, u32[]{:S(2)}) collective-permute-start(bf16[64,2048]{1,0:T(8,128)(2,1)} %reduce-scatter.3.cloned.1.call-done), channel_id=1, source_target_pairs={{0,0},{8,1},{16,2},{24,3},{1,4},{9,5},{17,6},{25,7},{2,8},{10,9},{... | collective-permute-start | bytes 786440 | tf_op jit(solution)/shard_map/ppermute | solution.py:1667
  498.0 5.7 %copy-start = (bf16[64,6144]{1,0:T(8,128)(2,1)S(1)}, bf16[64,6144]{1,0:T(8,128)(2,1)}, u32[]{:S(2)}) copy-start(bf16[64,6144]{1,0:T(8,128)(2,1)} %get-tuple-element.77) | copy-start | bytes 2359300
  503.6 4.6 copy-start.2
  504.9 4.1 copy-start.3
  504.9 4.9 copy-start.10
  504.9 5.5 %copy-start.8 = (f32[64,1024]{1,0:T(8,128)S(1)}, f32[64,1024]{1,0:T(8,128)}, u32[]{:S(2)}) copy-start(f32[64,1024]{1,0:T(8,128)} %get-tuple-element.124) | copy-start | bytes 786436
  505.7 5.4 %copy-start.7 = (f32[64,1024]{1,0:T(8,128)S(1)}, f32[64,1024]{1,0:T(8,128)}, u32[]{:S(2)}) copy-start(f32[64,1024]{1,0:T(8,128)} %get-tuple-element.125) | copy-start | bytes 786436
Sparse Core Ops, SparseCore 0:
  27.4 49.2 all-gather.2
  79.1 49.9 all-gather.4
  361.5 32.5 reduce-scatter.2
  397.2 62.9 reduce-scatter.4

commit v4 on v3

--- a/solution.py
+++ b/solution.py
@@ -1,4 +1,5 @@
 import functools
+import math
 
 import jax
 import jax.numpy as jnp
@@ -53,13 +54,15 @@
 def greet(peers):
     barrier = pltpu.get_barrier_semaphore()
     for axis, peer, exists in peers:
+        place = {"seq": peer[0], "ctx": peer[1]} if axis is None else {axis: peer}
+
+        def signal():
+            pl.semaphore_signal(barrier, inc=1, device_id=place, device_id_type=MESH)
+
         if exists is True:
-            pl.semaphore_signal(barrier, inc=1, device_id={axis: peer}, device_id_type=MESH)
+            signal()
         else:
-
-            @pl.when(exists)
-            def _():
-                pl.semaphore_signal(barrier, inc=1, device_id={axis: peer}, device_id_type=MESH)
+            pl.when(exists)(signal)
 
     arrivals = sum(1 for _, _, exists in peers if exists is True)
     for _, _, exists in peers:
@@ -387,174 +390,6 @@
     return block
 
 
-class Swap:
-    def __init__(self, pieces, send_of, recv_of, send_sem, recv_sem):
-        self.pieces, self.me = pieces, lax.axis_index("ctx")
-        self.send_of, self.recv_of = send_of, recv_of
-        self.send_sem, self.recv_sem = send_sem, recv_sem
-
-    def copy(self, shift):
-        peer = lax.rem(self.me + shift, self.pieces)
-        return remote(
-            self.send_of(peer),
-            self.recv_of(self.me),
-            self.send_sem.at[shift],
-            self.recv_sem.at[shift],
-            "ctx",
-            peer,
-        )
-
-    def start(self):
-        for shift in range(1, self.pieces):
-            self.copy(shift).start()
-
-    def wait_recv(self, shift):
-        source = lax.rem(self.me + self.pieces - shift, self.pieces)
-        remote(
-            self.send_of(source),
-            self.recv_of(source),
-            self.send_sem.at[shift],
-            self.recv_sem.at[shift],
-            "ctx",
-            source,
-        ).wait_recv()
-        return source
-
-    def finish(self):
-        for shift in range(1, self.pieces):
-            self.copy(shift).wait_send()
-
-
-def opening_kernel(
-    pieces,
-    groups,
-    parts,
-    hidden_ref,
-    gains_ref,
-    attn_ref,
-    normed_ref,
-    attn_out,
-    gains_out,
-    gains_row,
-    gains_all,
-    gain_vector,
-    normed,
-    own_sem,
-    own_attn,
-    ga_send,
-    ga_recv,
-    gs_send,
-    gs_recv,
-    at_send,
-    at_recv,
-    as_send,
-    as_recv,
-    *sems,
-):
-    line = Line(pieces)
-    me, group = line.me, lax.axis_index("seq")
-    greet(others("ctx", pieces) + others("seq", groups))
-    rows, model = hidden_ref.shape
-    gain_count = gains_ref.shape[1]
-    gains_row[...] = jnp.zeros(gains_row.shape, full)
-    gains_row[0:1, pl.ds(0, gain_count)] = gains_ref[...].astype(low).astype(full)
-    gains_all[group, me] = gains_row[...]
-    gain_swap = Swap(
-        pieces, lambda peer: gains_row, lambda peer: gains_all.at[group, peer], ga_send, ga_recv
-    )
-    gain_swap.start()
-    attn_swap = Swap(
-        pieces, lambda peer: attn_ref.at[peer], lambda peer: attn_out.at[group, peer], at_send, at_recv
-    )
-    attn_swap.start()
-    attn_own = pltpu.make_async_copy(attn_ref.at[me], attn_out.at[group, me], own_attn)
-    attn_own.start()
-    values = hidden_ref[...].astype(full)
-    inverse = lax.rsqrt(jnp.mean(values * values, axis=-1, keepdims=True) + epsilon)
-
-    def to_groups(ref, sends, receives, shift):
-        peer = lax.rem(group + shift, groups)
-        return remote(ref.at[group], ref.at[group], sends.at[shift], receives.at[shift], "seq", peer)
-
-    def from_groups(ref, sends, receives, shift):
-        peer = lax.rem(group + groups - shift, groups)
-        remote(
-            ref.at[peer], ref.at[peer], sends.at[shift], receives.at[shift], "seq", peer
-        ).wait_recv()
-
-    for shift in range(1, pieces):
-        gain_swap.wait_recv(shift)
-    for shift in range(1, groups):
-        to_groups(gains_all, gs_send, gs_recv, shift).start()
-    for shift in range(1, groups):
-        from_groups(gains_all, gs_send, gs_recv, shift)
-    for index in range(groups * pieces):
-        gain_vector[0:1, pl.ds(index * gain_count, gain_count)] = gains_all[
-            index // pieces, index % pieces, 0:1, pl.ds(0, gain_count)
-        ]
-    gains_out[...] = gain_vector[...]
-    normed[...] = (values * inverse * gain_vector[0:1, pl.ds(0, model)]).astype(low)
-    gather = Gather(line, parts, rows, normed_ref, sems)
-    gather.start(normed)
-    start = pl.multiple_of(me * rows, rows)
-    own = pltpu.make_async_copy(normed, normed_ref.at[pl.ds(start, rows)], own_sem)
-    own.start()
-    for shift in range(1, pieces):
-        attn_swap.wait_recv(shift)
-    attn_own.wait()
-    for shift in range(1, groups):
-        to_groups(attn_out, as_send, as_recv, shift).start()
-    for hop in range(1, line.chips):
-        gather.forward(hop)
-    own.wait()
-    gather.complete()
-    for shift in range(1, groups):
-        from_groups(attn_out, as_send, as_recv, shift)
-    gain_swap.finish()
-    attn_swap.finish()
-    for shift in range(1, groups):
-        to_groups(gains_all, gs_send, gs_recv, shift).wait_send()
-        to_groups(attn_out, as_send, as_recv, shift).wait_send()
-
-
-def opening(hidden_in, norm_gains, attn_blocks, number, parts=2):
-    pieces, groups = lax.axis_size("ctx"), lax.axis_size("seq")
-    rows, model = hidden_in.shape
-    gains = norm_gains.shape[0]
-    lanes = -(-gains // 128) * 128
-    return pl.pallas_call(
-        functools.partial(opening_kernel, pieces, groups, parts),
-        out_shape=(
-            jax.ShapeDtypeStruct((pieces * rows, model), low),
-            jax.ShapeDtypeStruct((groups,) + attn_blocks.shape, low),
-            jax.ShapeDtypeStruct((1, groups * pieces * gains), full),
-        ),
-        in_specs=[IN_VMEM, IN_VMEM, IN_VMEM],
-        out_specs=(ANY, ANY, IN_VMEM),
-        scratch_shapes=[
-            pltpu.VMEM((8, lanes), full),
-            pltpu.VMEM((groups, pieces, 8, lanes), full),
-            pltpu.VMEM((1, groups * pieces * gains), full),
-            pltpu.VMEM((rows, model), low),
-            DMA,
-            DMA,
-            DMA((pieces,)),
-            DMA((pieces,)),
-            DMA((groups,)),
-            DMA((groups,)),
-            DMA((pieces,)),
-            DMA((pieces,)),
-            DMA((groups,)),
-            DMA((groups,)),
-        ]
-        + gather_scratch(pieces, parts),
-        compiler_params=pltpu.CompilerParams(
-            collective_id=number, has_side_effects=True, vmem_limit_bytes=60 << 20
-        ),
-        name=f"opening_{number}",
-    )(hidden_in, norm_gains.reshape(1, gains), attn_blocks)
-
-
 class LineSwap:
     def __init__(self, line, send_of, recv_of, s_sem, r_sem):
         self.line, self.send_of, self.recv_of = line, send_of, recv_of
@@ -622,6 +457,18 @@
             else:
                 pl.when(comes)(wait)
 
+    def again(self, far, then):
+        line = self.line
+        for side, core, _, comes in self.legs(far):
+            if far == 0:
+                then(line.sibling)
+            else:
+                source = (line.chip + (-far if side == 0 else far)) * 2 + core
+
+                @pl.when(comes)
+                def _():
+                    then(source)
+
     def finish(self):
         for far in range(self.line.chips):
             for side, core, sends, _ in self.legs(far):
@@ -642,36 +489,394 @@
     def __init__(self, groups, place, s_sem, r_sem):
         self.groups, self.place, self.s_sem, self.r_sem = groups, place, s_sem, r_sem
         self.group = lax.axis_index("seq")
-
-    def copy(self, source, shift, origin=None):
-        peer = lax.rem(self.group + shift, self.groups)
+        self.square = groups == 4
+        self.across = self.group + 1 - 2 * lax.rem(self.group, 2)
+        self.along = lax.rem(self.group + 2, groups)
+        self.corner = groups - 1 - self.group
+
+    def copy(self, source, slot, peer, origin, target):
+        return remote(
+            origin, target, self.s_sem.at[source, slot], self.r_sem.at[source, slot], "seq", peer
+        )
+
+    def half(self, index, source, which):
+        ref = self.place(index, source)
+        rows = ref.shape[0] // 2
+        return ref.at[pl.ds(which * rows, rows)]
+
+    def first(self, source, origin=None):
         target = self.place(self.group, source)
-        return remote(
-            target if origin is None else origin,
-            target,
-            self.s_sem.at[source, shift],
-            self.r_sem.at[source, shift],
-            "seq",
-            peer,
-        )
+        origin = target if origin is None else origin
+        if self.square:
+            peers = [(1, self.across), (2, self.along)]
+        else:
+            peers = [
+                (shift, lax.rem(self.group + shift, self.groups)) for shift in range(1, self.groups)
+            ]
+        return [self.copy(source, slot, peer, origin, target) for slot, peer in peers]
+
+    def second(self, source):
+        one, two = self.half(self.across, source, 0), self.half(self.along, source, 1)
+        return [
+            self.copy(source, 3, self.along, one, one),
+            self.copy(source, 0, self.across, two, two),
+        ]
 
     def send(self, source, origin=None):
-        for shift in range(1, self.groups):
-            self.copy(source, shift, origin).start()
+        for copy in self.first(source, origin):
+            copy.start()
+
+    def relay(self, source):
+        if not self.square:
+            return
+        for slot, index, copy in zip((1, 2), (self.across, self.along), self.second(source)):
+            block = self.place(index, source)
+            self.copy(source, slot, index, block, block).wait_recv()
+            copy.start()
 
     def finish(self, sources):
         for source in range(sources):
-            for shift in range(1, self.groups):
-                peer = lax.rem(self.group + self.groups - shift, self.groups)
-                remote(
-                    self.place(peer, source),
-                    self.place(peer, source),
-                    self.s_sem.at[source, shift],
-                    self.r_sem.at[source, shift],
-                    "seq",
-                    peer,
-                ).wait_recv()
-                self.copy(source, shift).wait_send()
+            if self.square:
+                for slot, which in ((3, 0), (0, 1)):
+                    half = self.half(self.corner, source, which)
+                    self.copy(source, slot, self.corner, half, half).wait_recv()
+                for copy in self.second(source):
+                    copy.wait_send()
+            else:
+                for shift in range(1, self.groups):
+                    index = lax.rem(self.group + self.groups - shift, self.groups)
+                    block = self.place(index, source)
+                    self.copy(source, shift, index, block, block).wait_recv()
+            for copy in self.first(source):
+                copy.wait_send()
+
+
+class Fold:
+    def __init__(self, groups, term_ref, inbox, s_sem, r_sem):
+        self.groups, self.term, self.inbox = groups, term_ref, inbox
+        self.s_sem, self.r_sem = s_sem, r_sem
+        self.group = group = lax.axis_index("seq")
+        self.square = groups == 4
+        self.rows = term_ref.shape[1]
+        if self.square:
+            self.across = group + 1 - 2 * lax.rem(group, 2)
+            self.along = lax.rem(group + 2, groups)
+            self.order = [groups - 1 - group, self.across, self.along, group]
+        else:
+            self.order = [lax.rem(group + shift, groups) for shift in range(1, groups)] + [group]
+
+    def part(self, which):
+        return pl.ds(which * (self.rows // 2), self.rows // 2)
+
+    def copies(self, job):
+        index = self.order[job]
+        block = self.term.at[index]
+        if not self.square:
+            return [self.copy(job, block, self.inbox.at[job], index)]
+        if job == 0:
+            return [
+                self.copy(0, block.at[self.part(0)], self.inbox.at[0, self.part(0)], self.across),
+                self.copy(3, block.at[self.part(1)], self.inbox.at[0, self.part(1)], self.along),
+            ]
+        return [self.copy(job, block, self.inbox.at[job], index)]
+
+    def copy(self, slot, source, target, peer):
+        return remote(source, target, self.s_sem.at[slot], self.r_sem.at[slot], "seq", peer)
+
+    def ready(self, job):
+        if job < self.groups - 1 and (job == 0 or not self.square):
+            for copy in self.copies(job):
+                copy.start()
+
+    def mix(self):
+        if not self.square:
+            return
+        to_across, to_along = self.copies(0)
+        to_across.wait_recv()
+        mine, half = self.along, self.part(0)
+        self.term[mine, half, :] = (
+            self.term[mine, half, :].astype(full) + self.inbox[0, half, :].astype(full)
+        ).astype(low)
+        self.copies(2)[0].start()
+        to_along.wait_recv()
+        mine, half = self.across, self.part(1)
+        self.term[mine, half, :] = (
+            self.term[mine, half, :].astype(full) + self.inbox[0, half, :].astype(full)
+        ).astype(low)
+        self.copies(1)[0].start()
+
+    def arrive(self):
+        for job in range(1 if self.square else 0, self.groups - 1):
+            self.copies(job)[0].wait_recv()
+
+    def sum(self, across):
+        total = self.term[self.group, across, :].astype(full)
+        for job in range(1 if self.square else 0, self.groups - 1):
+            total = total + self.inbox[job, across, :].astype(full)
+        return total
+
+    def finish(self):
+        for job in range(self.groups - 1):
+            for copy in self.copies(job):
+                copy.wait_send()
+
+
+class Spread:
+    def __init__(self, groups, pieces):
+        group, me = lax.axis_index("seq"), lax.axis_index("ctx")
+        flat = group * pieces + me
+        self.use = (lax.rem(flat, groups), flat // groups)
+        held = me * groups + group
+        self.rest = (held // pieces, lax.rem(held, pieces))
+        self.moves = jnp.logical_or(self.use[0] != group, self.use[1] != me)
+
+    def peers(self):
+        return [(None, self.use, self.moves), (None, self.rest, self.moves)]
+
+    def copy(self, source, target, send, receive, back):
+        place = self.rest if back else self.use
+        return pltpu.make_async_remote_copy(
+            src_ref=source,
+            dst_ref=target,
+            send_sem=send,
+            recv_sem=receive,
+            device_id={"seq": place[0], "ctx": place[1]},
+            device_id_type=MESH,
+        )
+
+
+def opening_kernel(
+    shape,
+    parts,
+    hidden,
+    gains_ref,
+    query_weight,
+    key_weight,
+    value_weight,
+    gate_weight,
+    out_weight,
+    normed,
+    raw,
+    attn_low,
+    gains_out,
+    out_low,
+    hidden_all,
+    blocks,
+    out_block,
+    gains_row,
+    gains_all,
+    own_attn,
+    own_out,
+    out_s,
+    out_r,
+    ga_s,
+    ga_r,
+    gs_s,
+    gs_r,
+    at_s,
+    at_r,
+    as_s,
+    as_r,
+    os_s,
+    os_r,
+    *gather_sems,
+):
+    pieces, groups, heads, kv_heads, _ = shape
+    line = Line(pieces)
+    me, group = line.me, lax.axis_index("seq")
+    rows, model = hidden.shape
+    weight_rows = out_weight.shape[0]
+    q_width, kv_width = heads * HD, kv_heads * HD
+    copies = max(1, pieces // KV)
+    spread = Spread(groups, pieces)
+    greet(others("ctx", pieces) + others("seq", groups) + spread.peers())
+    gain_count = gains_ref.shape[1]
+    gains_row[...] = jnp.zeros(gains_row.shape, full)
+    gains_row[0:1, pl.ds(0, gain_count)] = gains_ref[...].astype(low).astype(full)
+    gains_all[group, me] = gains_row[...]
+    gain_swap = LineSwap(
+        line, lambda peer: gains_row, lambda source: gains_all.at[group, source], ga_s, ga_r
+    )
+    gain_swap.start()
+
+    blocks[:, :, pl.ds(q_width + 2 * kv_width, HD)] = jnp.zeros((pieces, weight_rows, HD), low)
+    for piece in range(pieces):
+        blocks[piece, :, pl.ds(0, q_width)] = query_weight[
+            :, pl.ds(piece * q_width, q_width)
+        ].astype(low)
+        start = piece // copies * kv_width
+        blocks[piece, :, pl.ds(q_width, kv_width)] = key_weight[:, pl.ds(start, kv_width)].astype(low)
+        blocks[piece, :, pl.ds(q_width + kv_width, kv_width)] = value_weight[
+            :, pl.ds(start, kv_width)
+        ].astype(low)
+        blocks[piece, :, pl.ds(q_width + 2 * kv_width, heads)] = gate_weight[
+            :, pl.ds(piece * heads, heads)
+        ].astype(low)
+
+    def place(index, source):
+        start = pl.multiple_of((index * pieces + source) * weight_rows, weight_rows)
+        return attn_low.at[pl.ds(start, weight_rows)]
+
+    attn_swap = LineSwap(
+        line, lambda peer: blocks.at[peer], lambda source: place(group, source), at_s, at_r
+    )
+    attn_swap.start()
+    share = Share(groups, place, as_s, as_r)
+    share.send(me, blocks.at[me])
+    attn_own = pltpu.make_async_copy(blocks.at[me], place(group, me), own_attn)
+    attn_own.start()
+    gather = Gather(line, parts, rows, hidden_all, gather_sems)
+    gather.start(hidden)
+    hidden_all[pl.ds(pl.multiple_of(me * rows, rows), rows), :] = hidden[...]
+    out_block[...] = out_weight[...].astype(low)
+
+    def out_place(index):
+        return out_low.at[pl.ds(pl.multiple_of(index * weight_rows, weight_rows), weight_rows)]
+
+    out_move = spread.copy(out_block, out_place(spread.use[0]), out_s, out_r, False)
+    out_stay = pltpu.make_async_copy(out_block, out_place(group), own_out)
+
+    @pl.when(spread.moves)
+    def _():
+        out_move.start()
+
+    @pl.when(jnp.logical_not(spread.moves))
+    def _():
+        out_stay.start()
+
+    def to_groups(shift):
+        peer = lax.rem(group + shift, groups)
+        return remote(
+            gains_all.at[group], gains_all.at[group], gs_s.at[shift], gs_r.at[shift], "seq", peer
+        )
+
+    def from_groups(shift):
+        peer = lax.rem(group + groups - shift, groups)
+        return remote(
+            gains_all.at[peer], gains_all.at[peer], gs_s.at[shift], gs_r.at[shift], "seq", peer
+        )
+
+    attn_swap.receive(0, share.send)
+    for far in range(line.chips):
+        gain_swap.receive(far, lambda source: None)
+    for shift in range(1, groups):
+        to_groups(shift).start()
+    if line.chips > 1:
+        attn_swap.receive(1, share.send)
+    for shift in range(1, groups):
+        from_groups(shift).wait_recv()
+    for index in range(groups * pieces):
+        gains_out[0:1, pl.ds(index * gain_count, gain_count)] = gains_all[
+            index // pieces, index % pieces, 0:1, pl.ds(0, gain_count)
+        ]
+
+    def chip_rows(chip):
+        return pl.ds(pl.multiple_of(chip * 2 * rows, 2 * rows), 2 * rows)
+
+    def both(far, body):
+        if far == 0:
+            body(chip_rows(line.chip))
+            return
+
+        @pl.when(line.chip - far >= 0)
+        def _():
+            body(chip_rows(line.chip - far))
+
+        @pl.when(line.chip + far < line.chips)
+        def _():
+            body(chip_rows(line.chip + far))
+
+    def normalise(across):
+        values = hidden_all[across, :].astype(full)
+        inverse = lax.rsqrt(jnp.mean(values * values, axis=-1, keepdims=True) + epsilon)
+        normed[across, :] = (values * inverse * gains_out[0:1, pl.ds(0, model)]).astype(low)
+
+    def project(across):
+        raw[across, :] = product(normed[across, :], attn_low[...])
+
+    share.relay(me)
+    attn_swap.again(0, share.relay)
+    for far in range(2, line.chips):
+        attn_swap.receive(far, share.send)
+        attn_swap.again(far - 1, share.relay)
+    out_share = Share(groups, lambda index, source: out_place(index), os_s, os_r)
+
+    @pl.when(spread.moves)
+    def _():
+        spread.copy(out_place(group), out_place(group), out_s, out_r, False).wait_recv()
+
+    @pl.when(jnp.logical_not(spread.moves))
+    def _():
+        out_stay.wait()
+
+    out_share.send(0)
+    if line.chips > 1:
+        attn_swap.again(line.chips - 1, share.relay)
+    for hop in range(1, line.chips - 1):
+        gather.forward(hop)
+        gather.arrive(hop - 1)
+        both(hop - 1, normalise)
+    gather.arrive(line.chips - 2)
+    both(line.chips - 2, normalise)
+    attn_own.wait()
+    out_share.relay(0)
+    share.finish(pieces)
+    for far in range(line.chips - 1):
+        both(far, project)
+    gather.forward(line.chips - 1)
+    gather.arrive(line.chips - 1)
+    both(line.chips - 1, normalise)
+    both(line.chips - 1, project)
+    out_share.finish(1)
+    gather.finish()
+    gain_swap.finish()
+    attn_swap.finish()
+    for shift in range(1, groups):
+        to_groups(shift).wait_send()
+
+    @pl.when(spread.moves)
+    def _():
+        out_move.wait_send()
+
+
+def opening(hidden, norm_gains, weights, shape, number, parts=2):
+    pieces, groups, heads, kv_heads, _ = shape
+    rows, model = hidden.shape
+    weight_rows = weights[0].shape[0]
+    gains = norm_gains.shape[0]
+    padded = -(-gains // 128) * 128
+    width = (heads + 2 * kv_heads + 1) * HD
+    struct, vmem = jax.ShapeDtypeStruct, pltpu.VMEM
+    return pl.pallas_call(
+        functools.partial(opening_kernel, shape, parts),
+        out_shape=(
+            struct((pieces * rows, model), low),
+            struct((pieces * rows, width), full),
+            struct((model, width), low),
+            struct((1, groups * pieces * gains), full),
+            struct((groups * weight_rows, model), low),
+        ),
+        in_specs=[IN_VMEM] * 7,
+        out_specs=(IN_VMEM,) * 5,
+        scratch_shapes=[
+            vmem((pieces * rows, model), low),
+            vmem((pieces, weight_rows, width), low),
+            vmem((weight_rows, model), low),
+            vmem((8, padded), full),
+            vmem((groups, pieces, 8, padded), full),
+        ]
+        + [DMA] * 4
+        + swap_scratch(pieces)
+        + [DMA((groups,))] * 2
+        + swap_scratch(pieces)
+        + [DMA((pieces, groups))] * 2
+        + [DMA((1, groups))] * 2
+        + gather_scratch(pieces, parts),
+        compiler_params=pltpu.CompilerParams(
+            collective_id=number, has_side_effects=True, vmem_limit_bytes=60 << 20
+        ),
+        name=f"opening_{number}",
+    )(hidden, norm_gains.reshape(1, gains), *weights)
 
 
 def lanes(start, size):
@@ -734,6 +939,7 @@
     out_grad,
     gate_weight,
     up_weight,
+    down_weight,
     raw_t,
     gate_t,
     q_ref,
@@ -748,15 +954,20 @@
     normed_two,
     og_all,
     ff_low,
+    down_low,
     vt_ref,
     gated,
     blocks,
+    down_block,
+    down_sem,
     own_sem,
     og_sem,
     swap_s,
     swap_r,
     share_s,
     share_r,
+    down_s,
+    down_r,
     *sems,
 ):
     pieces, groups, heads, kv_heads, ff_block = shape
@@ -781,6 +992,15 @@
     share.send(me, blocks.at[me])
     own = pltpu.make_async_copy(blocks.at[me], ff_low.at[group, me], own_sem)
     own.start()
+    down_block[...] = down_weight[...].astype(low)
+
+    def down_place(index, source):
+        start = pl.multiple_of(index * ff_block, ff_block)
+        return down_low.at[pl.ds(start, ff_block)]
+
+    down_share = Share(groups, down_place, down_s, down_r)
+    down_own = pltpu.make_async_copy(down_block, down_place(group, 0), down_sem)
+    down_own.start()
 
     prefix = prefix_ref[0, 0]
     scale = HD ** (-0.5)
@@ -825,7 +1045,10 @@
         gated_t[part, :] = scaled.astype(low)
         gated[:, part] = scaled.T.astype(low)
         if head == 0:
-            swap.receive(1, share.send)
+            share.relay(me)
+            swap.again(0, share.relay)
+            if line.chips > 1:
+                swap.receive(1, share.send)
 
     gather = Gather(line, 2, rows, og_all, gather_sems)
     scatter = Scatter(line, rows, scatter_refs)
@@ -846,11 +1069,17 @@
             scatter.fill(far, side, block)
     for far in range(2, line.chips):
         swap.receive(far, share.send)
+        swap.again(far - 1, share.relay)
+    down_share.send(0, down_block)
     for hop in range(1, line.chips):
         for far, side in scatter.order():
             if far == last - hop and far > 0:
                 scatter.push(far, side)
         gather.forward(hop)
+        if hop == 1:
+            swap.again(last, share.relay)
+        if hop == last:
+            down_share.relay(0)
     scatter.total(middle)
     values = hidden[...].astype(full) + middle[...]
     middle[...] = values
@@ -862,6 +1091,8 @@
     scatter.finish()
     swap.finish()
     share.finish(pieces)
+    down_own.wait()
+    down_share.finish(1)
 
 
 def attend(raw, tables, gains, prefix, out_low, hidden, swiglu_gain, out_grad, weights, shape, number):
@@ -887,18 +1118,22 @@
             struct((rows, model), low),
             struct((length, model), low),
             struct((groups, pieces, weight_rows, 2 * groups * ff_block), low),
+            struct((groups * ff_block, model), low),
         ),
-        in_specs=[IN_VMEM] * 5 + [pl.BlockSpec(memory_space=pltpu.SMEM)] + [IN_VMEM] * 6,
-        out_specs=(IN_VMEM,) * 12 + (ANY, ANY),
+        in_specs=[IN_VMEM] * 5 + [pl.BlockSpec(memory_space=pltpu.SMEM)] + [IN_VMEM] * 7,
+        out_specs=(IN_VMEM,) * 12 + (ANY, ANY, ANY),
         scratch_shapes=[
             pltpu.VMEM((kv_width, length), low),
             pltpu.VMEM((length, q_width), low),
             pltpu.VMEM((pieces, weight_rows, 2 * groups * ff_block), low),
+            pltpu.VMEM((ff_block, model), low),
+            DMA,
             DMA,
             DMA,
         ]
         + swap_scratch(pieces)
         + [DMA((pieces, groups))] * 2
+        + [DMA((1, groups))] * 2
         + gather_scratch(pieces, 2)
         + scatter_scratch(pieces, rows, model),
         compiler_params=pltpu.CompilerParams(
@@ -921,6 +1156,7 @@
     v_ref,
     att_t,
     lse_ref,
+    gated_t,
     cosine,
     sine,
     query_gain,
@@ -941,6 +1177,10 @@
     head_grad,
     gate_grad,
     up_grad,
+    out_grad,
+    out_term,
+    out_in,
+    out_send,
     gg_t,
     ga_t,
     ga,
@@ -972,6 +1212,10 @@
     ts_r,
     gs_s,
     gs_r,
+    ot_s,
+    ot_r,
+    om_s,
+    om_r,
     *scatter_refs,
 ):
     pieces, groups, heads, kv_heads, ff_block = shape
@@ -981,7 +1225,19 @@
     width, model = attn_low.shape[1], attn_low.shape[0]
     weight_rows = ff_share.shape[1]
     q_width, kv_width = heads * HD, kv_heads * HD
-    greet(others("ctx", pieces) + others("seq", groups))
+    spread = Spread(groups, pieces)
+    greet(others("ctx", pieces) + others("seq", groups) + spread.peers())
+    share = model // groups
+    fold = Fold(groups, term, term_in, ts_s, ts_r)
+    out_fold = Fold(groups, out_term, out_in, ot_s, ot_r)
+
+    def load(job):
+        index = fold.order[job]
+        return pltpu.make_async_copy(
+            normed.at[:, lanes(index * share, share)], normed_part.at[job % 2], part_sem.at[job % 2]
+        )
+
+    load(0).start()
     ff_swap = LineSwap(
         line, lambda peer: ff_share.at[peer], lambda source: ff_recv.at[source], ffs_s, ffs_r
     )
@@ -996,6 +1252,18 @@
         return unused
 
     lax.fori_loop(0, length // 256, branch, 0)
+
+    def out_grads(index, unused):
+        columns = lanes(index * 256, 256)
+        value = product(gated_t[...], grad_branch[:, columns]).astype(low)
+        for place in range(groups):
+            out_term[place, :, columns] = value[place * weight_rows : (place + 1) * weight_rows]
+        return unused
+
+    lax.fori_loop(0, model // 256, out_grads, 0)
+
+    for job in range(groups):
+        out_fold.ready(job)
     dk[...] = jnp.zeros(dk.shape, full)
     dv[...] = jnp.zeros(dv.shape, full)
     gate_rows = []
@@ -1028,6 +1296,8 @@
             dv[across, kv_part] += product(chance.astype(low), ga[columns, :])
 
         query_blocks(length, block)
+        if head == heads - 1:
+            out_fold.mix()
 
     gain_columns = [jnp.zeros((HD, 1), full), jnp.zeros((HD, 1), full)]
     for head in range(heads + kv_heads):
@@ -1066,54 +1336,93 @@
     scatter = Scatter(line, rows, scatter_refs)
     block = blocks_nt(grad, attn_low, rows)
     last = line.chips - 1
-    for far, side in scatter.order():
-        if far == last:
-            scatter.fill(far, side, block)
-    for far, side in scatter.order():
-        if far == last:
-            scatter.push(far, side)
-    for far, side in scatter.order():
-        if far == last - 1:
-            scatter.fill(far, side, block)
-
-    share = model // groups
-
-    def to_group(shift):
-        peer = lax.rem(group + shift, groups)
-        return remote(term.at[peer], term_in.at[shift], ts_s.at[shift], ts_r.at[shift], "seq", peer)
-
-    shifts = list(range(1, groups)) + [0]
-
-    def load(job):
-        index = lax.rem(group + shifts[job], groups)
-        return pltpu.make_async_copy(
-            normed.at[:, lanes(index * share, share)], normed_part.at[job % 2], part_sem.at[job % 2]
-        )
-
-    def weight_grad(job, index):
+
+    def fills(far):
+        for distance, side in scatter.order():
+            if distance == far:
+                scatter.fill(far, side, block)
+
+    def pushes(far):
+        for distance, side in scatter.order():
+            if distance == far and far > 0:
+                scatter.push(far, side)
+
+    def weight_grad(job):
+        index = fold.order[job]
         load(job).wait()
         if job + 1 < groups:
             load(job + 1).start()
 
         def step(tile, unused):
+            start = index * share + tile * 128
             value = product(grad_t[...], normed_part[job % 2, :, lanes(tile * 128, 128)])
-            term[index, pl.ds(pl.multiple_of(tile * 128, 128), 128), :] = value.T.astype(low)
+            turned = value.T
+            term[index, pl.ds(pl.multiple_of(tile * 128, 128), 128), :] = turned.astype(low)
+            weighted = jnp.sum(
+                turned * attn_low[pl.ds(pl.multiple_of(start, 128), 128), :].astype(full),
+                axis=1,
+                keepdims=True,
+            )
+            wide = jnp.broadcast_to(weighted, (128, 128)).T
+            gains_vector[:, lanes(start, 128)] = wide[0:1, :] / attention_gain[:, lanes(start, 128)]
             return unused
 
         lax.fori_loop(0, share // 128, step, 0)
-
-    load(0).start()
-    for job, shift in enumerate(shifts):
-        weight_grad(job, lax.rem(group + shift, groups))
-        if shift:
-            to_group(shift).start()
-    for far, side in scatter.order():
-        if far < last - 1:
-            scatter.fill(far, side, block)
-    for hop in range(1, line.chips):
-        for far, side in scatter.order():
-            if far == last - hop and far > 0:
-                scatter.push(far, side)
+        fold.ready(job)
+
+    weight_grad(0)
+    fills(last)
+    pushes(last)
+    for job in range(1, groups):
+        weight_grad(job)
+        if last - job >= 0:
+            fills(last - job)
+    fold.mix()
+    for far in range(last - groups, -1, -1):
+        fills(far)
+
+    gain_count = gains_grad.shape[1]
+    gains_vector[:, pl.ds(model, model)] = swiglu_gain_grad[...]
+    for kind in range(2):
+        wide = jnp.broadcast_to(gain_columns[kind], (HD, HD)).T
+        gains_vector[:, pl.ds(2 * model + kind * HD, HD)] = wide[0:1, :]
+    gain_give[...] = jnp.zeros(gain_give.shape, full)
+    for index in range(groups * pieces):
+        gain_give[index % pieces, index // pieces, 0:1, pl.ds(0, gain_count)] = gains_vector[
+            :, pl.ds(index * gain_count, gain_count)
+        ]
+    gain_swap = LineSwap(
+        line, lambda peer: gain_give.at[peer], lambda source: gain_sib.at[source], gc_s, gc_r
+    )
+    gain_swap.start()
+    gain_sib[me] = gain_give[me]
+    pushes(last - 1)
+
+    out_fold.arrive()
+    out_send[...] = out_fold.sum(pl.ds(0, weight_rows)).astype(low)
+    out_move = spread.copy(out_send, out_grad, om_s, om_r, True)
+
+    @pl.when(spread.moves)
+    def _():
+        out_move.start()
+
+    @pl.when(jnp.logical_not(spread.moves))
+    def _():
+        out_grad[...] = out_send[...]
+
+    for far in range(line.chips):
+        gain_swap.receive(far, lambda source: None)
+    gain_row[...] = jnp.sum(gain_sib[...], axis=0)
+
+    def gain_to(shift):
+        peer = lax.rem(group + shift, groups)
+        return remote(
+            gain_row.at[peer], gain_last.at[shift], gs_s.at[shift], gs_r.at[shift], "seq", peer
+        )
+
+    for shift in range(1, groups):
+        gain_to(shift).start()
+    gain_last[0] = gain_row[group]
 
     for far in range(line.chips):
         ff_swap.receive(far, lambda source: None)
@@ -1127,17 +1436,12 @@
                     piece, :, pl.ds(half * own_width + index * ff_block, ff_block)
                 ]
 
-    for shift in range(1, groups):
-        peer = lax.rem(group + groups - shift, groups)
-        remote(
-            term.at[peer], term_in.at[shift], ts_s.at[shift], ts_r.at[shift], "seq", peer
-        ).wait_recv()
+    for far in range(last - 2, 0, -1):
+        pushes(far)
+
+    fold.arrive()
     for piece in range(pieces):
-        across = pl.ds(piece * weight_rows, weight_rows)
-        summed = term[group, across, :].astype(full)
-        for shift in range(1, groups):
-            summed = summed + term_in[shift, across, :].astype(full)
-        attn_send[piece] = summed.astype(low)
+        attn_send[piece] = fold.sum(pl.ds(piece * weight_rows, weight_rows)).astype(low)
     attn_swap = LineSwap(
         line, lambda peer: attn_send.at[peer], lambda source: attn_recv.at[source], at_s, at_r
     )
@@ -1155,35 +1459,6 @@
         * (inverse * inverse * inverse * jnp.mean(scaled * values, axis=-1, keepdims=True))
     ).astype(low)
 
-    gain_count = gains_grad.shape[1]
-    gains_vector[:, pl.ds(0, model)] = jnp.sum(grads * values * inverse, axis=0, keepdims=True)
-    gains_vector[:, pl.ds(model, model)] = swiglu_gain_grad[...]
-    for kind in range(2):
-        wide = jnp.broadcast_to(gain_columns[kind], (HD, HD)).T
-        gains_vector[:, pl.ds(2 * model + kind * HD, HD)] = wide[0:1, :]
-    gain_give[...] = jnp.zeros(gain_give.shape, full)
-    for index in range(groups * pieces):
-        gain_give[index % pieces, index // pieces, 0:1, pl.ds(0, gain_count)] = gains_vector[
-            :, pl.ds(index * gain_count, gain_count)
-        ]
-    gain_swap = LineSwap(
-        line, lambda peer: gain_give.at[peer], lambda source: gain_sib.at[source], gc_s, gc_r
-    )
-    gain_swap.start()
-    gain_sib[me] = gain_give[me]
-    for far in range(line.chips):
-        gain_swap.receive(far, lambda source: None)
-    gain_row[...] = jnp.sum(gain_sib[...], axis=0)
-
-    def gain_to(shift):
-        peer = lax.rem(group + shift, groups)
-        return remote(
-            gain_row.at[peer], gain_last.at[shift], gs_s.at[shift], gs_r.at[shift], "seq", peer
-        )
-
-    for shift in range(1, groups):
-        gain_to(shift).start()
-    gain_last[0] = gain_row[group]
     for shift in range(1, groups):
         peer = lax.rem(group + groups - shift, groups)
         remote(
@@ -1207,17 +1482,24 @@
             for copy in range(1, copies):
                 summed = summed + attn_recv[place * copies + copy, :, columns].astype(full)
             grad_ref[:, pl.ds(place * kv_width, kv_width)] = summed
+
+    @pl.when(spread.moves)
+    def _():
+        spread.copy(out_grad, out_grad, om_s, om_r, True).wait_recv()
+        out_move.wait_send()
+
     scatter.finish()
     ff_swap.finish()
     attn_swap.finish()
     gain_swap.finish()
     for shift in range(1, groups):
-        to_group(shift).wait_send()
         gain_to(shift).wait_send()
+    fold.finish()
+    out_fold.finish()
 
 
 def attend_back(
-    grad_branch, out_low, saved, tables, gains, prefix, normed, attn_low, hidden, grad_middle,
+    grad_branch, out_low, saved, gated_t, tables, gains, prefix, normed, attn_low, hidden, grad_middle,
     attention_gain, swiglu_gain_grad, ff_share, gain_count, shape, number,
 ):
     pieces, groups, heads, kv_heads, ff_block = shape
@@ -1238,10 +1520,14 @@
             struct((weight_rows, H), full),
             struct((weight_rows, pieces * groups * ff_block), low),
             struct((weight_rows, pieces * groups * ff_block), low),
+            struct((weight_rows, model), low),
         ),
-        in_specs=[IN_VMEM] * 15 + [pl.BlockSpec(memory_space=pltpu.SMEM), ANY] + [IN_VMEM] * 6,
-        out_specs=(IN_VMEM,) * 8,
+        in_specs=[IN_VMEM] * 16 + [pl.BlockSpec(memory_space=pltpu.SMEM), ANY] + [IN_VMEM] * 6,
+        out_specs=(IN_VMEM,) * 9,
         scratch_shapes=[
+            vmem((groups, weight_rows, model), low),
+            vmem((groups - 1, weight_rows, model), low),
+            vmem((weight_rows, model), low),
             vmem((q_width, length), full),
             vmem((HD, length), low),
             vmem((length, HD), low),
@@ -1255,7 +1541,7 @@
             vmem((2, length, model // groups), low),
             DMA((2,)),
             vmem((groups, model // groups, width), low),
-            vmem((groups, model // groups, width), low),
+            vmem((groups - 1, model // groups, width), low),
             vmem((pieces, weight_rows, width), low),
             vmem((pieces, weight_rows, width), low),
             vmem((1, 2 * model + 2 * HD), full),
@@ -1265,14 +1551,15 @@
             vmem((groups, 8, padded), full),
         ]
         + swap_scratch(pieces) * 3
-        + [DMA((groups,))] * 4
+        + [DMA((groups,))] * 6
+        + [DMA] * 2
         + scatter_scratch(pieces, rows, model),
         compiler_params=pltpu.CompilerParams(
             collective_id=number, has_side_effects=True, vmem_limit_bytes=63 << 20
         ),
         name=f"attend_back_{number}",
     )(
-        grad_branch, out_low, *saved, *tables, *gains, prefix, normed, attn_low, hidden, grad_middle,
+        grad_branch, out_low, *saved, gated_t, *tables, *gains, prefix, normed, attn_low, hidden, grad_middle,
         attention_gain, swiglu_gain_grad, ff_share,
     )
 
@@ -1388,7 +1675,9 @@
     gain_grad,
     hidden_out,
     ff_share,
+    down_share,
     down_term,
+    down_in,
     total_ref,
     branch,
     n2_part,
@@ -1398,6 +1687,8 @@
     own_sem,
     ts_s,
     ts_r,
+    ds_s,
+    ds_r,
     *sems,
 ):
     pieces, groups = shape[:2]
@@ -1426,16 +1717,11 @@
 
     share = model // groups
 
-    def to_group(shift):
-        peer = lax.rem(group + shift, groups)
-        return remote(
-            term.at[peer], term_in.at[shift - 1], ts_s.at[shift], ts_r.at[shift], "seq", peer
-        )
-
-    shifts = list(range(1, groups)) + [0]
+    fold = Fold(groups, term, term_in, ts_s, ts_r)
+    down_fold = Fold(groups, down_term, down_in, ds_s, ds_r)
 
     def load(job):
-        index = lax.rem(group + shifts[job], groups)
+        index = fold.order[job]
         return pltpu.make_async_copy(
             n2_all.at[:, lanes(index * share, share)], n2_part.at[job % 2], part_sem.at[job % 2]
         )
@@ -1457,10 +1743,10 @@
     def some_grads(count):
         for _ in range(min(count, len(jobs))):
             job = jobs.pop(0)
-            shift = shifts[job]
-            ff_grad(job, lax.rem(group + shift, groups))
-            if shift:
-                to_group(shift).start()
+            ff_grad(job, fold.order[job])
+            fold.ready(job)
+            if not jobs:
+                fold.mix()
 
     load(0).start()
     fills(inner, last, block)
@@ -1475,14 +1761,21 @@
         some_grads(each)
     some_grads(groups)
 
-    def down_grad(index, unused):
-        across = pl.ds(pl.multiple_of(index * 128, 128), 128)
-        down_term[across, :] = product_tn(hidden_ff[:, lanes(index * 128, 128)], og_all[...]).astype(
-            low
-        )
+    down_rows = down_term.shape[1]
+    piece_rows = math.gcd(down_rows, 128)
+
+    def down_grads(index, unused):
+        value = product_tn(hidden_ff[:, lanes(index * 128, 128)], og_all[...]).astype(low)
+        for part in range(128 // piece_rows):
+            row = index * 128 + part * piece_rows
+            down_term[row // down_rows, pl.ds(pl.multiple_of(lax.rem(row, down_rows), piece_rows), piece_rows), :] = (
+                value[part * piece_rows : (part + 1) * piece_rows]
+            )
         return unused
 
-    lax.fori_loop(0, down_low.shape[0] // 128, down_grad, 0)
+    lax.fori_loop(0, down_low.shape[0] // 128, down_grads, 0)
+    for job in range(groups):
+        down_fold.ready(job)
     inner.total(total_ref)
     inner.finish()
     values, grads = middle[...], total_ref[...]
@@ -1512,17 +1805,13 @@
         pushes(outer, last - hop)
         if hop < last:
             fills(outer, last - 1 - hop, block)
-    for shift in range(1, groups):
-        peer = lax.rem(group + groups - shift, groups)
-        remote(
-            term.at[peer], term_in.at[shift - 1], ts_s.at[shift], ts_r.at[shift], "seq", peer
-        ).wait_recv()
+        if hop == 1:
+            down_fold.mix()
+    fold.arrive()
     for piece in range(pieces):
-        across = pl.ds(piece * weight_rows, weight_rows)
-        summed = term[group, across, :].astype(full)
-        for shift in range(1, groups):
-            summed = summed + term_in[shift - 1, across, :].astype(full)
-        ff_share[piece] = summed.astype(low)
+        ff_share[piece] = fold.sum(pl.ds(piece * weight_rows, weight_rows)).astype(low)
+    down_fold.arrive()
+    down_share[...] = down_fold.sum(pl.ds(0, down_rows)).astype(low)
     outer.total(total_ref)
     hidden_out[...] = (middle[...] + total_ref[...]).astype(low)
     own.wait()
@@ -1530,8 +1819,8 @@
         gather.arrive(hop)
     gather.finish()
     outer.finish()
-    for shift in range(1, groups):
-        to_group(shift).wait_send()
+    fold.finish()
+    down_fold.finish()
 
 
 def feed_back(
@@ -1551,11 +1840,13 @@
             struct((1, model), full),
             struct((rows, model), low),
             struct((pieces, weight_rows, width), low),
-            struct((own_width, model), low),
+            struct((own_width // groups, model), low),
         ),
         in_specs=[IN_VMEM] * 5 + [ANY] + [IN_VMEM] * 3,
         out_specs=(ANY,) + (IN_VMEM,) * 5,
         scratch_shapes=[
+            vmem((groups, own_width // groups, model), low),
+            vmem((groups - 1, own_width // groups, model), low),
             vmem((rows, model), full),
             vmem((rows, model), low),
             vmem((2, length, model // groups), low),
@@ -1563,6 +1854,8 @@
             vmem((groups - 1, model // groups, width), low),
             DMA((2,)),
             DMA,
+            DMA((groups,)),
+            DMA((groups,)),
             DMA((groups,)),
             DMA((groups,)),
         ]
@@ -1576,12 +1869,25 @@
     )(grad_pre, ff_low, hidden_ff, down_low, og_all, n2_all, middle, out_grad, swiglu_gain)
 
 
-def gather_seq(block):
-    return lax.all_gather(block, "seq", axis=0, tiled=True)
-
-
-def scatter_seq(block):
-    return lax.psum_scatter(block.astype(low), "seq", scatter_dimension=0, tiled=True)
+def widen_kernel(*refs):
+    for source, target in zip(refs[: len(refs) // 2], refs[len(refs) // 2 :]):
+        target[...] = source[...].astype(full)
+
+
+def widen(arrays):
+    steps = max(1, arrays[0].shape[0] // 16)
+    specs = [
+        pl.BlockSpec((array.shape[0] // steps, array.shape[1]), lambda step: (step, 0))
+        for array in arrays
+    ]
+    return pl.pallas_call(
+        widen_kernel,
+        grid=(steps,),
+        out_shape=[jax.ShapeDtypeStruct(array.shape, full) for array in arrays],
+        in_specs=specs,
+        out_specs=specs,
+        name="widen",
+    )(*arrays)
 
 
 def on_device(
@@ -1605,34 +1911,17 @@
     weight_rows = query_weight.shape[0]
     heads = H // pieces
     kv_heads = max(1, KV // pieces)
-    copies = max(1, pieces // KV)
     ff_block = down_weight.shape[0]
     ff_own = ff_block * groups
-    q_width, kv_width = heads * HD, kv_heads * HD
     gain_count = norm_gains.shape[0]
-    attn_width = q_width + 2 * kv_width + HD
     shape = (pieces, groups, heads, kv_heads, ff_block)
-
-    def kv_columns(weight):
-        columns = weight.astype(low).reshape(weight_rows, KV, HD)
-        return jnp.repeat(columns, copies, axis=1).reshape(weight_rows, pieces, kv_width)
-
-    attn_blocks = jnp.concatenate(
-        [
-            query_weight.astype(low).reshape(weight_rows, pieces, q_width),
-            kv_columns(key_weight),
-            kv_columns(value_weight),
-            head_gate_weight.astype(low).reshape(weight_rows, pieces, heads),
-            jnp.zeros((weight_rows, pieces, HD - heads), low),
-        ],
-        axis=-1,
-    ).transpose(1, 0, 2)
-    normed, attn_low, gains_full = opening(hidden_in, norm_gains, attn_blocks, 0)
-    attn_low = attn_low.reshape(model, attn_width)
-    down_low = gather_seq(down_weight.astype(low))
-    spread = [(i, (i % groups) * pieces + i // groups) for i in range(groups * pieces)]
-    collect = [(target, source) for source, target in spread]
-    out_low = gather_seq(lax.ppermute(out_weight.astype(low), ("seq", "ctx"), spread))
+    normed, raw, attn_low, gains_full, out_low = opening(
+        hidden_in,
+        norm_gains,
+        (query_weight, key_weight, value_weight, head_gate_weight, out_weight),
+        shape,
+        0,
+    )
     attention_gain = gains_full[:, :model]
     swiglu_gain = gains_full[:, model : 2 * model]
     head_gains = (
@@ -1644,8 +1933,7 @@
     tables = (jnp.cos(angles), jnp.sin(angles))
     prefix = prefix_len.reshape(1, 1)
 
-    raw = product(normed, attn_low)
-    *saved, gated_t, middle, normed_two, out_grad_all, ff_low = attend(
+    *saved, gated_t, middle, normed_two, out_grad_all, ff_low, down_low = attend(
         raw,
         tables,
         head_gains,
@@ -1654,24 +1942,21 @@
         hidden_in,
         swiglu_gain,
         out_grad,
-        (gate_weight, up_weight),
+        (gate_weight, up_weight, down_weight),
         shape,
         1,
     )
     ff_low = ff_low.reshape(model, 2 * ff_own)
     n2_all, hidden_ff, grad_pre = feed(normed_two, ff_low, down_low, out_grad_all, shape, 2)
-    grad_branch, grad_middle, swiglu_gain_grad, hidden_out, ff_share, down_term = feed_back(
+    grad_branch, grad_middle, swiglu_gain_grad, hidden_out, ff_share, down_share = feed_back(
         grad_pre, ff_low, hidden_ff, down_low, out_grad_all, n2_all, middle, out_grad, swiglu_gain, shape, 3
     )
-    down_share = scatter_seq(down_term).astype(full)
-    output_share = lax.ppermute(
-        scatter_seq(product(gated_t, grad_branch)), ("seq", "ctx"), collect
-    ).astype(full)
-    hidden_grad, gains_share, query_share, key_share, value_share, head_share, gate_share, up_share = (
+    hidden_grad, gains_share, query_share, key_share, value_share, head_share, gate_share, up_share, output_share = (
         attend_back(
             grad_branch,
             out_low,
             saved,
+            gated_t,
             tables,
             head_gains,
             prefix,
@@ -1687,17 +1972,20 @@
             4,
         )
     )
+    query_share, output_share, gate_share, up_share, down_share = widen(
+        (query_share, output_share, gate_share, up_share, down_share)
+    )
     return (
         hidden_out,
         hidden_grad,
         gains_share.reshape(gain_count),
-        query_share.astype(full),
+        query_share,
         key_share,
         value_share,
         head_share,
         output_share,
-        gate_share.astype(full),
-        up_share.astype(full),
+        gate_share,
+        up_share,
         down_share,
     )
 

time: 529 us -> 465 us (0.88)
  waiting for transfers between devices: 46.3 us -> 0 us
  Pallas kernels: 410 us -> 444 us
  between operations: 14.8 us -> 1.82 us
  matrix products: 12.8 us -> 0 us
  other arithmetic: 14.2 us -> 1.8 us
  starting transfers between devices: 9.57 us -> 0 us
    reduce_scatter x2 -> x0, waiting for transfers between devices: 32.1 us -> none  [scatter_seq(): lax.psum_scatter(block.astype(low), 'seq', scatter_dimension=0, tiled=True)]
    pallas_call x1 -> x2, Pallas kernels: 63.8 us -> 83 us  [the longest x1 78.1 us: opening(): pl.pallas_call(functools.partial(opening_kernel, shape, parts), out_shape...]
    ppermute x2 -> x0, waiting for transfers between devices: 13.5 us -> none  [the longest x1 13.5 us: on_device(): lax.ppermute(out_weight.astype(low), ('seq', 'ctx'), spread)]
    dot_general x2 -> x0, matrix products: 12.8 us -> none  [product(): return jnp.dot(left_side, right_side, preferred_element_type=full)]
    convert_element_type x9 -> x0, other arithmetic: 12.3 us -> none  [the longest x1 2.5 us: on_device(): down_share = scatter_seq(down_term).astype(full)]
    pallas_call x1, Pallas kernels: 98.9 us -> 108 us  [attend(): pl.pallas_call(functools.partial(attend_kernel, shape), out_shape=(struct...]
    ppermute x2 -> x0, starting transfers between devices: 9.41 us -> none  [the longest x1 4.77 us: on_device(): lax.ppermute(scatter_seq(product(gated_t, grad_branch)), ('seq', 'ctx'),...]
  transfers between devices with their start and end apart: 6 -> 0, of which waited for: 2 -> 0; matrix products, arithmetic and copies ran while one was open for 5% -> 0% of each run, Pallas kernels for 50% -> 0%
where the time goes in v4:
time: 465 us; the launch traced here: 458 us
  Pallas kernels  444 us (95%)
  local copies, waits for them, and re-layouts  9.97 us (2%)
    pallas_call x1, Pallas kernels, attend(): pl.pallas_call(functools.partial(attend_kernel, shape), out_shape=(struct...  108 us
    pallas_call x1, Pallas kernels, feed_back(): pl.pallas_call(functools.partial(feed_back_kernel, shape), out_shape=(str...  103 us
    pallas_call x1, Pallas kernels, attend_back(): pl.pallas_call(functools.partial(attend_back_kernel, shape), out_shape=(s...  99.9 us
    pallas_call x1, Pallas kernels, opening(): pl.pallas_call(functools.partial(opening_kernel, shape, parts), out_shape...  78.1 us
    pallas_call x1, Pallas kernels, feed(): pl.pallas_call(functools.partial(feed_kernel, shape), out_shape=(struct((...  49.3 us

profile of v4, /device:TPU:1, one launch (start us, length us, event | category | flops | bytes accessed | tf_op | source)
XLA Modules:
  0.0 457.5 jit_solution(17261766412496438026)
XLA Ops:
  1.3 1.4 copy.23.gate_weight
  2.7 1.8 multiply_sine_fusion
  4.5 78.1 %opening_0.1 = (bf16[1024,2048]{1,0:T(8,128)(2,1)}, f32[1024,640]{1,0:T(8,128)}, bf16[2048,640]{1,0:T(8,128)(2,1)}, f32[1,4352]{1,0:T(1,128)}, bf16[256,2048]{1,0:T(8,128)(2,1)}) custom-call(bf16[128,2048]{1,0:T(8,128)(2,1)} %hidden.5, f32[1,136]{1,0:T(1,128)} %bitcast.12, f32[64,2048]{1,0:T(8,128)} %query_weight.1, f32[64,1024]{1,0:T(8,128)} %key_weight.1, ...), custom_call_target="tpu_custom_call" | custom-call | tf_op jit(solution)/shard_map/opening_0/pallas_call | solution.py:850
  82.6 0.7 slice_bitcast_fusion
  83.3 1.3 fusion
  84.6 0.7 copy.25.key_gain
  85.4 0.7 copy.24.query_gain
  86.1 108.4 %attend_1.1 = (f32[384,1024]{1,0:T(8,128)}, f32[8,1024]{1,0:T(8,128)}, bf16[1024,256]{1,0:T(8,128)(2,1)}, bf16[256,1024]{1,0:T(8,128)(2,1)}, bf16[1024,128]{1,0:...) custom-call(f32[1024,640]{1,0:T(8,128)} %get-tuple-element.54.raw, ...), custom_call_target="tpu_custom_call" | custom-call | tf_op jit(solution)/shard_map/attend_1/pallas_call | solution.py:1104
  194.5 49.3 %feed_2.1 = (bf16[1024,2048]{1,0:T(8,128)(2,1)}, bf16[1024,768]{1,0:T(8,128)(2,1)}, bf16[1024,1536]{1,0:T(8,128)(2,1)}) custom-call(bf16[128,2048]{1,0:T(8,128)(2,1)} %get-tuple-element.57.normed_two, bf16[2048,1536]{1,0:T(8,128)(2,1)} %bitcast.10, bf16[768,2048]{1,0:T(8,128)(2,1)} %get-tuple-element.59.down_low, bf16[1024,2048]{1,0:T(8,128)(2,1)} %get-tuple-element.60.og_all), custom_call_target="tpu_custom_call" | custom-call | tf_op jit(solution)/shard_map/feed_2/pallas_call | solution.py:1645
  243.9 103.3 %feed_back_3.1 = (bf16[1024,2048]{1,0:T(8,128)(2,1)}, f32[128,2048]{1,0:T(8,128)}, f32[1,2048]{1,0:T(1,128)}, bf16[128,2048]{1,0:T(8,128)(2,1)}, bf16[8,64,1536]...) custom-call(bf16[1024,1536]{1,0:T(8,128)(2,1)} %get-tuple-element.61.grad_pre, bf16[2048,1536]{1,0:T(8,128)(2,1)} %bitcast.11, ...), custom_call_target="tpu_custom_call" | custom-call | tf_op jit(solution)/shard_map/feed_back_3/pallas_call | solution.py:1835
  347.1 99.9 %attend_back_4.1 = (bf16[128,2048]{1,0:T(8,128)(2,1)}, f32[1,136]{1,0:T(1,128)}, bf16[64,2048]{1,0:T(8,128)(2,1)}, f32[64,1024]{1,0:T(8,128)}, f32[64,1024]{1,0:...) custom-call(bf16[1024,2048]{1,0:T(8,128)(2,1)} %get-tuple-element.66, ...), custom_call_target="tpu_custom_call" | custom-call | tf_op jit(solution)/shard_map/attend_back_4/pallas_call | solution.py:1512
  447.1 0.0 copy-start
  447.1 0.0 copy-start.1
  447.1 0.0 copy-start.4
  447.1 0.0 copy-start.3
  447.1 1.5 copy.28
  448.6 4.9 %widen.1 = (f32[64,2048]{1,0:T(8,128)}, f32[64,2048]{1,0:T(8,128)}, f32[64,6144]{1,0:T(8,128)}, f32[64,6144]{1,0:T(8,128)}, f32[192,2048]{1,0:T(8,128)}) custom-call(bf16[64,2048]{1,0:T(8,128)(2,1)} %get-tuple-element.84.refs_0_, bf16[64,2048]{1,0:T(8,128)(2,1)} %get-tuple-element.85.refs_1_, bf16[64,6144]{1,0:T(8,128)(2,1)} %get-tuple-element.86.refs_2_, ...), custom_call_target="tpu_custom_call" | custom-call | tf_op jit(solution)/shard_map/widen/pallas_call | solution.py:1883
  453.5 0.0 copy-done
  453.5 0.8 copy.35
  454.3 0.0 copy-done.1
  454.3 0.8 copy.36
  455.1 0.6 copy.37
  455.7 0.7 copy.38
  456.4 0.7 copy.39
  (6 shorter events, 0.0 us)
Async XLA Ops:
  447.1 6.5 %copy-start = (bf16[128,2048]{1,0:T(8,128)(2,1)S(1)}, bf16[128,2048]{1,0:T(8,128)(2,1)}, u32[]{:S(2)}) copy-start(bf16[128,2048]{1,0:T(8,128)(2,1)} %get-tuple-element.125) | copy-start | bytes 1572868
  447.1 7.3 %copy-start.1 = (bf16[128,2048]{1,0:T(8,128)(2,1)S(1)}, bf16[128,2048]{1,0:T(8,128)(2,1)}, u32[]{:S(2)}) copy-start(bf16[128,2048]{1,0:T(8,128)(2,1)} %get-tuple-element.126) | copy-start | bytes 1572868
  447.1 8.0 %copy-start.4 = (f32[1,136]{1,0:T(1,128)S(1)}, f32[1,136]{1,0:T(1,128)}, u32[]{:S(2)}) copy-start(f32[1,136]{1,0:T(1,128)} %get-tuple-element.83) | copy-start | bytes 1636
  447.1 8.6 %copy-start.3 = (f32[64,1024]{1,0:T(8,128)S(1)}, f32[64,1024]{1,0:T(8,128)}, u32[]{:S(2)}) copy-start(f32[64,1024]{1,0:T(8,128)} %get-tuple-element.129) | copy-start | bytes 786436
  448.6 7.8 %copy-start.2 = (f32[64,1024]{1,0:T(8,128)S(1)}, f32[64,1024]{1,0:T(8,128)}, u32[]{:S(2)}) copy-start(f32[64,1024]{1,0:T(8,128)} %get-tuple-element.130) | copy-start | bytes 786436

commit v5 on v4

--- a/solution.py
+++ b/solution.py
@@ -38,6 +38,16 @@
     return lax.dot_general(
         left_side, right_side, (((0,), (0,)), ((), ())), preferred_element_type=full
     )
+
+
+def by_rows(rows, body, tile=32):
+    tile = min(tile, rows)
+
+    def step(index, unused):
+        body(pl.ds(pl.multiple_of(index * tile, tile), tile))
+        return unused
+
+    lax.fori_loop(0, rows // tile, step, 0)
 
 
 def remote(source, target, send, receive, axis, peer):
@@ -250,6 +260,17 @@
             self.l_send,
             self.l_recv,
         ) = scratch
+
+    def clear(self):
+        line = self.line
+
+        @pl.when(jnp.logical_not(line.has_left))
+        def _():
+            self.arrived[line.chip] = jnp.zeros(self.arrived.shape[1:], low)
+
+        @pl.when(jnp.logical_not(line.has_right))
+        def _():
+            self.arrived[line.chips] = jnp.zeros(self.arrived.shape[1:], low)
 
     def there(self, far, side):
         line = self.line
@@ -317,19 +338,31 @@
         def _():
             target = self.target(far, side)
             self.exchange(target).wait_recv()
-            total = self.own[target].astype(full) + self.sib[target].astype(full)
+
+            def add(across):
+                self.own[target, across, :] = (
+                    self.own[target, across, :].astype(full) + self.sib[target, across, :].astype(full)
+                ).astype(low)
+
+            def add_all(across):
+                self.own[target, across, :] = (
+                    self.own[target, across, :].astype(full)
+                    + self.sib[target, across, :].astype(full)
+                    + self.arrived[target, across, :].astype(full)
+                ).astype(low)
+
             if far == line.chips - 1:
-                self.own[target] = total.astype(low)
+                by_rows(self.rows, add)
             else:
 
                 @pl.when(behind)
                 def _():
                     self.send(target, side).wait_recv()
-                    self.own[target] = (total + self.arrived[target].astype(full)).astype(low)
+                    by_rows(self.rows, add_all)
 
                 @pl.when(jnp.logical_not(behind))
                 def _():
-                    self.own[target] = total.astype(low)
+                    by_rows(self.rows, add)
 
             self.send(target, side).start()
 
@@ -337,17 +370,25 @@
         line = self.line
         chip = line.chip
         self.exchange(chip).wait_recv()
-        total_ref[...] = self.own[chip].astype(full) + self.sib[chip].astype(full)
 
         @pl.when(line.has_left)
         def _():
             self.send(chip, 0).wait_recv()
-            total_ref[...] += self.arrived[chip].astype(full)
 
         @pl.when(line.has_right)
         def _():
             self.send(chip, 1).wait_recv()
-            total_ref[...] += self.arrived[line.chips].astype(full)
+
+        def add(across):
+            total = self.own[chip, across, :].astype(full) + self.sib[chip, across, :].astype(full)
+            total = total + jnp.where(
+                line.has_left, self.arrived[chip, across, :].astype(full), 0.0
+            )
+            total_ref[across, :] = total + jnp.where(
+                line.has_right, self.arrived[line.chips, across, :].astype(full), 0.0
+            )
+
+        by_rows(self.rows, add)
 
     def finish(self):
         for far, side in self.order():
@@ -486,10 +527,10 @@
 
 
 class Share:
-    def __init__(self, groups, place, s_sem, r_sem):
+    def __init__(self, groups, place, s_sem, r_sem, relays=True):
         self.groups, self.place, self.s_sem, self.r_sem = groups, place, s_sem, r_sem
         self.group = lax.axis_index("seq")
-        self.square = groups == 4
+        self.square = groups == 4 and relays
         self.across = self.group + 1 - 2 * lax.rem(self.group, 2)
         self.along = lax.rem(self.group + 2, groups)
         self.corner = groups - 1 - self.group
@@ -555,70 +596,38 @@
     def __init__(self, groups, term_ref, inbox, s_sem, r_sem):
         self.groups, self.term, self.inbox = groups, term_ref, inbox
         self.s_sem, self.r_sem = s_sem, r_sem
-        self.group = group = lax.axis_index("seq")
-        self.square = groups == 4
-        self.rows = term_ref.shape[1]
-        if self.square:
-            self.across = group + 1 - 2 * lax.rem(group, 2)
-            self.along = lax.rem(group + 2, groups)
-            self.order = [groups - 1 - group, self.across, self.along, group]
-        else:
-            self.order = [lax.rem(group + shift, groups) for shift in range(1, groups)] + [group]
-
-    def part(self, which):
-        return pl.ds(which * (self.rows // 2), self.rows // 2)
-
-    def copies(self, job):
-        index = self.order[job]
-        block = self.term.at[index]
-        if not self.square:
-            return [self.copy(job, block, self.inbox.at[job], index)]
-        if job == 0:
-            return [
-                self.copy(0, block.at[self.part(0)], self.inbox.at[0, self.part(0)], self.across),
-                self.copy(3, block.at[self.part(1)], self.inbox.at[0, self.part(1)], self.along),
-            ]
-        return [self.copy(job, block, self.inbox.at[job], index)]
-
-    def copy(self, slot, source, target, peer):
-        return remote(source, target, self.s_sem.at[slot], self.r_sem.at[slot], "seq", peer)
+        self.group = lax.axis_index("seq")
+        self.order = [lax.rem(self.group + shift, groups) for shift in range(1, groups)] + [
+            self.group
+        ]
+
+    def copy(self, job):
+        return remote(
+            self.term.at[self.order[job]],
+            self.inbox.at[job],
+            self.s_sem.at[job],
+            self.r_sem.at[job],
+            "seq",
+            self.order[job],
+        )
 
     def ready(self, job):
-        if job < self.groups - 1 and (job == 0 or not self.square):
-            for copy in self.copies(job):
-                copy.start()
-
-    def mix(self):
-        if not self.square:
-            return
-        to_across, to_along = self.copies(0)
-        to_across.wait_recv()
-        mine, half = self.along, self.part(0)
-        self.term[mine, half, :] = (
-            self.term[mine, half, :].astype(full) + self.inbox[0, half, :].astype(full)
-        ).astype(low)
-        self.copies(2)[0].start()
-        to_along.wait_recv()
-        mine, half = self.across, self.part(1)
-        self.term[mine, half, :] = (
-            self.term[mine, half, :].astype(full) + self.inbox[0, half, :].astype(full)
-        ).astype(low)
-        self.copies(1)[0].start()
+        if job < self.groups - 1:
+            self.copy(job).start()
 
     def arrive(self):
-        for job in range(1 if self.square else 0, self.groups - 1):
-            self.copies(job)[0].wait_recv()
-
-    def sum(self, across):
-        total = self.term[self.group, across, :].astype(full)
-        for job in range(1 if self.square else 0, self.groups - 1):
+        for job in range(self.groups - 1):
+            self.copy(job).wait_recv()
+
+    def sum(self, across, own=None):
+        total = (self.term[self.group, across, :] if own is None else own[across, :]).astype(full)
+        for job in range(self.groups - 1):
             total = total + self.inbox[job, across, :].astype(full)
         return total
 
     def finish(self):
         for job in range(self.groups - 1):
-            for copy in self.copies(job):
-                copy.wait_send()
+            self.copy(job).wait_send()
 
 
 class Spread:
@@ -665,6 +674,7 @@
     out_block,
     gains_row,
     gains_all,
+    corner,
     own_attn,
     own_out,
     out_s,
@@ -700,6 +710,9 @@
     gain_swap.start()
 
     blocks[:, :, pl.ds(q_width + 2 * kv_width, HD)] = jnp.zeros((pieces, weight_rows, HD), low)
+    corner[...] = jnp.zeros(corner.shape, full)
+    corner[pl.ds(0, gate_weight.shape[0]), pl.ds(0, weight_rows)] = gate_weight[...]
+    gate_rows = corner[...].T
     for piece in range(pieces):
         blocks[piece, :, pl.ds(0, q_width)] = query_weight[
             :, pl.ds(piece * q_width, q_width)
@@ -709,8 +722,8 @@
         blocks[piece, :, pl.ds(q_width + kv_width, kv_width)] = value_weight[
             :, pl.ds(start, kv_width)
         ].astype(low)
-        blocks[piece, :, pl.ds(q_width + 2 * kv_width, heads)] = gate_weight[
-            :, pl.ds(piece * heads, heads)
+        blocks[piece, :, pl.ds(q_width + 2 * kv_width, heads)] = gate_rows[
+            :weight_rows, piece * heads : (piece + 1) * heads
         ].astype(low)
 
     def place(index, source):
@@ -721,7 +734,7 @@
         line, lambda peer: blocks.at[peer], lambda source: place(group, source), at_s, at_r
     )
     attn_swap.start()
-    share = Share(groups, place, as_s, as_r)
+    share = Share(groups, place, as_s, as_r, False)
     share.send(me, blocks.at[me])
     attn_own = pltpu.make_async_copy(blocks.at[me], place(group, me), own_attn)
     attn_own.start()
@@ -771,7 +784,7 @@
         ]
 
     def chip_rows(chip):
-        return pl.ds(pl.multiple_of(chip * 2 * rows, 2 * rows), 2 * rows)
+        return chip * 2 * rows
 
     def both(far, body):
         if far == 0:
@@ -786,19 +799,21 @@
         def _():
             body(chip_rows(line.chip + far))
 
-    def normalise(across):
-        values = hidden_all[across, :].astype(full)
-        inverse = lax.rsqrt(jnp.mean(values * values, axis=-1, keepdims=True) + epsilon)
-        normed[across, :] = (values * inverse * gains_out[0:1, pl.ds(0, model)]).astype(low)
-
-    def project(across):
+    def normalise(start):
+        def some(part):
+            across = pl.ds(pl.multiple_of(start + part.start, part.size), part.size)
+            values = hidden_all[across, :].astype(full)
+            inverse = lax.rsqrt(jnp.mean(values * values, axis=-1, keepdims=True) + epsilon)
+            normed[across, :] = (values * inverse * gains_out[0:1, pl.ds(0, model)]).astype(low)
+
+        by_rows(2 * rows, some)
+
+    def project(start):
+        across = pl.ds(pl.multiple_of(start, 2 * rows), 2 * rows)
         raw[across, :] = product(normed[across, :], attn_low[...])
 
-    share.relay(me)
-    attn_swap.again(0, share.relay)
     for far in range(2, line.chips):
         attn_swap.receive(far, share.send)
-        attn_swap.again(far - 1, share.relay)
     out_share = Share(groups, lambda index, source: out_place(index), os_s, os_r)
 
     @pl.when(spread.moves)
@@ -810,8 +825,6 @@
         out_stay.wait()
 
     out_share.send(0)
-    if line.chips > 1:
-        attn_swap.again(line.chips - 1, share.relay)
     for hop in range(1, line.chips - 1):
         gather.forward(hop)
         gather.arrive(hop - 1)
@@ -864,6 +877,7 @@
             vmem((weight_rows, model), low),
             vmem((8, padded), full),
             vmem((groups, pieces, 8, padded), full),
+            vmem((HD, HD), full),
         ]
         + [DMA] * 4
         + swap_scratch(pieces)
@@ -899,6 +913,10 @@
     )
 
 
+def column(gains, start):
+    return jnp.broadcast_to(gains[:, pl.ds(start, HD)], (HD, HD)).T[:, 0:1]
+
+
 def inverse_rms(values):
     return lax.rsqrt(jnp.mean(values * values, axis=0, keepdims=True) + epsilon)
 
@@ -930,16 +948,13 @@
     raw,
     cosine,
     sine,
-    query_gain,
-    key_gain,
+    gains,
     prefix_ref,
     out_low,
     hidden,
-    swiglu_gain,
     out_grad,
     gate_weight,
     up_weight,
-    down_weight,
     raw_t,
     gate_t,
     q_ref,
@@ -954,20 +969,15 @@
     normed_two,
     og_all,
     ff_low,
-    down_low,
     vt_ref,
     gated,
     blocks,
-    down_block,
-    down_sem,
     own_sem,
     og_sem,
     swap_s,
     swap_r,
     share_s,
     share_r,
-    down_s,
-    down_r,
     *sems,
 ):
     pieces, groups, heads, kv_heads, ff_block = shape
@@ -977,38 +987,34 @@
     length, rows = raw.shape[0], hidden.shape[0]
     greet(others("ctx", pieces) + others("seq", groups))
     own_width = groups * ff_block
-    for half, weight_ref in enumerate((gate_weight, up_weight)):
-        for index in range(groups):
-            for piece in range(pieces):
-                start = (index * pieces + piece) * ff_block
-                blocks[piece, :, pl.ds(half * own_width + index * ff_block, ff_block)] = weight_ref[
-                    :, pl.ds(start, ff_block)
-                ].astype(low)
+
+    def prepare(across):
+        for half, weight_ref in enumerate((gate_weight, up_weight)):
+            for index in range(groups):
+                for piece in range(pieces):
+                    start = (index * pieces + piece) * ff_block
+                    blocks[piece, across, pl.ds(half * own_width + index * ff_block, ff_block)] = (
+                        weight_ref[across, pl.ds(start, ff_block)].astype(low)
+                    )
+
+    by_rows(gate_weight.shape[0], prepare, 16)
     swap = LineSwap(
         line, lambda peer: blocks.at[peer], lambda source: ff_low.at[group, source], swap_s, swap_r
     )
     swap.start()
-    share = Share(groups, lambda index, source: ff_low.at[index, source], share_s, share_r)
+    share = Share(groups, lambda index, source: ff_low.at[index, source], share_s, share_r, False)
     share.send(me, blocks.at[me])
     own = pltpu.make_async_copy(blocks.at[me], ff_low.at[group, me], own_sem)
     own.start()
-    down_block[...] = down_weight[...].astype(low)
-
-    def down_place(index, source):
-        start = pl.multiple_of(index * ff_block, ff_block)
-        return down_low.at[pl.ds(start, ff_block)]
-
-    down_share = Share(groups, down_place, down_s, down_r)
-    down_own = pltpu.make_async_copy(down_block, down_place(group, 0), down_sem)
-    down_own.start()
-
     prefix = prefix_ref[0, 0]
+    model = hidden.shape[1]
+    query_gain, key_gain = column(gains, 2 * model), column(gains, 2 * model + HD)
     scale = HD ** (-0.5)
     for head in range(heads + kv_heads):
         part = pl.ds(head * HD, HD)
         values = raw[:, part].T
         raw_t[part, :] = values
-        gain = query_gain[...] if head < heads else key_gain[...]
+        gain = query_gain if head < heads else key_gain
         turned = turn(values * inverse_rms(values) * gain, cosine[...], sine[...])
         if head < heads:
             qt_ref[part, :] = turned.astype(low)
@@ -1044,14 +1050,12 @@
         scaled = att_t[part, :] * jax.nn.sigmoid(gate_t[head : head + 1, :])
         gated_t[part, :] = scaled.astype(low)
         gated[:, part] = scaled.T.astype(low)
-        if head == 0:
-            share.relay(me)
-            swap.again(0, share.relay)
-            if line.chips > 1:
-                swap.receive(1, share.send)
+        if head == 0 and line.chips > 1:
+            swap.receive(1, share.send)
 
     gather = Gather(line, 2, rows, og_all, gather_sems)
     scatter = Scatter(line, rows, scatter_refs)
+    scatter.clear()
     block = blocks_nn(gated, out_low, rows)
     last = line.chips - 1
     for far, side in scatter.order():
@@ -1069,33 +1073,29 @@
             scatter.fill(far, side, block)
     for far in range(2, line.chips):
         swap.receive(far, share.send)
-        swap.again(far - 1, share.relay)
-    down_share.send(0, down_block)
     for hop in range(1, line.chips):
         for far, side in scatter.order():
             if far == last - hop and far > 0:
                 scatter.push(far, side)
         gather.forward(hop)
-        if hop == 1:
-            swap.again(last, share.relay)
-        if hop == last:
-            down_share.relay(0)
     scatter.total(middle)
-    values = hidden[...].astype(full) + middle[...]
-    middle[...] = values
-    inverse = lax.rsqrt(jnp.mean(values * values, axis=-1, keepdims=True) + epsilon)
-    normed_two[...] = (values * inverse * swiglu_gain[...]).astype(low)
+
+    def normalise(across):
+        values = hidden[across, :].astype(full) + middle[across, :]
+        middle[across, :] = values
+        inverse = lax.rsqrt(jnp.mean(values * values, axis=-1, keepdims=True) + epsilon)
+        normed_two[across, :] = (values * inverse * gains[:, pl.ds(model, model)]).astype(low)
+
+    by_rows(rows, normalise)
     og_own.wait()
     own.wait()
     gather.complete()
     scatter.finish()
     swap.finish()
     share.finish(pieces)
-    down_own.wait()
-    down_share.finish(1)
-
-
-def attend(raw, tables, gains, prefix, out_low, hidden, swiglu_gain, out_grad, weights, shape, number):
+
+
+def attend(raw, tables, gains, prefix, out_low, hidden, out_grad, weights, shape, number):
     pieces, groups, heads, kv_heads, ff_block = shape
     length, rows, model = raw.shape[0], hidden.shape[0], hidden.shape[1]
     q_width, kv_width = heads * HD, kv_heads * HD
@@ -1118,29 +1118,25 @@
             struct((rows, model), low),
             struct((length, model), low),
             struct((groups, pieces, weight_rows, 2 * groups * ff_block), low),
-            struct((groups * ff_block, model), low),
         ),
-        in_specs=[IN_VMEM] * 5 + [pl.BlockSpec(memory_space=pltpu.SMEM)] + [IN_VMEM] * 7,
-        out_specs=(IN_VMEM,) * 12 + (ANY, ANY, ANY),
+        in_specs=[IN_VMEM] * 4 + [pl.BlockSpec(memory_space=pltpu.SMEM)] + [IN_VMEM] * 5,
+        out_specs=(IN_VMEM,) * 12 + (ANY, ANY),
         scratch_shapes=[
             pltpu.VMEM((kv_width, length), low),
             pltpu.VMEM((length, q_width), low),
             pltpu.VMEM((pieces, weight_rows, 2 * groups * ff_block), low),
-            pltpu.VMEM((ff_block, model), low),
-            DMA,
             DMA,
             DMA,
         ]
         + swap_scratch(pieces)
         + [DMA((pieces, groups))] * 2
-        + [DMA((1, groups))] * 2
         + gather_scratch(pieces, 2)
         + scatter_scratch(pieces, rows, model),
         compiler_params=pltpu.CompilerParams(
             collective_id=number, has_side_effects=True, vmem_limit_bytes=60 << 20
         ),
         name=f"attend_{number}",
-    )(raw, *tables, *gains, prefix, out_low, hidden, swiglu_gain, out_grad, *weights)
+    )(raw, *tables, gains, prefix, out_low, hidden, out_grad, *weights)
 
 
 def attend_back_kernel(
@@ -1159,16 +1155,15 @@
     gated_t,
     cosine,
     sine,
-    query_gain,
-    key_gain,
+    gains,
     prefix_ref,
     normed,
     attn_low,
     hidden,
     grad_middle,
-    attention_gain,
     swiglu_gain_grad,
     ff_share,
+    down_term,
     hidden_grad,
     gains_grad,
     query_grad,
@@ -1178,6 +1173,12 @@
     gate_grad,
     up_grad,
     out_grad,
+    down_grad,
+    down_in,
+    down_mine,
+    down_sem,
+    ff_sem,
+    corner,
     out_term,
     out_in,
     out_send,
@@ -1216,6 +1217,10 @@
     ot_r,
     om_s,
     om_r,
+    de_s,
+    de_r,
+    dl_s,
+    dl_r,
     *scatter_refs,
 ):
     pieces, groups, heads, kv_heads, ff_block = shape
@@ -1238,12 +1243,24 @@
         )
 
     load(0).start()
+    down_rows = down_in.shape[1]
+    half = down_rows // 32 * 16
+    early, late = pl.ds(0, half), pl.ds(half, down_rows - half)
+    down_early = Fold(groups, down_term.at[:, early], down_in.at[:, early], de_s, de_r)
+    down_late = Fold(groups, down_term.at[:, late], down_in.at[:, late], dl_s, dl_r)
+    for job in range(groups):
+        down_early.ready(job)
+    down_own = pltpu.make_async_copy(down_term.at[group], down_mine, down_sem)
+    down_own.start()
+    ff_own = pltpu.make_async_copy(ff_share.at[me], ff_recv.at[me], ff_sem)
+    ff_own.start()
     ff_swap = LineSwap(
         line, lambda peer: ff_share.at[peer], lambda source: ff_recv.at[source], ffs_s, ffs_r
     )
     ff_swap.start()
 
     prefix = prefix_ref[0, 0]
+    query_gain, key_gain = column(gains, 2 * model), column(gains, 2 * model + HD)
     scale = HD ** (-0.5)
 
     def branch(index, unused):
@@ -1296,18 +1313,16 @@
             dv[across, kv_part] += product(chance.astype(low), ga[columns, :])
 
         query_blocks(length, block)
-        if head == heads - 1:
-            out_fold.mix()
 
     gain_columns = [jnp.zeros((HD, 1), full), jnp.zeros((HD, 1), full)]
     for head in range(heads + kv_heads):
         part = pl.ds(head * HD, HD)
         if head < heads:
             turned = gqt[part, :]
-            gain = query_gain[...]
+            gain = query_gain
         else:
             turned = dk[:, pl.ds((head - heads) * HD, HD)].T * scale
-            gain = key_gain[...]
+            gain = key_gain
         grads = turn_back(turned, cosine[...], sine[...])
         values = raw_t[part, :]
         inverse = inverse_rms(values)
@@ -1334,6 +1349,7 @@
     grad[:, part] = gate_block.T.astype(low)
 
     scatter = Scatter(line, rows, scatter_refs)
+    scatter.clear()
     block = blocks_nt(grad, attn_low, rows)
     last = line.chips - 1
 
@@ -1364,7 +1380,7 @@
                 keepdims=True,
             )
             wide = jnp.broadcast_to(weighted, (128, 128)).T
-            gains_vector[:, lanes(start, 128)] = wide[0:1, :] / attention_gain[:, lanes(start, 128)]
+            gains_vector[:, lanes(start, 128)] = wide[0:1, :] / gains[:, lanes(start, 128)]
             return unused
 
         lax.fori_loop(0, share // 128, step, 0)
@@ -1375,11 +1391,13 @@
     pushes(last)
     for job in range(1, groups):
         weight_grad(job)
-        if last - job >= 0:
+        if job <= last:
             fills(last - job)
-    fold.mix()
     for far in range(last - groups, -1, -1):
         fills(far)
+
+    for job in range(groups):
+        down_late.ready(job)
 
     gain_count = gains_grad.shape[1]
     gains_vector[:, pl.ds(model, model)] = swiglu_gain_grad[...]
@@ -1399,7 +1417,11 @@
     pushes(last - 1)
 
     out_fold.arrive()
-    out_send[...] = out_fold.sum(pl.ds(0, weight_rows)).astype(low)
+
+    def total_out(across):
+        out_send[across, :] = out_fold.sum(across).astype(low)
+
+    by_rows(weight_rows, total_out, 16)
     out_move = spread.copy(out_send, out_grad, om_s, om_r, True)
 
     @pl.when(spread.moves)
@@ -1426,39 +1448,59 @@
 
     for far in range(line.chips):
         ff_swap.receive(far, lambda source: None)
-    ff_recv[me] = ff_share[me]
+    ff_own.wait()
     own_width = groups * ff_block
-    for half, grad_ref in enumerate((gate_grad, up_grad)):
-        for index in range(groups):
-            for piece in range(pieces):
-                start = (index * pieces + piece) * ff_block
-                grad_ref[:, pl.ds(start, ff_block)] = ff_recv[
-                    piece, :, pl.ds(half * own_width + index * ff_block, ff_block)
-                ]
+
+    def restore(across):
+        for part, grad_ref in enumerate((gate_grad, up_grad)):
+            for index in range(groups):
+                for piece in range(pieces):
+                    start = (index * pieces + piece) * ff_block
+                    grad_ref[across, pl.ds(start, ff_block)] = ff_recv[
+                        piece, across, pl.ds(part * own_width + index * ff_block, ff_block)
+                    ]
+
+    by_rows(weight_rows, restore, 16)
 
     for far in range(last - 2, 0, -1):
         pushes(far)
 
     fold.arrive()
-    for piece in range(pieces):
-        attn_send[piece] = fold.sum(pl.ds(piece * weight_rows, weight_rows)).astype(low)
+
+    def total_term(piece, unused):
+        across = pl.ds(pl.multiple_of(piece * weight_rows, weight_rows), weight_rows)
+        attn_send[piece] = fold.sum(across).astype(low)
+        return unused
+
+    lax.fori_loop(0, pieces, total_term, 0)
     attn_swap = LineSwap(
         line, lambda peer: attn_send.at[peer], lambda source: attn_recv.at[source], at_s, at_r
     )
     attn_swap.start()
 
     scatter.total(total_ref)
-    values = hidden[...].astype(full)
-    inverse = lax.rsqrt(jnp.mean(values * values, axis=-1, keepdims=True) + epsilon)
-    grads = total_ref[...]
-    scaled = grads * attention_gain[...]
-    hidden_grad[...] = (
-        grad_middle[...]
-        + inverse * scaled
-        - values
-        * (inverse * inverse * inverse * jnp.mean(scaled * values, axis=-1, keepdims=True))
-    ).astype(low)
-
+
+    def rest(across):
+        values = hidden[across, :].astype(full)
+        inverse = lax.rsqrt(jnp.mean(values * values, axis=-1, keepdims=True) + epsilon)
+        scaled = total_ref[across, :] * gains[:, pl.ds(0, model)]
+        hidden_grad[across, :] = (
+            grad_middle[across, :]
+            + inverse * scaled
+            - values
+            * (inverse * inverse * inverse * jnp.mean(scaled * values, axis=-1, keepdims=True))
+        ).astype(low)
+
+    by_rows(rows, rest)
+    down_early.arrive()
+    down_late.arrive()
+    down_own.wait()
+    whole_fold = Fold(groups, down_term, down_in, de_s, de_r)
+
+    def total_down(across):
+        down_grad[across, :] = whole_fold.sum(across, down_mine).astype(low)
+
+    by_rows(down_grad.shape[0], total_down, 16)
     for shift in range(1, groups):
         peer = lax.rem(group + groups - shift, groups)
         remote(
@@ -1470,11 +1512,13 @@
         attn_swap.receive(far, lambda source: None)
     attn_recv[me] = attn_send[me]
     copies = max(1, pieces // KV)
+    corner[...] = jnp.zeros(corner.shape, full)
     for piece in range(pieces):
         query_grad[:, pl.ds(piece * q_width, q_width)] = attn_recv[piece, :, pl.ds(0, q_width)]
-        head_grad[:, pl.ds(piece * heads, heads)] = attn_recv[
+        corner[pl.ds(0, weight_rows), pl.ds(piece * heads, heads)] = attn_recv[
             piece, :, pl.ds(q_width + 2 * kv_width, heads)
         ].astype(full)
+    head_grad[...] = corner[...].T[: head_grad.shape[0], :weight_rows]
     for place in range(pieces // copies):
         for kind, grad_ref in enumerate((key_grad, value_grad)):
             columns = pl.ds(q_width + kind * kv_width, kv_width)
@@ -1496,11 +1540,13 @@
         gain_to(shift).wait_send()
     fold.finish()
     out_fold.finish()
+    down_early.finish()
+    down_late.finish()
 
 
 def attend_back(
     grad_branch, out_low, saved, gated_t, tables, gains, prefix, normed, attn_low, hidden, grad_middle,
-    attention_gain, swiglu_gain_grad, ff_share, gain_count, shape, number,
+    swiglu_gain_grad, ff_share, down_term, gain_count, shape, number,
 ):
     pieces, groups, heads, kv_heads, ff_block = shape
     length, (rows, model) = grad_branch.shape[0], hidden.shape
@@ -1517,14 +1563,20 @@
             struct((weight_rows, H * HD), low),
             struct((weight_rows, KV * HD), full),
             struct((weight_rows, KV * HD), full),
-            struct((weight_rows, H), full),
+            struct((H, weight_rows), full),
             struct((weight_rows, pieces * groups * ff_block), low),
             struct((weight_rows, pieces * groups * ff_block), low),
             struct((weight_rows, model), low),
+            struct(down_term.shape[1:], low),
         ),
-        in_specs=[IN_VMEM] * 16 + [pl.BlockSpec(memory_space=pltpu.SMEM), ANY] + [IN_VMEM] * 6,
-        out_specs=(IN_VMEM,) * 9,
+        in_specs=[IN_VMEM] * 15 + [pl.BlockSpec(memory_space=pltpu.SMEM), ANY] + [IN_VMEM] * 4 + [ANY, ANY],
+        out_specs=(IN_VMEM,) * 10,
         scratch_shapes=[
+            vmem((groups - 1,) + down_term.shape[1:], low),
+            vmem(down_term.shape[1:], low),
+            DMA,
+            DMA,
+            vmem((HD, HD), full),
             vmem((groups, weight_rows, model), low),
             vmem((groups - 1, weight_rows, model), low),
             vmem((weight_rows, model), low),
@@ -1553,14 +1605,15 @@
         + swap_scratch(pieces) * 3
         + [DMA((groups,))] * 6
         + [DMA] * 2
+        + [DMA((groups,))] * 4
         + scatter_scratch(pieces, rows, model),
         compiler_params=pltpu.CompilerParams(
-            collective_id=number, has_side_effects=True, vmem_limit_bytes=63 << 20
+            collective_id=number, has_side_effects=True, vmem_limit_bytes=67043328
         ),
         name=f"attend_back_{number}",
     )(
-        grad_branch, out_low, *saved, gated_t, *tables, *gains, prefix, normed, attn_low, hidden, grad_middle,
-        attention_gain, swiglu_gain_grad, ff_share,
+        grad_branch, out_low, *saved, gated_t, *tables, gains, prefix, normed, attn_low, hidden, grad_middle,
+        swiglu_gain_grad, ff_share, down_term,
     )
 
 
@@ -1568,30 +1621,42 @@
     shape,
     normed_two,
     ff_low,
-    down_low,
+    down_weight,
     og_all,
     n2_all,
     hidden_ff,
     grad_pre,
-    grad_hidden,
+    down_low,
+    down_block,
+    before,
+    share_s,
+    share_r,
     *gather_sems,
 ):
-    pieces = shape[0]
+    pieces, groups = shape[:2]
     line = Line(pieces)
     rows, length = normed_two.shape[0], og_all.shape[0]
-    own_width = down_low.shape[0]
+    own_width = ff_low.shape[1] // 2
     tile = own_width // 3 if own_width % 384 == 0 else 128
-    greet(line.peers())
+    greet(line.peers() + others("seq", groups))
+    group = lax.axis_index("seq")
+    block_rows = down_weight.shape[0]
+
+    def place(index, source):
+        start = pl.multiple_of(index * block_rows, block_rows)
+        return down_low.at[pl.ds(start, block_rows)]
+
     gather = Gather(line, 2, rows, n2_all, gather_sems)
     gather.start(normed_two)
     n2_all[pl.ds(pl.multiple_of(line.me * rows, rows), rows), :] = normed_two[...]
 
-    def backward(index, unused):
-        across = pl.ds(pl.multiple_of(index * 256, 256), 256)
-        grad_hidden[across, :] = product_nt(og_all[across, :], down_low[...])
-        return unused
-
-    lax.fori_loop(0, length // 256, backward, 0)
+    def narrow(across):
+        down_block[across, :] = down_weight[across, :].astype(low)
+
+    by_rows(block_rows, narrow, 16)
+    share = Share(groups, place, share_s, share_r, False)
+    share.send(0, down_block)
+    down_low[pl.ds(pl.multiple_of(group * block_rows, block_rows), block_rows), :] = down_block[...]
 
     def chip_rows(chip):
         across = pl.ds(pl.multiple_of(chip * 2 * rows, 2 * rows), 2 * rows)
@@ -1599,9 +1664,42 @@
         def step(index, unused):
             start = index * tile
             first, second = lanes(start, tile), lanes(own_width + start, tile)
-            gate = product(n2_all[across, :], ff_low[:, first])
-            up = product(n2_all[across, :], ff_low[:, second])
-            grads = grad_hidden[across, first]
+            before[across, first] = product(n2_all[across, :], ff_low[:, first])
+            before[across, second] = product(n2_all[across, :], ff_low[:, second])
+            return unused
+
+        lax.fori_loop(0, own_width // tile, step, 0)
+
+    def compute(far):
+        gather.arrive(far)
+        if far == 0:
+            chip_rows(line.chip)
+            return
+
+        @pl.when(line.chip - far >= 0)
+        def _():
+            chip_rows(line.chip - far)
+
+        @pl.when(line.chip + far < line.chips)
+        def _():
+            chip_rows(line.chip + far)
+
+    for hop in range(1, line.chips - 1):
+        gather.forward(hop)
+        compute(hop - 1)
+    if line.chips > 1:
+        compute(line.chips - 2)
+        gather.forward(line.chips - 1)
+    compute(line.chips - 1)
+    share.finish(1)
+
+    def swiglu(index, unused):
+        across = pl.ds(pl.multiple_of(index * 256, 256), 256)
+
+        def step(column, unused):
+            first, second = lanes(column * tile, tile), lanes(own_width + column * tile, tile)
+            grads = product_nt(og_all[across, :], down_low[lanes(column * tile, tile), :])
+            gate, up = before[across, first], before[across, second]
             sigmoid = jax.nn.sigmoid(gate)
             silu = gate * sigmoid
             hidden_ff[across, first] = (silu * up).astype(low)
@@ -1611,36 +1709,16 @@
             grad_pre[across, second] = (grads * silu).astype(low)
             return unused
 
-        lax.fori_loop(0, own_width // tile, step, 0)
-
-    def compute(far):
-        gather.arrive(far)
-        if far == 0:
-            chip_rows(line.chip)
-            return
-
-        @pl.when(line.chip - far >= 0)
-        def _():
-            chip_rows(line.chip - far)
-
-        @pl.when(line.chip + far < line.chips)
-        def _():
-            chip_rows(line.chip + far)
-
-    for hop in range(1, line.chips - 1):
-        gather.forward(hop)
-        compute(hop - 1)
-    if line.chips > 1:
-        compute(line.chips - 2)
-        gather.forward(line.chips - 1)
-    compute(line.chips - 1)
+        return lax.fori_loop(0, own_width // tile, step, unused)
+
+    lax.fori_loop(0, length // 256, swiglu, 0)
     gather.finish()
 
 
-def feed(normed_two, ff_low, down_low, og_all, shape, number):
-    pieces = shape[0]
+def feed(normed_two, ff_low, down_weight, og_all, shape, number):
+    pieces, groups = shape[:2]
     length, model = og_all.shape
-    own_width = down_low.shape[0]
+    own_width = ff_low.shape[1] // 2
     struct = jax.ShapeDtypeStruct
     return pl.pallas_call(
         functools.partial(feed_kernel, shape),
@@ -1648,15 +1726,22 @@
             struct((length, model), low),
             struct((length, own_width), low),
             struct((length, 2 * own_width), low),
+            struct((own_width, model), low),
         ),
         in_specs=[IN_VMEM] * 4,
-        out_specs=(IN_VMEM,) * 3,
-        scratch_shapes=[pltpu.VMEM((length, own_width), full)] + gather_scratch(pieces, 2),
+        out_specs=(IN_VMEM,) * 4,
+        scratch_shapes=[
+            pltpu.VMEM(down_weight.shape, low),
+            pltpu.VMEM((length, 2 * own_width), full),
+            DMA((1, groups)),
+            DMA((1, groups)),
+        ]
+        + gather_scratch(pieces, 2),
         compiler_params=pltpu.CompilerParams(
             collective_id=number, has_side_effects=True, vmem_limit_bytes=60 << 20
         ),
         name=f"feed_{number}",
-    )(normed_two, ff_low, down_low, og_all)
+    )(normed_two, ff_low, down_weight, og_all)
 
 
 def feed_back_kernel(
@@ -1669,15 +1754,13 @@
     n2_all,
     middle,
     out_grad,
-    swiglu_gain,
+    gains,
     gb_all,
     grad_middle,
     gain_grad,
     hidden_out,
     ff_share,
-    down_share,
     down_term,
-    down_in,
     total_ref,
     branch,
     n2_part,
@@ -1687,8 +1770,6 @@
     own_sem,
     ts_s,
     ts_r,
-    ds_s,
-    ds_r,
     *sems,
 ):
     pieces, groups = shape[:2]
@@ -1702,6 +1783,8 @@
     half = len(sems) // 2
     inner = Scatter(line, rows, buffers + sems[:half])
     outer = Scatter(line, rows, buffers + sems[half:])
+    inner.clear()
+    outer.clear()
     block = blocks_nt(grad_pre, ff_low, rows)
     last = line.chips - 1
 
@@ -1718,7 +1801,6 @@
     share = model // groups
 
     fold = Fold(groups, term, term_in, ts_s, ts_r)
-    down_fold = Fold(groups, down_term, down_in, ds_s, ds_r)
 
     def load(job):
         index = fold.order[job]
@@ -1745,8 +1827,6 @@
             job = jobs.pop(0)
             ff_grad(job, fold.order[job])
             fold.ready(job)
-            if not jobs:
-                fold.mix()
 
     load(0).start()
     fills(inner, last, block)
@@ -1774,22 +1854,25 @@
         return unused
 
     lax.fori_loop(0, down_low.shape[0] // 128, down_grads, 0)
-    for job in range(groups):
-        down_fold.ready(job)
     inner.total(total_ref)
     inner.finish()
-    values, grads = middle[...], total_ref[...]
-    inverse = lax.rsqrt(jnp.mean(values * values, axis=-1, keepdims=True) + epsilon)
-    gain_grad[...] = jnp.sum(grads * values * inverse, axis=0, keepdims=True)
-    scaled = grads * swiglu_gain[...]
-    result = (
-        out_grad[...].astype(full)
-        + inverse * scaled
-        - values
-        * (inverse * inverse * inverse * jnp.mean(scaled * values, axis=-1, keepdims=True))
-    )
-    grad_middle[...] = result
-    branch[...] = result.astype(low)
+    gain_grad[...] = jnp.zeros(gain_grad.shape, full)
+
+    def rest(across):
+        values, grads = middle[across, :], total_ref[across, :]
+        inverse = lax.rsqrt(jnp.mean(values * values, axis=-1, keepdims=True) + epsilon)
+        gain_grad[...] += jnp.sum(grads * values * inverse, axis=0, keepdims=True)
+        scaled = grads * gains[:, pl.ds(model, model)]
+        result = (
+            out_grad[across, :].astype(full)
+            + inverse * scaled
+            - values
+            * (inverse * inverse * inverse * jnp.mean(scaled * values, axis=-1, keepdims=True))
+        )
+        grad_middle[across, :] = result
+        branch[across, :] = result.astype(low)
+
+    by_rows(rows, rest)
 
     gather = Gather(line, 2, rows, gb_all, gather_sems)
     gather.start(branch)
@@ -1805,26 +1888,30 @@
         pushes(outer, last - hop)
         if hop < last:
             fills(outer, last - 1 - hop, block)
-        if hop == 1:
-            down_fold.mix()
     fold.arrive()
-    for piece in range(pieces):
-        ff_share[piece] = fold.sum(pl.ds(piece * weight_rows, weight_rows)).astype(low)
-    down_fold.arrive()
-    down_share[...] = down_fold.sum(pl.ds(0, down_rows)).astype(low)
+
+    def total_term(piece, unused):
+        across = pl.ds(pl.multiple_of(piece * weight_rows, weight_rows), weight_rows)
+        ff_share[piece] = fold.sum(across).astype(low)
+        return unused
+
+    lax.fori_loop(0, pieces, total_term, 0)
     outer.total(total_ref)
-    hidden_out[...] = (middle[...] + total_ref[...]).astype(low)
+
+    def output(across):
+        hidden_out[across, :] = (middle[across, :] + total_ref[across, :]).astype(low)
+
+    by_rows(rows, output)
     own.wait()
     for hop in range(line.chips):
         gather.arrive(hop)
     gather.finish()
     outer.finish()
     fold.finish()
-    down_fold.finish()
 
 
 def feed_back(
-    grad_pre, ff_low, hidden_ff, down_low, og_all, n2_all, middle, out_grad, swiglu_gain, shape, number
+    grad_pre, ff_low, hidden_ff, down_low, og_all, n2_all, middle, out_grad, gains, shape, number
 ):
     pieces, groups = shape[:2]
     length, (rows, model) = og_all.shape[0], middle.shape
@@ -1840,13 +1927,11 @@
             struct((1, model), full),
             struct((rows, model), low),
             struct((pieces, weight_rows, width), low),
-            struct((own_width // groups, model), low),
+            struct((groups, own_width // groups, model), low),
         ),
         in_specs=[IN_VMEM] * 5 + [ANY] + [IN_VMEM] * 3,
         out_specs=(ANY,) + (IN_VMEM,) * 5,
         scratch_shapes=[
-            vmem((groups, own_width // groups, model), low),
-            vmem((groups - 1, own_width // groups, model), low),
             vmem((rows, model), full),
             vmem((rows, model), low),
             vmem((2, length, model // groups), low),
@@ -1854,8 +1939,6 @@
             vmem((groups - 1, model // groups, width), low),
             DMA((2,)),
             DMA,
-            DMA((groups,)),
-            DMA((groups,)),
             DMA((groups,)),
             DMA((groups,)),
         ]
@@ -1866,24 +1949,26 @@
             collective_id=number, has_side_effects=True, vmem_limit_bytes=63 << 20
         ),
         name=f"feed_back_{number}",
-    )(grad_pre, ff_low, hidden_ff, down_low, og_all, n2_all, middle, out_grad, swiglu_gain)
+    )(grad_pre, ff_low, hidden_ff, down_low, og_all, n2_all, middle, out_grad, gains)
 
 
 def widen_kernel(*refs):
     for source, target in zip(refs[: len(refs) // 2], refs[len(refs) // 2 :]):
-        target[...] = source[...].astype(full)
-
-
-def widen(arrays):
-    steps = max(1, arrays[0].shape[0] // 16)
+        target[...] = source[...].astype(target.dtype)
+
+
+def widen(arrays, kinds):
+    steps = math.gcd(*(array.shape[0] for array in arrays[:-2])) // 16
     specs = [
         pl.BlockSpec((array.shape[0] // steps, array.shape[1]), lambda step: (step, 0))
-        for array in arrays
-    ]
+        for array in arrays[:-2]
+    ] + [pl.BlockSpec(array.shape, lambda step: (0, 0)) for array in arrays[-2:]]
     return pl.pallas_call(
         widen_kernel,
         grid=(steps,),
-        out_shape=[jax.ShapeDtypeStruct(array.shape, full) for array in arrays],
+        out_shape=[
+            jax.ShapeDtypeStruct(array.shape, kind) for array, kind in zip(arrays, kinds)
+        ],
         in_specs=specs,
         out_specs=specs,
         name="widen",
@@ -1918,62 +2003,82 @@
     normed, raw, attn_low, gains_full, out_low = opening(
         hidden_in,
         norm_gains,
-        (query_weight, key_weight, value_weight, head_gate_weight, out_weight),
+        (query_weight, key_weight, value_weight, head_gate_weight.T, out_weight),
         shape,
         0,
-    )
-    attention_gain = gains_full[:, :model]
-    swiglu_gain = gains_full[:, model : 2 * model]
-    head_gains = (
-        gains_full[0, 2 * model : 2 * model + HD, None],
-        gains_full[0, 2 * model + HD :, None],
     )
     inverse = rope_base ** (-jnp.arange(HD // 2, dtype=full) * 2.0 / HD)
     angles = inverse[:, None] * jnp.arange(length, dtype=jnp.int32).astype(full)[None, :]
     tables = (jnp.cos(angles), jnp.sin(angles))
     prefix = prefix_len.reshape(1, 1)
 
-    *saved, gated_t, middle, normed_two, out_grad_all, ff_low, down_low = attend(
+    *saved, gated_t, middle, normed_two, out_grad_all, ff_low = attend(
         raw,
         tables,
-        head_gains,
+        gains_full,
         prefix,
         out_low,
         hidden_in,
-        swiglu_gain,
         out_grad,
-        (gate_weight, up_weight, down_weight),
+        (gate_weight, up_weight),
         shape,
         1,
     )
     ff_low = ff_low.reshape(model, 2 * ff_own)
-    n2_all, hidden_ff, grad_pre = feed(normed_two, ff_low, down_low, out_grad_all, shape, 2)
-    grad_branch, grad_middle, swiglu_gain_grad, hidden_out, ff_share, down_share = feed_back(
-        grad_pre, ff_low, hidden_ff, down_low, out_grad_all, n2_all, middle, out_grad, swiglu_gain, shape, 3
+    n2_all, hidden_ff, grad_pre, down_low = feed(
+        normed_two, ff_low, down_weight, out_grad_all, shape, 2
     )
-    hidden_grad, gains_share, query_share, key_share, value_share, head_share, gate_share, up_share, output_share = (
+    grad_branch, grad_middle, swiglu_gain_grad, hidden_out, ff_share, down_term = feed_back(
+        grad_pre, ff_low, hidden_ff, down_low, out_grad_all, n2_all, middle, out_grad, gains_full, shape, 3
+    )
+    hidden_grad, gains_share, query_share, key_share, value_share, head_share, gate_share, up_share, output_share, down_share = (
         attend_back(
             grad_branch,
             out_low,
             saved,
             gated_t,
             tables,
-            head_gains,
+            gains_full,
             prefix,
             normed,
             attn_low,
             hidden_in,
             grad_middle,
-            attention_gain,
             swiglu_gain_grad,
             ff_share,
+            down_term,
             gain_count,
             shape,
             4,
         )
     )
-    query_share, output_share, gate_share, up_share, down_share = widen(
-        (query_share, output_share, gate_share, up_share, down_share)
+    (
+        hidden_out,
+        hidden_grad,
+        query_share,
+        key_share,
+        value_share,
+        output_share,
+        gate_share,
+        up_share,
+        down_share,
+        head_share,
+        gains_share,
+    ) = widen(
+        (
+            hidden_out,
+            hidden_grad,
+            query_share,
+            key_share,
+            value_share,
+            output_share,
+            gate_share,
+            up_share,
+            down_share,
+            head_share,
+            gains_share,
+        ),
+        (low, low) + (full,) * 9,
     )
     return (
         hidden_out,
@@ -1982,7 +2087,7 @@
         query_share,
         key_share,
         value_share,
-        head_share,
+        head_share.T,
         output_share,
         gate_share,
         up_share,

time: 465 us -> 453 us (0.974)
  the two profiles are of different devices: /device:TPU:1 before, /device:TPU:3 now
where the time goes in v5:
time: 453 us; the launch traced here: 445 us
  Pallas kernels  441 us (97%)
    pallas_call x1, Pallas kernels, attend(): pl.pallas_call(functools.partial(attend_kernel, shape), out_shape=(struct...  105 us
    pallas_call x1, Pallas kernels, attend_back(): pl.pallas_call(functools.partial(attend_back_kernel, shape), out_shape=(s...  104 us
    pallas_call x1, Pallas kernels, feed_back(): pl.pallas_call(functools.partial(feed_back_kernel, shape), out_shape=(str...  98.7 us
    pallas_call x1, Pallas kernels, opening(): pl.pallas_call(functools.partial(opening_kernel, shape, parts), out_shape...  72.3 us
    pallas_call x1, Pallas kernels, feed(): pl.pallas_call(functools.partial(feed_kernel, shape), out_shape=(struct((...  55.6 us

profile of v5, /device:TPU:3, one launch (start us, length us, event | category | flops | bytes accessed | tf_op | source)
XLA Modules:
  0.0 445.0 jit_solution(9844564219921282399)
XLA Ops:
  1.3 1.8 multiply_sine_fusion
  3.1 72.3 %opening_0.1 = (bf16[1024,2048]{1,0:T(8,128)(2,1)}, f32[1024,640]{1,0:T(8,128)}, bf16[2048,640]{1,0:T(8,128)(2,1)}, f32[1,4352]{1,0:T(1,128)}, bf16[256,2048]{1,0:T(8,128)(2,1)}) custom-call(bf16[128,2048]{1,0:T(8,128)(2,1)} %hidden.5, f32[1,136]{1,0:T(1,128)} %bitcast.11, f32[64,2048]{1,0:T(8,128)} %query_weight.1, f32[64,1024]{1,0:T(8,128)} %key_weight.1, ...), custom_call_target="tpu_custom_call" | custom-call | tf_op jit(solution)/shard_map/opening_0/pallas_call | solution.py:863
  75.4 104.8 %attend_1.1 = (f32[384,1024]{1,0:T(8,128)}, f32[8,1024]{1,0:T(8,128)}, bf16[1024,256]{1,0:T(8,128)(2,1)}, bf16[256,1024]{1,0:T(8,128)(2,1)}, bf16[1024,128]{1,0:...) custom-call(f32[1024,640]{1,0:T(8,128)} %get-tuple-element.61.raw, ...), custom_call_target="tpu_custom_call" | custom-call | tf_op jit(solution)/shard_map/attend_1/pallas_call | solution.py:1104
  180.2 55.6 %feed_2.1 = (bf16[1024,2048]{1,0:T(8,128)(2,1)}, bf16[1024,768]{1,0:T(8,128)(2,1)}, bf16[1024,1536]{1,0:T(8,128)(2,1)}, bf16[768,2048]{1,0:T(8,128)(2,1)}) custom-call(bf16[128,2048]{1,0:T(8,128)(2,1)} %get-tuple-element.64.normed_two, bf16[2048,1536]{1,0:T(8,128)(2,1)} %bitcast.8, f32[192,2048]{1,0:T(8,128)} %down_weight.1, ...), custom_call_target="tpu_custom_call" | custom-call | tf_op jit(solution)/shard_map/feed_2/pallas_call | solution.py:1723
  235.9 98.7 %feed_back_3.1 = (bf16[1024,2048]{1,0:T(8,128)(2,1)}, f32[128,2048]{1,0:T(8,128)}, f32[1,2048]{1,0:T(1,128)}, bf16[128,2048]{1,0:T(8,128)(2,1)}, bf16[8,64,1536]...) custom-call(bf16[1024,1536]{1,0:T(8,128)(2,1)} %get-tuple-element.67.grad_pre, bf16[2048,1536]{1,0:T(8,128)(2,1)} %bitcast.9, ...), custom_call_target="tpu_custom_call" | custom-call | tf_op jit(solution)/shard_map/feed_back_3/pallas_call | solution.py:1922
  334.6 104.2 %attend_back_4.1 = (bf16[128,2048]{1,0:T(8,128)(2,1)}, f32[1,136]{1,0:T(1,128)}, bf16[64,2048]{1,0:T(8,128)(2,1)}, f32[64,1024]{1,0:T(8,128)}, f32[64,1024]{1,0:...) custom-call(bf16[1024,2048]{1,0:T(8,128)(2,1)} %get-tuple-element.73, ...), custom_call_target="tpu_custom_call" | custom-call | tf_op jit(solution)/shard_map/attend_back_4/pallas_call | solution.py:1558
  438.8 5.7 %widen.1 = (bf16[128,2048]{1,0:T(8,128)(2,1)}, bf16[128,2048]{1,0:T(8,128)(2,1)}, f32[64,2048]{1,0:T(8,128)}, f32[64,1024]{1,0:T(8,128)}, f32[64,1024]{1,0:T(8,1...) custom-call(bf16[128,2048]{1,0:T(8,128)(2,1)} %get-tuple-element.72., ...), custom_call_target="tpu_custom_call" | custom-call | tf_op jit(solution)/shard_map/widen/pallas_call | solution.py:1966
  (2 shorter events, 0.0 us)

commit v6 on v5

--- a/solution.py
+++ b/solution.py
@@ -654,245 +654,6 @@
         )
 
 
-def opening_kernel(
-    shape,
-    parts,
-    hidden,
-    gains_ref,
-    query_weight,
-    key_weight,
-    value_weight,
-    gate_weight,
-    out_weight,
-    normed,
-    raw,
-    attn_low,
-    gains_out,
-    out_low,
-    hidden_all,
-    blocks,
-    out_block,
-    gains_row,
-    gains_all,
-    corner,
-    own_attn,
-    own_out,
-    out_s,
-    out_r,
-    ga_s,
-    ga_r,
-    gs_s,
-    gs_r,
-    at_s,
-    at_r,
-    as_s,
-    as_r,
-    os_s,
-    os_r,
-    *gather_sems,
-):
-    pieces, groups, heads, kv_heads, _ = shape
-    line = Line(pieces)
-    me, group = line.me, lax.axis_index("seq")
-    rows, model = hidden.shape
-    weight_rows = out_weight.shape[0]
-    q_width, kv_width = heads * HD, kv_heads * HD
-    copies = max(1, pieces // KV)
-    spread = Spread(groups, pieces)
-    greet(others("ctx", pieces) + others("seq", groups) + spread.peers())
-    gain_count = gains_ref.shape[1]
-    gains_row[...] = jnp.zeros(gains_row.shape, full)
-    gains_row[0:1, pl.ds(0, gain_count)] = gains_ref[...].astype(low).astype(full)
-    gains_all[group, me] = gains_row[...]
-    gain_swap = LineSwap(
-        line, lambda peer: gains_row, lambda source: gains_all.at[group, source], ga_s, ga_r
-    )
-    gain_swap.start()
-
-    blocks[:, :, pl.ds(q_width + 2 * kv_width, HD)] = jnp.zeros((pieces, weight_rows, HD), low)
-    corner[...] = jnp.zeros(corner.shape, full)
-    corner[pl.ds(0, gate_weight.shape[0]), pl.ds(0, weight_rows)] = gate_weight[...]
-    gate_rows = corner[...].T
-    for piece in range(pieces):
-        blocks[piece, :, pl.ds(0, q_width)] = query_weight[
-            :, pl.ds(piece * q_width, q_width)
-        ].astype(low)
-        start = piece // copies * kv_width
-        blocks[piece, :, pl.ds(q_width, kv_width)] = key_weight[:, pl.ds(start, kv_width)].astype(low)
-        blocks[piece, :, pl.ds(q_width + kv_width, kv_width)] = value_weight[
-            :, pl.ds(start, kv_width)
-        ].astype(low)
-        blocks[piece, :, pl.ds(q_width + 2 * kv_width, heads)] = gate_rows[
-            :weight_rows, piece * heads : (piece + 1) * heads
-        ].astype(low)
-
-    def place(index, source):
-        start = pl.multiple_of((index * pieces + source) * weight_rows, weight_rows)
-        return attn_low.at[pl.ds(start, weight_rows)]
-
-    attn_swap = LineSwap(
-        line, lambda peer: blocks.at[peer], lambda source: place(group, source), at_s, at_r
-    )
-    attn_swap.start()
-    share = Share(groups, place, as_s, as_r, False)
-    share.send(me, blocks.at[me])
-    attn_own = pltpu.make_async_copy(blocks.at[me], place(group, me), own_attn)
-    attn_own.start()
-    gather = Gather(line, parts, rows, hidden_all, gather_sems)
-    gather.start(hidden)
-    hidden_all[pl.ds(pl.multiple_of(me * rows, rows), rows), :] = hidden[...]
-    out_block[...] = out_weight[...].astype(low)
-
-    def out_place(index):
-        return out_low.at[pl.ds(pl.multiple_of(index * weight_rows, weight_rows), weight_rows)]
-
-    out_move = spread.copy(out_block, out_place(spread.use[0]), out_s, out_r, False)
-    out_stay = pltpu.make_async_copy(out_block, out_place(group), own_out)
-
-    @pl.when(spread.moves)
-    def _():
-        out_move.start()
-
-    @pl.when(jnp.logical_not(spread.moves))
-    def _():
-        out_stay.start()
-
-    def to_groups(shift):
-        peer = lax.rem(group + shift, groups)
-        return remote(
-            gains_all.at[group], gains_all.at[group], gs_s.at[shift], gs_r.at[shift], "seq", peer
-        )
-
-    def from_groups(shift):
-        peer = lax.rem(group + groups - shift, groups)
-        return remote(
-            gains_all.at[peer], gains_all.at[peer], gs_s.at[shift], gs_r.at[shift], "seq", peer
-        )
-
-    attn_swap.receive(0, share.send)
-    for far in range(line.chips):
-        gain_swap.receive(far, lambda source: None)
-    for shift in range(1, groups):
-        to_groups(shift).start()
-    if line.chips > 1:
-        attn_swap.receive(1, share.send)
-    for shift in range(1, groups):
-        from_groups(shift).wait_recv()
-    for index in range(groups * pieces):
-        gains_out[0:1, pl.ds(index * gain_count, gain_count)] = gains_all[
-            index // pieces, index % pieces, 0:1, pl.ds(0, gain_count)
-        ]
-
-    def chip_rows(chip):
-        return chip * 2 * rows
-
-    def both(far, body):
-        if far == 0:
-            body(chip_rows(line.chip))
-            return
-
-        @pl.when(line.chip - far >= 0)
-        def _():
-            body(chip_rows(line.chip - far))
-
-        @pl.when(line.chip + far < line.chips)
-        def _():
-            body(chip_rows(line.chip + far))
-
-    def normalise(start):
-        def some(part):
-            across = pl.ds(pl.multiple_of(start + part.start, part.size), part.size)
-            values = hidden_all[across, :].astype(full)
-            inverse = lax.rsqrt(jnp.mean(values * values, axis=-1, keepdims=True) + epsilon)
-            normed[across, :] = (values * inverse * gains_out[0:1, pl.ds(0, model)]).astype(low)
-
-        by_rows(2 * rows, some)
-
-    def project(start):
-        across = pl.ds(pl.multiple_of(start, 2 * rows), 2 * rows)
-        raw[across, :] = product(normed[across, :], attn_low[...])
-
-    for far in range(2, line.chips):
-        attn_swap.receive(far, share.send)
-    out_share = Share(groups, lambda index, source: out_place(index), os_s, os_r)
-
-    @pl.when(spread.moves)
-    def _():
-        spread.copy(out_place(group), out_place(group), out_s, out_r, False).wait_recv()
-
-    @pl.when(jnp.logical_not(spread.moves))
-    def _():
-        out_stay.wait()
-
-    out_share.send(0)
-    for hop in range(1, line.chips - 1):
-        gather.forward(hop)
-        gather.arrive(hop - 1)
-        both(hop - 1, normalise)
-    gather.arrive(line.chips - 2)
-    both(line.chips - 2, normalise)
-    attn_own.wait()
-    out_share.relay(0)
-    share.finish(pieces)
-    for far in range(line.chips - 1):
-        both(far, project)
-    gather.forward(line.chips - 1)
-    gather.arrive(line.chips - 1)
-    both(line.chips - 1, normalise)
-    both(line.chips - 1, project)
-    out_share.finish(1)
-    gather.finish()
-    gain_swap.finish()
-    attn_swap.finish()
-    for shift in range(1, groups):
-        to_groups(shift).wait_send()
-
-    @pl.when(spread.moves)
-    def _():
-        out_move.wait_send()
-
-
-def opening(hidden, norm_gains, weights, shape, number, parts=2):
-    pieces, groups, heads, kv_heads, _ = shape
-    rows, model = hidden.shape
-    weight_rows = weights[0].shape[0]
-    gains = norm_gains.shape[0]
-    padded = -(-gains // 128) * 128
-    width = (heads + 2 * kv_heads + 1) * HD
-    struct, vmem = jax.ShapeDtypeStruct, pltpu.VMEM
-    return pl.pallas_call(
-        functools.partial(opening_kernel, shape, parts),
-        out_shape=(
-            struct((pieces * rows, model), low),
-            struct((pieces * rows, width), full),
-            struct((model, width), low),
-            struct((1, groups * pieces * gains), full),
-            struct((groups * weight_rows, model), low),
-        ),
-        in_specs=[IN_VMEM] * 7,
-        out_specs=(IN_VMEM,) * 5,
-        scratch_shapes=[
-            vmem((pieces * rows, model), low),
-            vmem((pieces, weight_rows, width), low),
-            vmem((weight_rows, model), low),
-            vmem((8, padded), full),
-            vmem((groups, pieces, 8, padded), full),
-            vmem((HD, HD), full),
-        ]
-        + [DMA] * 4
-        + swap_scratch(pieces)
-        + [DMA((groups,))] * 2
-        + swap_scratch(pieces)
-        + [DMA((pieces, groups))] * 2
-        + [DMA((1, groups))] * 2
-        + gather_scratch(pieces, parts),
-        compiler_params=pltpu.CompilerParams(
-            collective_id=number, has_side_effects=True, vmem_limit_bytes=60 << 20
-        ),
-        name=f"opening_{number}",
-    )(hidden, norm_gains.reshape(1, gains), *weights)
-
-
 def lanes(start, size):
     return pl.ds(pl.multiple_of(start, 128), size)
 
@@ -943,18 +704,25 @@
     lax.fori_loop(0, half // tile, late, 0)
 
 
-def attend_kernel(
+def forward_kernel(
     shape,
-    raw,
+    hidden,
+    gains_ref,
+    query_weight,
+    key_weight,
+    value_weight,
+    gate_weight_t,
+    out_weight,
     cosine,
     sine,
-    gains,
     prefix_ref,
-    out_low,
-    hidden,
     out_grad,
     gate_weight,
     up_weight,
+    normed,
+    attn_low,
+    gains_out,
+    out_low,
     raw_t,
     gate_t,
     q_ref,
@@ -969,23 +737,174 @@
     normed_two,
     og_all,
     ff_low,
+    raw,
+    hidden_all,
+    blocks,
+    out_block,
+    gains_row,
+    gains_all,
+    corner,
     vt_ref,
     gated,
-    blocks,
-    own_sem,
+    ff_blocks,
+    own_attn,
+    own_out,
+    out_s,
+    out_r,
+    ff_sem,
     og_sem,
-    swap_s,
-    swap_r,
-    share_s,
-    share_r,
+    ga_s,
+    ga_r,
+    gs_s,
+    gs_r,
+    at_s,
+    at_r,
+    as_s,
+    as_r,
+    os_s,
+    os_r,
+    fs_s,
+    fs_r,
+    fh_s,
+    fh_r,
     *sems,
 ):
     pieces, groups, heads, kv_heads, ff_block = shape
-    gather_sems, scatter_refs = sems[:6], sems[6:]
+    rows_sems, og_sems, scatter_refs = sems[:6], sems[6:12], sems[12:]
     line = Line(pieces)
     me, group = line.me, lax.axis_index("seq")
-    length, rows = raw.shape[0], hidden.shape[0]
-    greet(others("ctx", pieces) + others("seq", groups))
+    rows, model = hidden.shape
+    length = pieces * rows
+    weight_rows = out_weight.shape[0]
+    q_width, kv_width = heads * HD, kv_heads * HD
+    copies = max(1, pieces // KV)
+    spread = Spread(groups, pieces)
+    greet(others("ctx", pieces) + others("seq", groups) + spread.peers())
+    gain_count = gains_ref.shape[1]
+    gains_row[...] = jnp.zeros(gains_row.shape, full)
+    gains_row[0:1, pl.ds(0, gain_count)] = gains_ref[...].astype(low).astype(full)
+    gains_all[group, me] = gains_row[...]
+    gain_swap = LineSwap(
+        line, lambda peer: gains_row, lambda source: gains_all.at[group, source], ga_s, ga_r
+    )
+    gain_swap.start()
+
+    blocks[:, :, pl.ds(q_width + 2 * kv_width, HD)] = jnp.zeros((pieces, weight_rows, HD), low)
+    corner[...] = jnp.zeros(corner.shape, full)
+    corner[pl.ds(0, gate_weight_t.shape[0]), pl.ds(0, weight_rows)] = gate_weight_t[...]
+    gate_rows = corner[...].T
+    for piece in range(pieces):
+        blocks[piece, :, pl.ds(0, q_width)] = query_weight[
+            :, pl.ds(piece * q_width, q_width)
+        ].astype(low)
+        start = piece // copies * kv_width
+        blocks[piece, :, pl.ds(q_width, kv_width)] = key_weight[:, pl.ds(start, kv_width)].astype(low)
+        blocks[piece, :, pl.ds(q_width + kv_width, kv_width)] = value_weight[
+            :, pl.ds(start, kv_width)
+        ].astype(low)
+        blocks[piece, :, pl.ds(q_width + 2 * kv_width, heads)] = gate_rows[
+            :weight_rows, piece * heads : (piece + 1) * heads
+        ].astype(low)
+
+    def place(index, source):
+        start = pl.multiple_of((index * pieces + source) * weight_rows, weight_rows)
+        return attn_low.at[pl.ds(start, weight_rows)]
+
+    attn_swap = LineSwap(
+        line, lambda peer: blocks.at[peer], lambda source: place(group, source), at_s, at_r
+    )
+    attn_swap.start()
+    share = Share(groups, place, as_s, as_r, False)
+    share.send(me, blocks.at[me])
+    attn_own = pltpu.make_async_copy(blocks.at[me], place(group, me), own_attn)
+    attn_own.start()
+    gather = Gather(line, 2, rows, hidden_all, rows_sems)
+    gather.start(hidden)
+    hidden_all[pl.ds(pl.multiple_of(me * rows, rows), rows), :] = hidden[...]
+    out_block[...] = out_weight[...].astype(low)
+
+    def out_place(index):
+        return out_low.at[pl.ds(pl.multiple_of(index * weight_rows, weight_rows), weight_rows)]
+
+    out_move = spread.copy(out_block, out_place(spread.use[0]), out_s, out_r, False)
+    out_stay = pltpu.make_async_copy(out_block, out_place(group), own_out)
+
+    @pl.when(spread.moves)
+    def _():
+        out_move.start()
+
+    @pl.when(jnp.logical_not(spread.moves))
+    def _():
+        out_stay.start()
+
+    def to_groups(shift):
+        peer = lax.rem(group + shift, groups)
+        return remote(
+            gains_all.at[group], gains_all.at[group], gs_s.at[shift], gs_r.at[shift], "seq", peer
+        )
+
+    def from_groups(shift):
+        peer = lax.rem(group + groups - shift, groups)
+        return remote(
+            gains_all.at[peer], gains_all.at[peer], gs_s.at[shift], gs_r.at[shift], "seq", peer
+        )
+
+    attn_swap.receive(0, share.send)
+    for far in range(line.chips):
+        gain_swap.receive(far, lambda source: None)
+    for shift in range(1, groups):
+        to_groups(shift).start()
+    if line.chips > 1:
+        attn_swap.receive(1, share.send)
+
+    def chip_rows(chip):
+        return chip * 2 * rows
+
+    def both(far, body):
+        if far == 0:
+            body(chip_rows(line.chip))
+            return
+
+        @pl.when(line.chip - far >= 0)
+        def _():
+            body(chip_rows(line.chip - far))
+
+        @pl.when(line.chip + far < line.chips)
+        def _():
+            body(chip_rows(line.chip + far))
+
+    def normalise(start):
+        def some(part):
+            across = pl.ds(pl.multiple_of(start + part.start, part.size), part.size)
+            values = hidden_all[across, :].astype(full)
+            inverse = lax.rsqrt(jnp.mean(values * values, axis=-1, keepdims=True) + epsilon)
+            normed[across, :] = (values * inverse * gains_out[0:1, pl.ds(0, model)]).astype(low)
+
+        by_rows(2 * rows, some)
+
+    def project(start):
+        across = pl.ds(pl.multiple_of(start, 2 * rows), 2 * rows)
+        raw[across, :] = product(normed[across, :], attn_low[...])
+
+    for far in range(2, line.chips):
+        attn_swap.receive(far, share.send)
+    out_share = Share(groups, lambda index, source: out_place(index), os_s, os_r)
+
+    @pl.when(spread.moves)
+    def _():
+        spread.copy(out_place(group), out_place(group), out_s, out_r, False).wait_recv()
+
+    @pl.when(jnp.logical_not(spread.moves))
+    def _():
+        out_stay.wait()
+
+    out_share.send(0)
+    for shift in range(1, groups):
+        from_groups(shift).wait_recv()
+    for index in range(groups * pieces):
+        gains_out[0:1, pl.ds(index * gain_count, gain_count)] = gains_all[
+            index // pieces, index % pieces, 0:1, pl.ds(0, gain_count)
+        ]
     own_width = groups * ff_block
 
     def prepare(across):
@@ -993,22 +912,41 @@
             for index in range(groups):
                 for piece in range(pieces):
                     start = (index * pieces + piece) * ff_block
-                    blocks[piece, across, pl.ds(half * own_width + index * ff_block, ff_block)] = (
+                    ff_blocks[piece, across, pl.ds(half * own_width + index * ff_block, ff_block)] = (
                         weight_ref[across, pl.ds(start, ff_block)].astype(low)
                     )
 
     by_rows(gate_weight.shape[0], prepare, 16)
-    swap = LineSwap(
-        line, lambda peer: blocks.at[peer], lambda source: ff_low.at[group, source], swap_s, swap_r
+    for hop in range(1, line.chips - 1):
+        gather.forward(hop)
+        gather.arrive(hop - 1)
+        both(hop - 1, normalise)
+    ff_swap = LineSwap(
+        line, lambda peer: ff_blocks.at[peer], lambda source: ff_low.at[group, source], fs_s, fs_r
     )
-    swap.start()
-    share = Share(groups, lambda index, source: ff_low.at[index, source], share_s, share_r, False)
-    share.send(me, blocks.at[me])
-    own = pltpu.make_async_copy(blocks.at[me], ff_low.at[group, me], own_sem)
-    own.start()
+    ff_swap.start()
+    ff_share = Share(groups, lambda index, source: ff_low.at[index, source], fh_s, fh_r, False)
+    ff_share.send(me, ff_blocks.at[me])
+    ff_own = pltpu.make_async_copy(ff_blocks.at[me], ff_low.at[group, me], ff_sem)
+    ff_own.start()
+    gather.arrive(line.chips - 2)
+    both(line.chips - 2, normalise)
+    attn_own.wait()
+    out_share.relay(0)
+    share.finish(pieces)
+    for far in range(line.chips - 1):
+        both(far, project)
+    gather.forward(line.chips - 1)
+    gather.arrive(line.chips - 1)
+    both(line.chips - 1, normalise)
+    both(line.chips - 1, project)
+    og_gather = Gather(line, 2, rows, og_all, og_sems)
+    og_gather.start(out_grad)
+    start = pl.multiple_of(me * rows, rows)
+    og_own = pltpu.make_async_copy(out_grad, og_all.at[pl.ds(start, rows)], og_sem)
+    og_own.start()
     prefix = prefix_ref[0, 0]
-    model = hidden.shape[1]
-    query_gain, key_gain = column(gains, 2 * model), column(gains, 2 * model + HD)
+    query_gain, key_gain = column(gains_out, 2 * model), column(gains_out, 2 * model + HD)
     scale = HD ** (-0.5)
     for head in range(heads + kv_heads):
         part = pl.ds(head * HD, HD)
@@ -1029,7 +967,7 @@
         v_ref[:, part] = values.astype(low)
         vt_ref[part, :] = values.T.astype(low)
     gate_t[...] = raw[:, pl.ds((heads + 2 * kv_heads) * HD, HD)].T[: gate_t.shape[0]]
-    swap.receive(0, share.send)
+    ff_swap.receive(0, ff_share.send)
     for head in range(heads):
         part = pl.ds(head * HD, HD)
         kv_part = pl.ds(head * kv_heads // heads * HD, HD)
@@ -1051,9 +989,9 @@
         gated_t[part, :] = scaled.astype(low)
         gated[:, part] = scaled.T.astype(low)
         if head == 0 and line.chips > 1:
-            swap.receive(1, share.send)
-
-    gather = Gather(line, 2, rows, og_all, gather_sems)
+            ff_swap.receive(1, ff_share.send)
+
+    out_share.finish(1)
     scatter = Scatter(line, rows, scatter_refs)
     scatter.clear()
     block = blocks_nn(gated, out_low, rows)
@@ -1061,10 +999,6 @@
     for far, side in scatter.order():
         if far == last:
             scatter.fill(far, side, block)
-    gather.start(out_grad)
-    start = pl.multiple_of(me * rows, rows)
-    og_own = pltpu.make_async_copy(out_grad, og_all.at[pl.ds(start, rows)], og_sem)
-    og_own.start()
     for far, side in scatter.order():
         if far == last:
             scatter.push(far, side)
@@ -1072,38 +1006,56 @@
         if far < last:
             scatter.fill(far, side, block)
     for far in range(2, line.chips):
-        swap.receive(far, share.send)
+        ff_swap.receive(far, ff_share.send)
     for hop in range(1, line.chips):
+        og_gather.forward(hop)
         for far, side in scatter.order():
             if far == last - hop and far > 0:
                 scatter.push(far, side)
-        gather.forward(hop)
     scatter.total(middle)
 
-    def normalise(across):
+    def normalise_two(across):
         values = hidden[across, :].astype(full) + middle[across, :]
         middle[across, :] = values
         inverse = lax.rsqrt(jnp.mean(values * values, axis=-1, keepdims=True) + epsilon)
-        normed_two[across, :] = (values * inverse * gains[:, pl.ds(model, model)]).astype(low)
-
-    by_rows(rows, normalise)
+        normed_two[across, :] = (values * inverse * gains_out[:, pl.ds(model, model)]).astype(low)
+
+    by_rows(rows, normalise_two)
     og_own.wait()
-    own.wait()
-    gather.complete()
+    ff_own.wait()
+    og_gather.complete()
     scatter.finish()
-    swap.finish()
-    share.finish(pieces)
-
-
-def attend(raw, tables, gains, prefix, out_low, hidden, out_grad, weights, shape, number):
+    ff_swap.finish()
+    ff_share.finish(pieces)
+    gather.finish()
+    gain_swap.finish()
+    attn_swap.finish()
+    for shift in range(1, groups):
+        to_groups(shift).wait_send()
+
+    @pl.when(spread.moves)
+    def _():
+        out_move.wait_send()
+
+
+def forward(hidden, norm_gains, weights, tables, prefix, out_grad, ff_weights, shape, number):
     pieces, groups, heads, kv_heads, ff_block = shape
-    length, rows, model = raw.shape[0], hidden.shape[0], hidden.shape[1]
+    rows, model = hidden.shape
+    length = pieces * rows
+    weight_rows = weights[0].shape[0]
+    gains = norm_gains.shape[0]
+    padded = -(-gains // 128) * 128
     q_width, kv_width = heads * HD, kv_heads * HD
-    weight_rows = weights[0].shape[0]
-    struct = jax.ShapeDtypeStruct
+    width = (heads + 2 * kv_heads + 1) * HD
+    ff_shape = (pieces, weight_rows, 2 * groups * ff_block)
+    struct, vmem = jax.ShapeDtypeStruct, pltpu.VMEM
     return pl.pallas_call(
-        functools.partial(attend_kernel, shape),
+        functools.partial(forward_kernel, shape),
         out_shape=(
+            struct((length, model), low),
+            struct((model, width), low),
+            struct((1, groups * pieces * gains), full),
+            struct((groups * weight_rows, model), low),
             struct((q_width + kv_width, length), full),
             struct((8, length), full),
             struct((length, q_width), low),
@@ -1117,26 +1069,39 @@
             struct((rows, model), full),
             struct((rows, model), low),
             struct((length, model), low),
-            struct((groups, pieces, weight_rows, 2 * groups * ff_block), low),
+            struct((groups,) + ff_shape, low),
         ),
-        in_specs=[IN_VMEM] * 4 + [pl.BlockSpec(memory_space=pltpu.SMEM)] + [IN_VMEM] * 5,
-        out_specs=(IN_VMEM,) * 12 + (ANY, ANY),
+        in_specs=[IN_VMEM] * 9 + [pl.BlockSpec(memory_space=pltpu.SMEM)] + [IN_VMEM] * 3,
+        out_specs=(IN_VMEM,) * 16 + (ANY, ANY),
         scratch_shapes=[
-            pltpu.VMEM((kv_width, length), low),
-            pltpu.VMEM((length, q_width), low),
-            pltpu.VMEM((pieces, weight_rows, 2 * groups * ff_block), low),
-            DMA,
-            DMA,
+            vmem((length, width), full),
+            vmem((length, model), low),
+            vmem((pieces, weight_rows, width), low),
+            vmem((weight_rows, model), low),
+            vmem((8, padded), full),
+            vmem((groups, pieces, 8, padded), full),
+            vmem((HD, HD), full),
+            vmem((kv_width, length), low),
+            vmem((length, q_width), low),
+            vmem(ff_shape, low),
         ]
+        + [DMA] * 6
+        + swap_scratch(pieces)
+        + [DMA((groups,))] * 2
         + swap_scratch(pieces)
         + [DMA((pieces, groups))] * 2
-        + gather_scratch(pieces, 2)
+        + [DMA((1, groups))] * 2
+        + swap_scratch(pieces)
+        + [DMA((pieces, groups))] * 2
+        + gather_scratch(pieces, 2) * 2
         + scatter_scratch(pieces, rows, model),
         compiler_params=pltpu.CompilerParams(
-            collective_id=number, has_side_effects=True, vmem_limit_bytes=60 << 20
+            collective_id=number, has_side_effects=True, vmem_limit_bytes=67043328
         ),
-        name=f"attend_{number}",
-    )(raw, *tables, gains, prefix, out_low, hidden, out_grad, *weights)
+        name=f"forward_{number}",
+    )(
+        hidden, norm_gains.reshape(1, gains), *weights, *tables, prefix, out_grad, *ff_weights,
+    )
 
 
 def attend_back_kernel(
@@ -2000,29 +1965,23 @@
     ff_own = ff_block * groups
     gain_count = norm_gains.shape[0]
     shape = (pieces, groups, heads, kv_heads, ff_block)
-    normed, raw, attn_low, gains_full, out_low = opening(
-        hidden_in,
-        norm_gains,
-        (query_weight, key_weight, value_weight, head_gate_weight.T, out_weight),
-        shape,
-        0,
-    )
     inverse = rope_base ** (-jnp.arange(HD // 2, dtype=full) * 2.0 / HD)
     angles = inverse[:, None] * jnp.arange(length, dtype=jnp.int32).astype(full)[None, :]
     tables = (jnp.cos(angles), jnp.sin(angles))
     prefix = prefix_len.reshape(1, 1)
 
-    *saved, gated_t, middle, normed_two, out_grad_all, ff_low = attend(
-        raw,
+    (
+        normed, attn_low, gains_full, out_low, *saved, gated_t, middle, normed_two, out_grad_all, ff_low
+    ) = forward(
+        hidden_in,
+        norm_gains,
+        (query_weight, key_weight, value_weight, head_gate_weight.T, out_weight),
         tables,
-        gains_full,
         prefix,
-        out_low,
-        hidden_in,
         out_grad,
         (gate_weight, up_weight),
         shape,
-        1,
+        0,
     )
     ff_low = ff_low.reshape(model, 2 * ff_own)
     n2_all, hidden_ff, grad_pre, down_low = feed(

time: 453 us -> 433 us (0.956)
  the two profiles are of different devices: /device:TPU:3 before, /device:TPU:1 now
where the time goes in v6:
time: 433 us; the launch traced here: 425 us
  Pallas kernels  421 us (97%)
    pallas_call x1, Pallas kernels, forward(): pl.pallas_call(functools.partial(forward_kernel, shape), out_shape=(struc...  150 us
    pallas_call x1, Pallas kernels, feed_back(): pl.pallas_call(functools.partial(feed_back_kernel, shape), out_shape=(str...  111 us
    pallas_call x1, Pallas kernels, attend_back(): pl.pallas_call(functools.partial(attend_back_kernel, shape), out_shape=(s...  98.3 us
    pallas_call x1, Pallas kernels, feed(): pl.pallas_call(functools.partial(feed_kernel, shape), out_shape=(struct((...  55.9 us

profile of v6, /device:TPU:1, one launch (start us, length us, event | category | flops | bytes accessed | tf_op | source)
XLA Modules:
  0.0 424.9 jit_solution(1837162312334566647)
XLA Ops:
  1.3 1.8 multiply_sine_fusion
  3.1 149.9 %forward_0.1 = (bf16[1024,2048]{1,0:T(8,128)(2,1)}, bf16[2048,640]{1,0:T(8,128)(2,1)}, f32[1,4352]{1,0:T(1,128)}, bf16[256,2048]{1,0:T(8,128)(2,1)}, f32[384,102...) custom-call(bf16[128,2048]{1,0:T(8,128)(2,1)} %hidden.3, ...), custom_call_target="tpu_custom_call" | custom-call | tf_op jit(solution)/shard_map/forward_0/pallas_call | solution.py:1052
  153.0 55.9 %feed_2.1 = (bf16[1024,2048]{1,0:T(8,128)(2,1)}, bf16[1024,768]{1,0:T(8,128)(2,1)}, bf16[1024,1536]{1,0:T(8,128)(2,1)}, bf16[768,2048]{1,0:T(8,128)(2,1)}) custom-call(bf16[128,2048]{1,0:T(8,128)(2,1)} %get-tuple-element.60.normed_two, bf16[2048,1536]{1,0:T(8,128)(2,1)} %bitcast.8, f32[192,2048]{1,0:T(8,128)} %down_weight.1, ...), custom_call_target="tpu_custom_call" | custom-call | tf_op jit(solution)/shard_map/feed_2/pallas_call | solution.py:1688
  209.0 111.4 %feed_back_3.1 = (bf16[1024,2048]{1,0:T(8,128)(2,1)}, f32[128,2048]{1,0:T(8,128)}, f32[1,2048]{1,0:T(1,128)}, bf16[128,2048]{1,0:T(8,128)(2,1)}, bf16[8,64,1536]...) custom-call(bf16[1024,1536]{1,0:T(8,128)(2,1)} %get-tuple-element.63.grad_pre, bf16[2048,1536]{1,0:T(8,128)(2,1)} %bitcast.9, ...), custom_call_target="tpu_custom_call" | custom-call | tf_op jit(solution)/shard_map/feed_back_3/pallas_call | solution.py:1887
  320.4 98.3 %attend_back_4.1 = (bf16[128,2048]{1,0:T(8,128)(2,1)}, f32[1,136]{1,0:T(1,128)}, bf16[64,2048]{1,0:T(8,128)(2,1)}, f32[64,1024]{1,0:T(8,128)}, f32[64,1024]{1,0:...) custom-call(bf16[1024,2048]{1,0:T(8,128)(2,1)} %get-tuple-element.70, ...), custom_call_target="tpu_custom_call" | custom-call | tf_op jit(solution)/shard_map/attend_back_4/pallas_call | solution.py:1523
  418.7 5.7 %widen.1 = (bf16[128,2048]{1,0:T(8,128)(2,1)}, bf16[128,2048]{1,0:T(8,128)(2,1)}, f32[64,2048]{1,0:T(8,128)}, f32[64,1024]{1,0:T(8,128)}, f32[64,1024]{1,0:T(8,1...) custom-call(bf16[128,2048]{1,0:T(8,128)(2,1)} %get-tuple-element.69., ...), custom_call_target="tpu_custom_call" | custom-call | tf_op jit(solution)/shard_map/widen/pallas_call | solution.py:1931
  (2 shorter events, 0.0 us)

commit v7 on v6

--- a/solution.py
+++ b/solution.py
@@ -316,19 +316,26 @@
             for side in range(2 if far else 1)
         ]
 
-    def fill(self, far, side, block):
-        @pl.when(self.there(far, side))
-        def _():
-            target = self.target(far, side)
-
-            def store(columns, value):
-                first, second = value[: self.rows], value[self.rows :]
-                mine = self.line.core == 0
-                self.own[target, :, columns] = jnp.where(mine, first, second).astype(low)
-                self.give[target, :, columns] = jnp.where(mine, second, first).astype(low)
-
-            block(target, store)
-            self.exchange(target).start()
+    def fill(self, least, most, block):
+        line = self.line
+
+        def step(target, unused):
+            far = jnp.abs(target - line.chip)
+
+            @pl.when(jnp.logical_and(far >= least, far <= most))
+            def _():
+                def store(columns, value):
+                    first, second = value[: self.rows], value[self.rows :]
+                    mine = line.core == 0
+                    self.own[target, :, columns] = jnp.where(mine, first, second).astype(low)
+                    self.give[target, :, columns] = jnp.where(mine, second, first).astype(low)
+
+                block(target, store)
+                self.exchange(target).start()
+
+            return unused
+
+        lax.fori_loop(0, line.chips, step, 0)
 
     def push(self, far, side):
         line = self.line
@@ -882,9 +889,18 @@
 
         by_rows(2 * rows, some)
 
-    def project(start):
-        across = pl.ds(pl.multiple_of(start, 2 * rows), 2 * rows)
-        raw[across, :] = product(normed[across, :], attn_low[...])
+    def project(least, most):
+        def step(chip, unused):
+            far = jnp.abs(chip - line.chip)
+
+            @pl.when(jnp.logical_and(far >= least, far <= most))
+            def _():
+                across = pl.ds(pl.multiple_of(chip * 2 * rows, 2 * rows), 2 * rows)
+                raw[across, :] = product(normed[across, :], attn_low[...])
+
+            return unused
+
+        lax.fori_loop(0, line.chips, step, 0)
 
     for far in range(2, line.chips):
         attn_swap.receive(far, share.send)
@@ -934,12 +950,11 @@
     attn_own.wait()
     out_share.relay(0)
     share.finish(pieces)
-    for far in range(line.chips - 1):
-        both(far, project)
+    project(0, line.chips - 2)
     gather.forward(line.chips - 1)
     gather.arrive(line.chips - 1)
     both(line.chips - 1, normalise)
-    both(line.chips - 1, project)
+    project(line.chips - 1, line.chips - 1)
     og_gather = Gather(line, 2, rows, og_all, og_sems)
     og_gather.start(out_grad)
     start = pl.multiple_of(me * rows, rows)
@@ -996,15 +1011,11 @@
     scatter.clear()
     block = blocks_nn(gated, out_low, rows)
     last = line.chips - 1
-    for far, side in scatter.order():
-        if far == last:
-            scatter.fill(far, side, block)
+    scatter.fill(last, last, block)
     for far, side in scatter.order():
         if far == last:
             scatter.push(far, side)
-    for far, side in scatter.order():
-        if far < last:
-            scatter.fill(far, side, block)
+    scatter.fill(0, last - 1, block)
     for far in range(2, line.chips):
         ff_swap.receive(far, ff_share.send)
     for hop in range(1, line.chips):
@@ -1319,9 +1330,7 @@
     last = line.chips - 1
 
     def fills(far):
-        for distance, side in scatter.order():
-            if distance == far:
-                scatter.fill(far, side, block)
+        scatter.fill(far, far, block)
 
     def pushes(far):
         for distance, side in scatter.order():
@@ -1619,7 +1628,7 @@
         down_block[across, :] = down_weight[across, :].astype(low)
 
     by_rows(block_rows, narrow, 16)
-    share = Share(groups, place, share_s, share_r, False)
+    share = Share(groups, place, share_s, share_r)
     share.send(0, down_block)
     down_low[pl.ds(pl.multiple_of(group * block_rows, block_rows), block_rows), :] = down_block[...]
 
@@ -1635,6 +1644,32 @@
 
         lax.fori_loop(0, own_width // tile, step, 0)
 
+    def swiglu(least, most):
+        def rows_of(chip, unused):
+            far = jnp.abs(chip - line.chip)
+            across = pl.ds(pl.multiple_of(chip * 2 * rows, 2 * rows), 2 * rows)
+
+            def step(column, unused):
+                first, second = lanes(column * tile, tile), lanes(own_width + column * tile, tile)
+                grads = product_nt(og_all[across, :], down_low[lanes(column * tile, tile), :])
+                gate, up = before[across, first], before[across, second]
+                sigmoid = jax.nn.sigmoid(gate)
+                silu = gate * sigmoid
+                hidden_ff[across, first] = (silu * up).astype(low)
+                grad_pre[across, first] = (
+                    grads * up * (sigmoid * (1.0 + gate * (1.0 - sigmoid)))
+                ).astype(low)
+                grad_pre[across, second] = (grads * silu).astype(low)
+                return unused
+
+            @pl.when(jnp.logical_and(far >= least, far <= most))
+            def _():
+                lax.fori_loop(0, own_width // tile, step, 0)
+
+            return unused
+
+        lax.fori_loop(0, line.chips, rows_of, 0)
+
     def compute(far):
         gather.arrive(far)
         if far == 0:
@@ -1652,31 +1687,15 @@
     for hop in range(1, line.chips - 1):
         gather.forward(hop)
         compute(hop - 1)
+        if hop == 1:
+            share.relay(0)
     if line.chips > 1:
         compute(line.chips - 2)
+        share.finish(1)
+        swiglu(0, line.chips - 2)
         gather.forward(line.chips - 1)
     compute(line.chips - 1)
-    share.finish(1)
-
-    def swiglu(index, unused):
-        across = pl.ds(pl.multiple_of(index * 256, 256), 256)
-
-        def step(column, unused):
-            first, second = lanes(column * tile, tile), lanes(own_width + column * tile, tile)
-            grads = product_nt(og_all[across, :], down_low[lanes(column * tile, tile), :])
-            gate, up = before[across, first], before[across, second]
-            sigmoid = jax.nn.sigmoid(gate)
-            silu = gate * sigmoid
-            hidden_ff[across, first] = (silu * up).astype(low)
-            grad_pre[across, first] = (
-                grads * up * (sigmoid * (1.0 + gate * (1.0 - sigmoid)))
-            ).astype(low)
-            grad_pre[across, second] = (grads * silu).astype(low)
-            return unused
-
-        return lax.fori_loop(0, own_width // tile, step, unused)
-
-    lax.fori_loop(0, length // 256, swiglu, 0)
+    swiglu(line.chips - 1, line.chips - 1)
     gather.finish()
 
 
@@ -1754,9 +1773,7 @@
     last = line.chips - 1
 
     def fills(scatter, far, block):
-        for distance, side in scatter.order():
-            if distance == far:
-                scatter.fill(far, side, block)
+        scatter.fill(far, far, block)
 
     def pushes(scatter, far):
         for distance, side in scatter.order():

time: 433 us -> 421 us (0.972); the launches traced: 425 us -> 420 us
    pallas_call x1, Pallas kernels: 55.9 us -> 51.5 us  [feed(): pl.pallas_call(functools.partial(feed_kernel, shape), out_shape=(struct((...]
where the time goes in v7:
time: 421 us; the launch traced here: 420 us
  Pallas kernels  417 us (99%)
    pallas_call x1, Pallas kernels, forward(): pl.pallas_call(functools.partial(forward_kernel, shape), out_shape=(struc...  150 us
    pallas_call x1, Pallas kernels, feed_back(): pl.pallas_call(functools.partial(feed_back_kernel, shape), out_shape=(str...  114 us
    pallas_call x1, Pallas kernels, attend_back(): pl.pallas_call(functools.partial(attend_back_kernel, shape), out_shape=(s...  96.4 us
    pallas_call x1, Pallas kernels, feed(): pl.pallas_call(functools.partial(feed_kernel, shape), out_shape=(struct((...  51.5 us

profile of v7, /device:TPU:1, one launch (start us, length us, event | category | flops | bytes accessed | tf_op | source)
XLA Modules:
  0.0 420.4 jit_solution(5939037284503537044)
XLA Ops:
  1.3 1.8 multiply_sine_fusion
  3.1 149.9 %forward_0.1 = (bf16[1024,2048]{1,0:T(8,128)(2,1)}, bf16[2048,640]{1,0:T(8,128)(2,1)}, f32[1,4352]{1,0:T(1,128)}, bf16[256,2048]{1,0:T(8,128)(2,1)}, f32[384,102...) custom-call(bf16[128,2048]{1,0:T(8,128)(2,1)} %hidden.3, ...), custom_call_target="tpu_custom_call" | custom-call | tf_op jit(solution)/shard_map/forward_0/pallas_call | solution.py:1063
  153.1 51.5 %feed_2.1 = (bf16[1024,2048]{1,0:T(8,128)(2,1)}, bf16[1024,768]{1,0:T(8,128)(2,1)}, bf16[1024,1536]{1,0:T(8,128)(2,1)}, bf16[768,2048]{1,0:T(8,128)(2,1)}) custom-call(bf16[128,2048]{1,0:T(8,128)(2,1)} %get-tuple-element.60.normed_two, bf16[2048,1536]{1,0:T(8,128)(2,1)} %bitcast.8, f32[192,2048]{1,0:T(8,128)} %down_weight.1, ...), custom_call_target="tpu_custom_call" | custom-call | tf_op jit(solution)/shard_map/feed_2/pallas_call | solution.py:1707
  204.6 113.5 %feed_back_3.1 = (bf16[1024,2048]{1,0:T(8,128)(2,1)}, f32[128,2048]{1,0:T(8,128)}, f32[1,2048]{1,0:T(1,128)}, bf16[128,2048]{1,0:T(8,128)(2,1)}, bf16[8,64,1536]...) custom-call(bf16[1024,1536]{1,0:T(8,128)(2,1)} %get-tuple-element.63.grad_pre, bf16[2048,1536]{1,0:T(8,128)(2,1)} %bitcast.9, ...), custom_call_target="tpu_custom_call" | custom-call | tf_op jit(solution)/shard_map/feed_back_3/pallas_call | solution.py:1904
  318.1 96.4 %attend_back_4.1 = (bf16[128,2048]{1,0:T(8,128)(2,1)}, f32[1,136]{1,0:T(1,128)}, bf16[64,2048]{1,0:T(8,128)(2,1)}, f32[64,1024]{1,0:T(8,128)}, f32[64,1024]{1,0:...) custom-call(bf16[1024,2048]{1,0:T(8,128)(2,1)} %get-tuple-element.70, ...), custom_call_target="tpu_custom_call" | custom-call | tf_op jit(solution)/shard_map/attend_back_4/pallas_call | solution.py:1532
  414.5 5.7 %widen.1 = (bf16[128,2048]{1,0:T(8,128)(2,1)}, bf16[128,2048]{1,0:T(8,128)(2,1)}, f32[64,2048]{1,0:T(8,128)}, f32[64,1024]{1,0:T(8,128)}, f32[64,1024]{1,0:T(8,1...) custom-call(bf16[128,2048]{1,0:T(8,128)(2,1)} %get-tuple-element.69., ...), custom_call_target="tpu_custom_call" | custom-call | tf_op jit(solution)/shard_map/widen/pallas_call | solution.py:1948
  (2 shorter events, 0.0 us)

commit v8 on v7

--- a/solution.py
+++ b/solution.py
@@ -242,7 +242,7 @@
 def scatter_scratch(pieces, rows, width):
     chips = pieces // 2
     slots = pltpu.VMEM((chips, rows, width), low)
-    return [slots] * 3 + [pltpu.VMEM((chips + 1, rows, width), low)] + [DMA((chips,))] * 6
+    return [slots] * 3 + [pltpu.VMEM((chips + 1, rows, width), low)] + [DMA((chips,))] * 2 + [DMA((chips, 2))] * 4
 
 
 class Scatter:
@@ -289,22 +289,26 @@
             self.line.sibling,
         )
 
-    def send(self, target, side):
+    def part(self, which):
+        return pl.ds(which * (self.rows // 2), self.rows // 2)
+
+    def send(self, target, side, which):
+        part = self.part(which)
         if side == 0:
             return remote(
-                self.own.at[target],
-                self.arrived.at[target],
-                self.r_send.at[target],
-                self.r_recv.at[target],
+                self.own.at[target, part],
+                self.arrived.at[target, part],
+                self.r_send.at[target, which],
+                self.r_recv.at[target, which],
                 "ctx",
                 self.line.right,
             )
         chips, chip = self.line.chips, self.line.chip
         return remote(
-            self.own.at[target],
-            self.arrived.at[jnp.where(target == chip - 1, chips, target)],
-            self.l_send.at[target],
-            self.l_recv.at[target],
+            self.own.at[target, part],
+            self.arrived.at[jnp.where(target == chip - 1, chips, target), part],
+            self.l_send.at[target, which],
+            self.l_recv.at[target, which],
             "ctx",
             self.line.left,
         )
@@ -346,32 +350,38 @@
             target = self.target(far, side)
             self.exchange(target).wait_recv()
 
-            def add(across):
-                self.own[target, across, :] = (
-                    self.own[target, across, :].astype(full) + self.sib[target, across, :].astype(full)
-                ).astype(low)
-
-            def add_all(across):
-                self.own[target, across, :] = (
-                    self.own[target, across, :].astype(full)
-                    + self.sib[target, across, :].astype(full)
-                    + self.arrived[target, across, :].astype(full)
-                ).astype(low)
-
-            if far == line.chips - 1:
-                by_rows(self.rows, add)
-            else:
-
-                @pl.when(behind)
-                def _():
-                    self.send(target, side).wait_recv()
-                    by_rows(self.rows, add_all)
-
-                @pl.when(jnp.logical_not(behind))
-                def _():
-                    by_rows(self.rows, add)
-
-            self.send(target, side).start()
+            for which in range(2):
+                first = which * (self.rows // 2)
+
+                def add(part):
+                    across = pl.ds(pl.multiple_of(first + part.start, part.size), part.size)
+                    self.own[target, across, :] = (
+                        self.own[target, across, :].astype(full)
+                        + self.sib[target, across, :].astype(full)
+                    ).astype(low)
+
+                def add_all(part):
+                    across = pl.ds(pl.multiple_of(first + part.start, part.size), part.size)
+                    self.own[target, across, :] = (
+                        self.own[target, across, :].astype(full)
+                        + self.sib[target, across, :].astype(full)
+                        + self.arrived[target, across, :].astype(full)
+                    ).astype(low)
+
+                if far == line.chips - 1:
+                    by_rows(self.rows // 2, add)
+                else:
+
+                    @pl.when(behind)
+                    def _():
+                        self.send(target, side, which).wait_recv()
+                        by_rows(self.rows // 2, add_all)
+
+                    @pl.when(jnp.logical_not(behind))
+                    def _():
+                        by_rows(self.rows // 2, add)
+
+                self.send(target, side, which).start()
 
     def total(self, total_ref):
         line = self.line
@@ -380,11 +390,13 @@
 
         @pl.when(line.has_left)
         def _():
-            self.send(chip, 0).wait_recv()
+            for which in range(2):
+                self.send(chip, 0, which).wait_recv()
 
         @pl.when(line.has_right)
         def _():
-            self.send(chip, 1).wait_recv()
+            for which in range(2):
+                self.send(chip, 1, which).wait_recv()
 
         def add(across):
             total = self.own[chip, across, :].astype(full) + self.sib[chip, across, :].astype(full)
@@ -405,7 +417,8 @@
                 target = self.target(far, side)
                 self.exchange(target).wait_send()
                 if far > 0:
-                    self.send(target, side).wait_send()
+                    for which in range(2):
+                        self.send(target, side, which).wait_send()
 
 
 def blocks_nn(left_ref, right_ref, rows, tile=512):

time: 421 us -> 418 us (level)
    pallas_call x1, Pallas kernels: 114 us -> 104 us  [feed_back(): pl.pallas_call(functools.partial(feed_back_kernel, shape), out_shape=(str...]
    pallas_call x1, Pallas kernels: 96.4 us -> 104 us  [attend_back(): pl.pallas_call(functools.partial(attend_back_kernel, shape), out_shape=(s...]
where the time goes in v8:
time: 418 us
  Pallas kernels  415 us (99%)
    pallas_call x1, Pallas kernels, forward(): pl.pallas_call(functools.partial(forward_kernel, shape), out_shape=(struc...  150 us
    pallas_call x1, Pallas kernels, feed_back(): pl.pallas_call(functools.partial(feed_back_kernel, shape), out_shape=(str...  104 us
    pallas_call x1, Pallas kernels, attend_back(): pl.pallas_call(functools.partial(attend_back_kernel, shape), out_shape=(s...  104 us
    pallas_call x1, Pallas kernels, feed(): pl.pallas_call(functools.partial(feed_kernel, shape), out_shape=(struct((...  51.4 us

profile of v8, /device:TPU:1, one launch (start us, length us, event | category | flops | bytes accessed | tf_op | source)
XLA Modules:
  0.0 418.2 jit_solution(1163270341722694583)
XLA Ops:
  1.3 1.8 multiply_sine_fusion
  3.1 150.2 %forward_0.1 = (bf16[1024,2048]{1,0:T(8,128)(2,1)}, bf16[2048,640]{1,0:T(8,128)(2,1)}, f32[1,4352]{1,0:T(1,128)}, bf16[256,2048]{1,0:T(8,128)(2,1)}, f32[384,102...) custom-call(bf16[128,2048]{1,0:T(8,128)(2,1)} %hidden.3, ...), custom_call_target="tpu_custom_call" | custom-call | tf_op jit(solution)/shard_map/forward_0/pallas_call | solution.py:1076
  153.3 51.4 %feed_2.1 = (bf16[1024,2048]{1,0:T(8,128)(2,1)}, bf16[1024,768]{1,0:T(8,128)(2,1)}, bf16[1024,1536]{1,0:T(8,128)(2,1)}, bf16[768,2048]{1,0:T(8,128)(2,1)}) custom-call(bf16[128,2048]{1,0:T(8,128)(2,1)} %get-tuple-element.60.normed_two, bf16[2048,1536]{1,0:T(8,128)(2,1)} %bitcast.8, f32[192,2048]{1,0:T(8,128)} %down_weight.1, ...), custom_call_target="tpu_custom_call" | custom-call | tf_op jit(solution)/shard_map/feed_2/pallas_call | solution.py:1720
  204.7 104.0 %feed_back_3.1 = (bf16[1024,2048]{1,0:T(8,128)(2,1)}, f32[128,2048]{1,0:T(8,128)}, f32[1,2048]{1,0:T(1,128)}, bf16[128,2048]{1,0:T(8,128)(2,1)}, bf16[8,64,1536]...) custom-call(bf16[1024,1536]{1,0:T(8,128)(2,1)} %get-tuple-element.63.grad_pre, bf16[2048,1536]{1,0:T(8,128)(2,1)} %bitcast.9, ...), custom_call_target="tpu_custom_call" | custom-call | tf_op jit(solution)/shard_map/feed_back_3/pallas_call | solution.py:1917
  308.7 103.6 %attend_back_4.1 = (bf16[128,2048]{1,0:T(8,128)(2,1)}, f32[1,136]{1,0:T(1,128)}, bf16[64,2048]{1,0:T(8,128)(2,1)}, f32[64,1024]{1,0:T(8,128)}, f32[64,1024]{1,0:...) custom-call(bf16[1024,2048]{1,0:T(8,128)(2,1)} %get-tuple-element.70, ...), custom_call_target="tpu_custom_call" | custom-call | tf_op jit(solution)/shard_map/attend_back_4/pallas_call | solution.py:1545
  412.3 5.7 %widen.1 = (bf16[128,2048]{1,0:T(8,128)(2,1)}, bf16[128,2048]{1,0:T(8,128)(2,1)}, f32[64,2048]{1,0:T(8,128)}, f32[64,1024]{1,0:T(8,128)}, f32[64,1024]{1,0:T(8,1...) custom-call(bf16[128,2048]{1,0:T(8,128)(2,1)} %get-tuple-element.69., ...), custom_call_target="tpu_custom_call" | custom-call | tf_op jit(solution)/shard_map/widen/pallas_call | solution.py:1961
  (2 shorter events, 0.0 us)

commit v9 on v8

--- a/solution.py
+++ b/solution.py
@@ -1029,13 +1029,16 @@
         if far == last:
             scatter.push(far, side)
     scatter.fill(0, last - 1, block)
-    for far in range(2, line.chips):
-        ff_swap.receive(far, ff_share.send)
+    if line.chips > 2:
+        ff_swap.receive(2, ff_share.send)
     for hop in range(1, line.chips):
         og_gather.forward(hop)
         for far, side in scatter.order():
             if far == last - hop and far > 0:
                 scatter.push(far, side)
+        if hop == 1:
+            for far in range(3, line.chips):
+                ff_swap.receive(far, ff_share.send)
     scatter.total(middle)
 
     def normalise_two(across):
@@ -1373,9 +1376,9 @@
         lax.fori_loop(0, share // 128, step, 0)
         fold.ready(job)
 
-    weight_grad(0)
     fills(last)
     pushes(last)
+    weight_grad(0)
     for job in range(1, groups):
         weight_grad(job)
         if job <= last:

time: 418 us -> 418 us (level)
  no operation moved by 1% of the time
where the time goes in v9:
time: 418 us
  Pallas kernels  415 us (99%)
    pallas_call x1, Pallas kernels, forward(): pl.pallas_call(functools.partial(forward_kernel, shape), out_shape=(struc...  150 us
    pallas_call x1, Pallas kernels, feed_back(): pl.pallas_call(functools.partial(feed_back_kernel, shape), out_shape=(str...  104 us
    pallas_call x1, Pallas kernels, attend_back(): pl.pallas_call(functools.partial(attend_back_kernel, shape), out_shape=(s...  104 us
    pallas_call x1, Pallas kernels, feed(): pl.pallas_call(functools.partial(feed_kernel, shape), out_shape=(struct((...  51.4 us

profile of v9, /device:TPU:1, one launch (start us, length us, event | category | flops | bytes accessed | tf_op | source)
XLA Modules:
  0.0 418.2 jit_solution(4615575505537742516)
XLA Ops:
  1.3 1.8 multiply_sine_fusion
  3.1 150.2 %forward_0.1 = (bf16[1024,2048]{1,0:T(8,128)(2,1)}, bf16[2048,640]{1,0:T(8,128)(2,1)}, f32[1,4352]{1,0:T(1,128)}, bf16[256,2048]{1,0:T(8,128)(2,1)}, f32[384,102...) custom-call(bf16[128,2048]{1,0:T(8,128)(2,1)} %hidden.3, ...), custom_call_target="tpu_custom_call" | custom-call | tf_op jit(solution)/shard_map/forward_0/pallas_call | solution.py:1079
  153.3 51.4 %feed_2.1 = (bf16[1024,2048]{1,0:T(8,128)(2,1)}, bf16[1024,768]{1,0:T(8,128)(2,1)}, bf16[1024,1536]{1,0:T(8,128)(2,1)}, bf16[768,2048]{1,0:T(8,128)(2,1)}) custom-call(bf16[128,2048]{1,0:T(8,128)(2,1)} %get-tuple-element.60.normed_two, bf16[2048,1536]{1,0:T(8,128)(2,1)} %bitcast.8, f32[192,2048]{1,0:T(8,128)} %down_weight.1, ...), custom_call_target="tpu_custom_call" | custom-call | tf_op jit(solution)/shard_map/feed_2/pallas_call | solution.py:1723
  204.7 104.0 %feed_back_3.1 = (bf16[1024,2048]{1,0:T(8,128)(2,1)}, f32[128,2048]{1,0:T(8,128)}, f32[1,2048]{1,0:T(1,128)}, bf16[128,2048]{1,0:T(8,128)(2,1)}, bf16[8,64,1536]...) custom-call(bf16[1024,1536]{1,0:T(8,128)(2,1)} %get-tuple-element.63.grad_pre, bf16[2048,1536]{1,0:T(8,128)(2,1)} %bitcast.9, ...), custom_call_target="tpu_custom_call" | custom-call | tf_op jit(solution)/shard_map/feed_back_3/pallas_call | solution.py:1920
  308.7 103.6 %attend_back_4.1 = (bf16[128,2048]{1,0:T(8,128)(2,1)}, f32[1,136]{1,0:T(1,128)}, bf16[64,2048]{1,0:T(8,128)(2,1)}, f32[64,1024]{1,0:T(8,128)}, f32[64,1024]{1,0:...) custom-call(bf16[1024,2048]{1,0:T(8,128)(2,1)} %get-tuple-element.70, ...), custom_call_target="tpu_custom_call" | custom-call | tf_op jit(solution)/shard_map/attend_back_4/pallas_call | solution.py:1548
  412.3 5.7 %widen.1 = (bf16[128,2048]{1,0:T(8,128)(2,1)}, bf16[128,2048]{1,0:T(8,128)(2,1)}, f32[64,2048]{1,0:T(8,128)}, f32[64,1024]{1,0:T(8,128)}, f32[64,1024]{1,0:T(8,1...) custom-call(bf16[128,2048]{1,0:T(8,128)(2,1)} %get-tuple-element.69., ...), custom_call_target="tpu_custom_call" | custom-call | tf_op jit(solution)/shard_map/widen/pallas_call | solution.py:1964
  (2 shorter events, 0.0 us)
